TPU v7x, 32 devices: a whole 2x2x4 slice. The times are simulated.
32 devices in a mesh: seq: 4 (over y, x), rows: 8 (over z, core).
Axes of the slice: x: 2, y: 2, z: 4, core: 2. Of those that a mesh axis runs over, the one named last changes fastest.
Arguments:
- frames: bfloat16 [8, 1024, 768], P('rows', 'seq'), may hold values from -6 to 6
- text_tokens: bfloat16 [8, 308, 768], P('rows'), may hold values from -6 to 6
- step_embed: bfloat16 [8, 4, 768], P('rows'), may hold values from -6 to 6
- segments: int32 [8, 1024], P('rows'), may hold values from 0 to 3, as said below
- cotangent: bfloat16 [8, 1024, 768], P('rows', 'seq'), may hold values from -6 to 6
- w_ada: bfloat16 [768, 4608], replicated, may hold values from -0.21875 to 0.21875
- b_ada: bfloat16 [4608], replicated, may hold values from -1.5 to 1.5
- w_qkv: bfloat16 [768, 2304], replicated, may hold values from -0.21875 to 0.21875
- w_out: bfloat16 [768, 768], replicated, may hold values from -1.75 to 1.75
- g_cross: bfloat16 [768], replicated, may hold values from 0.25 to 1.75
- w_cq: bfloat16 [768, 768], replicated, may hold values from -0.21875 to 0.21875
- w_ckv: bfloat16 [768, 1536], replicated, may hold values from -0.21875 to 0.21875
- w_co: bfloat16 [768, 768], replicated, may hold values from -0.875 to 0.875
- w_up: bfloat16 [768, 3072], replicated, may hold values from -0.21875 to 0.21875
- b_up: bfloat16 [3072], replicated, may hold values from -2.5 to 2.5
- w_down: bfloat16 [3072, 768], replicated, may hold values from -0.109375 to 0.109375
- b_down: bfloat16 [768], replicated, may hold values from -1.5 to 1.5
Outputs:
- output: bfloat16 [8, 1024, 768], P('rows', 'seq')
- d_frames: float32 [8, 1024, 768], P('rows', 'seq')
- d_text: float32 [8, 308, 768], P('rows', 'seq')
- d_step: float32 [8, 4, 768], P('rows', 'seq')
- d_w_ada: float32 [768, 4608], P('rows', 'seq')
- d_b_ada: float32 [4608], P('rows')
- d_w_qkv: float32 [768, 2304], P('rows', 'seq')
- d_w_out: float32 [768, 768], P('rows', 'seq')
- d_g_cross: float32 [768], P('rows')
- d_w_cq: float32 [768, 768], P('rows', 'seq')
- d_w_ckv: float32 [768, 1536], P('rows', 'seq')
- d_w_co: float32 [768, 768], P('rows', 'seq')
- d_w_up: float32 [768, 3072], P('rows', 'seq')
- d_b_up: float32 [3072], P('rows')
- d_w_down: float32 [3072, 768], P('rows', 'seq')
- d_b_down: float32 [768], P('rows')
Inputs may be any that keep to these rules, and one draw needn't show every extreme that they name: `segments`: in each row the slot numbers start at 0, never fall and rise by one from item to item; each item covers a quarter, a half or all of the 1024 frames; some row holds four items.
All inputs are finite; a program needn't handle non-finite values.
Results may differ from a plain program's by a relative error of at most 0.02.
Values may be sent and summed in bfloat16 or wider, within the bound.
A program may use at most 192 MiB of HBM per device.

v0:
```python
import jax
import jax.numpy as jnp
from jax import lax
from jax.sharding import PartitionSpec as P

HEADS = 12
HEAD = 64
TXT = 77
ITEMS = 4


EPSILON = 1e-06
NEG_FILL = -1e30
PRECISE = lax.Precision.HIGHEST


def norm_rows(values):
    center = values - jnp.mean(values, axis=-1, keepdims=True)
    return center * lax.rsqrt(jnp.mean(center * center, axis=-1, keepdims=True) + EPSILON)


def modulate(values, scale_part, shift_part):
    return norm_rows(values) * (1.0 + scale_part) + shift_part


def with_gain(values, gain_row):
    return norm_rows(values) * gain_row


def gelu_tanh(values):
    return jax.nn.gelu(values, approximate=True)


def project(inputs, weight):
    return jnp.einsum("bnd,de->bne", inputs, weight, preferred_element_type=jnp.float32)


def project_back(upstream, weight):
    return jnp.einsum("bne,de->bnd", upstream, weight, preferred_element_type=jnp.float32)


def outer_sum(inputs, upstream):
    return jnp.einsum("bnd,bne->de", inputs, upstream, preferred_element_type=jnp.float32)


def split_heads(matrix):
    return matrix.reshape(matrix.shape[0], matrix.shape[1], HEADS, HEAD)


def masked_scores(queries, keyset, allowed):
    raw_scores = jnp.einsum(
        "bqhd,bkhd->bhqk",
        split_heads(queries),
        split_heads(keyset),
        preferred_element_type=jnp.float32,
    )
    return jnp.where(allowed[:, None], raw_scores * HEAD ** (-0.5), NEG_FILL)


def attend_forward(queries, keyset, valueset, allowed):
    scores = masked_scores(queries, keyset, allowed)
    top_score = jnp.max(scores, axis=-1, keepdims=True)
    exp_scores = jnp.exp(scores - top_score)
    totals = jnp.sum(exp_scores, axis=-1, keepdims=True)
    probs_low = (exp_scores / totals).astype(jnp.bfloat16)
    mixed_out = jnp.einsum(
        "bhqk,bkhd->bqhd", probs_low, split_heads(valueset), preferred_element_type=jnp.float32
    )
    return (mixed_out.reshape(queries.shape).astype(jnp.bfloat16), top_score + jnp.log(totals))


def attend_backward(queries, keyset, valueset, allowed, log_total, upstream):
    prob_rows = jnp.exp(masked_scores(queries, keyset, allowed) - log_total)
    up_heads = split_heads(upstream)
    grad_probs = jnp.einsum(
        "bqhd,bkhd->bhqk", up_heads, split_heads(valueset), preferred_element_type=jnp.float32
    )
    inner_sum = jnp.sum(prob_rows * grad_probs, axis=-1, keepdims=True)
    grad_scores = (prob_rows * (grad_probs - inner_sum)).astype(jnp.bfloat16)
    grad_query = jnp.einsum(
        "bhqk,bkhd->bqhd", grad_scores, split_heads(keyset), preferred_element_type=jnp.float32
    ) * HEAD ** (-0.5)
    grad_key = jnp.einsum(
        "bhqk,bqhd->bkhd", grad_scores, split_heads(queries), preferred_element_type=jnp.float32
    ) * HEAD ** (-0.5)
    grad_value = jnp.einsum(
        "bhqk,bqhd->bkhd",
        prob_rows.astype(jnp.bfloat16),
        up_heads,
        preferred_element_type=jnp.float32,
    )
    return (
        grad_query.reshape(queries.shape),
        grad_key.reshape(keyset.shape),
        grad_value.reshape(valueset.shape),
    )


def spread_items(item_table, local_items):
    picked = jnp.zeros(local_items.shape + (item_table.shape[-1],), jnp.float32)
    for slot_num in range(item_table.shape[1]):
        picked = picked + jnp.where(
            (local_items == slot_num)[:, :, None], item_table[:, slot_num][:, None, :], 0.0
        )
    return picked


def collect_items(frame_grad, local_items, slot_count):
    return jnp.stack(
        [
            jnp.sum(jnp.where((local_items == slot_num)[:, :, None], frame_grad, 0.0), axis=1)
            for slot_num in range(slot_count)
        ],
        axis=1,
    )


def per_device(
    frames,
    text_tokens,
    step_embed,
    segments,
    cotangent,
    w_ada,
    b_ada,
    w_qkv,
    w_out,
    g_cross,
    w_cq,
    w_ckv,
    w_co,
    w_up,
    b_up,
    w_down,
    b_down,
):
    seq_count = lax.axis_size("seq")
    seq_index = lax.axis_index("seq")
    frames_here = frames.shape[1]
    local_items = lax.dynamic_slice_in_dim(segments, seq_index * frames_here, frames_here, axis=1)
    slot_ids = jnp.arange(text_tokens.shape[1], dtype=jnp.int32) // TXT
    allowed_self = local_items[:, :, None] == segments[:, None, :]
    allowed_cross = local_items[:, :, None] == slot_ids[None, None, :]
    step_f32 = step_embed.astype(jnp.float32)
    ada_in = jax.nn.silu(step_f32).astype(jnp.bfloat16)
    item_mod = jnp.einsum(
        "bid,de->bie", ada_in, w_ada, preferred_element_type=jnp.float32
    ) + b_ada.astype(jnp.float32)
    frame_mod = spread_items(item_mod, local_items)
    shift_a, scale_a, gate_a, shift_b, scale_b, gate_b = jnp.split(frame_mod, 6, axis=-1)
    frames_f32 = frames.astype(jnp.float32)
    h_one = modulate(frames_f32, scale_a, shift_a).astype(jnp.bfloat16)
    proj_all = project(h_one, w_qkv).astype(jnp.bfloat16)
    query_a, key_a, value_a = jnp.split(proj_all, 3, axis=-1)
    key_all, value_all = (
        lax.all_gather(key_a, "seq", axis=1, tiled=True),
        lax.all_gather(value_a, "seq", axis=1, tiled=True),
    )
    attn_low, lse_self = attend_forward(query_a, key_all, value_all, allowed_self)
    branch_a = project(attn_low, w_out)
    x_one = frames_f32 + gate_a * branch_a
    gain_f32 = g_cross.astype(jnp.float32)
    h_two = with_gain(x_one, gain_f32).astype(jnp.bfloat16)
    query_c = project(h_two, w_cq).astype(jnp.bfloat16)
    text_kv = project(text_tokens, w_ckv).astype(jnp.bfloat16)
    key_c, value_c = jnp.split(text_kv, 2, axis=-1)
    cross_low, lse_cross = attend_forward(query_c, key_c, value_c, allowed_cross)
    x_two = x_one + project(cross_low, w_co)
    h_three = modulate(x_two, scale_b, shift_b).astype(jnp.bfloat16)
    pre_act = project(h_three, w_up) + b_up.astype(jnp.float32)
    act_low = gelu_tanh(pre_act).astype(jnp.bfloat16)
    branch_m = project(act_low, w_down) + b_down.astype(jnp.float32)
    output = (x_two + gate_b * branch_m).astype(jnp.bfloat16)
    grad_out = cotangent.astype(jnp.float32)
    grad_m = (gate_b * grad_out).astype(jnp.bfloat16)
    d_w_down = outer_sum(act_low, grad_m)
    d_b_down = jnp.sum(grad_m.astype(jnp.float32), axis=(0, 1))
    grad_act = project_back(grad_m, w_down)
    unused_act, gelu_back = jax.vjp(gelu_tanh, pre_act)
    grad_pre = gelu_back(grad_act)[0].astype(jnp.bfloat16)
    d_w_up = outer_sum(h_three, grad_pre)
    d_b_up = jnp.sum(grad_pre.astype(jnp.float32), axis=(0, 1))
    up_three = project_back(grad_pre, w_up)
    unused_three, back_three = jax.vjp(modulate, x_two, scale_b, shift_b)
    norm_x2, d_scale_b, d_shift_b = back_three(up_three)
    grad_x2 = grad_out + norm_x2
    grad_c = grad_x2.astype(jnp.bfloat16)
    d_w_co = outer_sum(cross_low, grad_c)
    grad_cross = project_back(grad_c, w_co).astype(jnp.bfloat16)
    grad_qc_f32, grad_kc_part, grad_vc_part = attend_backward(
        query_c, key_c, value_c, allowed_cross, lse_cross, grad_cross
    )
    grad_qc = grad_qc_f32.astype(jnp.bfloat16)
    d_w_cq = outer_sum(h_two, grad_qc)
    up_two = project_back(grad_qc, w_cq)
    unused_two, back_two = jax.vjp(with_gain, x_one, gain_f32)
    norm_x1, d_g_cross = back_two(up_two)
    grad_x1 = grad_x2 + norm_x1
    grad_a = (gate_a * grad_x1).astype(jnp.bfloat16)
    d_w_out = outer_sum(attn_low, grad_a)
    grad_attn = project_back(grad_a, w_out).astype(jnp.bfloat16)
    key_back, value_back = (key_all, value_all)
    grad_qa, grad_ka_part, grad_va_part = attend_backward(
        query_a, key_back, value_back, allowed_self, lse_self, grad_attn
    )
    grad_ka, grad_va = (
        lax.psum_scatter(
            grad_ka_part.astype(jnp.bfloat16), "seq", scatter_dimension=1, tiled=True
        ).astype(jnp.float32),
        lax.psum_scatter(
            grad_va_part.astype(jnp.bfloat16), "seq", scatter_dimension=1, tiled=True
        ).astype(jnp.float32),
    )
    grad_qkv = jnp.concatenate(
        [grad_qa.astype(jnp.bfloat16), grad_ka.astype(jnp.bfloat16), grad_va.astype(jnp.bfloat16)],
        axis=-1,
    )
    d_w_qkv = outer_sum(h_one, grad_qkv)
    up_one = project_back(grad_qkv, w_qkv)
    unused_one, back_one = jax.vjp(modulate, frames_f32, scale_a, shift_a)
    norm_x0, d_scale_a, d_shift_a = back_one(up_one)
    d_frames = grad_x1 + norm_x0
    frame_grad = jnp.concatenate(
        [d_shift_a, d_scale_a, grad_x1 * branch_a, d_shift_b, d_scale_b, grad_out * branch_m],
        axis=-1,
    )
    item_grad = collect_items(frame_grad, local_items, ITEMS)
    grad_kc, grad_vc, item_mine = (
        lax.psum_scatter(
            grad_kc_part.astype(jnp.bfloat16), "seq", scatter_dimension=1, tiled=True
        ).astype(jnp.float32),
        lax.psum_scatter(
            grad_vc_part.astype(jnp.bfloat16), "seq", scatter_dimension=1, tiled=True
        ).astype(jnp.float32),
        lax.psum_scatter(
            item_grad.astype(jnp.bfloat16), "seq", scatter_dimension=1, tiled=True
        ).astype(jnp.float32),
    )
    text_share = text_tokens.shape[1] // seq_count
    item_share = ITEMS // seq_count
    my_text = lax.dynamic_slice_in_dim(text_tokens, seq_index * text_share, text_share, axis=1)
    my_ada = lax.dynamic_slice_in_dim(ada_in, seq_index * item_share, item_share, axis=1)
    my_step = lax.dynamic_slice_in_dim(step_f32, seq_index * item_share, item_share, axis=1)
    text_grad_low = jnp.concatenate(
        [grad_kc.astype(jnp.bfloat16), grad_vc.astype(jnp.bfloat16)], axis=-1
    )
    d_w_ckv = outer_sum(my_text, text_grad_low)
    d_text = project_back(text_grad_low, w_ckv)
    d_w_ada = jnp.einsum("bid,bie->de", my_ada.astype(jnp.float32), item_mine, precision=PRECISE)
    d_b_ada = jnp.sum(item_mine, axis=(0, 1))
    d_ada = jnp.einsum("bie,de->bid", item_mine, w_ada.astype(jnp.float32), precision=PRECISE)
    unused_step, silu_back = jax.vjp(jax.nn.silu, my_step)
    d_step = silu_back(d_ada)[0]
    all_rows = (
        lax.psum_scatter(d_w_ada, "rows", scatter_dimension=0, tiled=True),
        lax.psum_scatter(d_b_ada, "rows", scatter_dimension=0, tiled=True),
        lax.psum_scatter(d_w_qkv, "rows", scatter_dimension=0, tiled=True),
        lax.psum_scatter(d_w_out, "rows", scatter_dimension=0, tiled=True),
        lax.psum_scatter(d_g_cross, "rows", scatter_dimension=0, tiled=True),
        lax.psum_scatter(d_w_cq, "rows", scatter_dimension=0, tiled=True),
        lax.psum_scatter(d_w_ckv, "rows", scatter_dimension=0, tiled=True),
        lax.psum_scatter(d_w_co, "rows", scatter_dimension=0, tiled=True),
        lax.psum_scatter(d_w_up, "rows", scatter_dimension=0, tiled=True),
        lax.psum_scatter(d_b_up, "rows", scatter_dimension=0, tiled=True),
        lax.psum_scatter(d_w_down, "rows", scatter_dimension=0, tiled=True),
        lax.psum_scatter(d_b_down, "rows", scatter_dimension=0, tiled=True),
    )
    matrix_done = (
        lax.psum_scatter(
            all_rows[0].astype(jnp.bfloat16), "seq", scatter_dimension=1, tiled=True
        ).astype(jnp.float32),
        lax.psum_scatter(
            all_rows[2].astype(jnp.bfloat16), "seq", scatter_dimension=1, tiled=True
        ).astype(jnp.float32),
        lax.psum_scatter(
            all_rows[3].astype(jnp.bfloat16), "seq", scatter_dimension=1, tiled=True
        ).astype(jnp.float32),
        lax.psum_scatter(
            all_rows[5].astype(jnp.bfloat16), "seq", scatter_dimension=1, tiled=True
        ).astype(jnp.float32),
        lax.psum_scatter(
            all_rows[6].astype(jnp.bfloat16), "seq", scatter_dimension=1, tiled=True
        ).astype(jnp.float32),
        lax.psum_scatter(
            all_rows[7].astype(jnp.bfloat16), "seq", scatter_dimension=1, tiled=True
        ).astype(jnp.float32),
        lax.psum_scatter(
            all_rows[8].astype(jnp.bfloat16), "seq", scatter_dimension=1, tiled=True
        ).astype(jnp.float32),
        lax.psum_scatter(
            all_rows[10].astype(jnp.bfloat16), "seq", scatter_dimension=1, tiled=True
        ).astype(jnp.float32),
    )
    small_done = lax.psum((all_rows[1], all_rows[4], all_rows[9], all_rows[11]), "seq")
    return (
        output,
        d_frames,
        d_text,
        d_step,
        matrix_done[0],
        small_done[0],
        matrix_done[1],
        matrix_done[2],
        small_done[1],
        matrix_done[3],
        matrix_done[4],
        matrix_done[5],
        matrix_done[6],
        small_done[2],
        matrix_done[7],
        small_done[3],
    )


def solution(mesh):
    in_specs = (
        P("rows", "seq", None),
        P("rows", None, None),
        P("rows", None, None),
        P("rows", None),
        P("rows", "seq", None),
        P(),
        P(),
        P(),
        P(),
        P(),
        P(),
        P(),
        P(),
        P(),
        P(),
        P(),
        P(),
    )
    out_specs = (
        P("rows", "seq", None),
        P("rows", "seq", None),
        P("rows", "seq", None),
        P("rows", "seq", None),
        P("rows", "seq"),
        P("rows"),
        P("rows", "seq"),
        P("rows", "seq"),
        P("rows"),
        P("rows", "seq"),
        P("rows", "seq"),
        P("rows", "seq"),
        P("rows", "seq"),
        P("rows"),
        P("rows", "seq"),
        P("rows"),
    )
    return jax.shard_map(
        per_device, mesh=mesh, in_specs=in_specs, out_specs=out_specs, check_vma=False
    )
```

profile of v0, /device:TPU:0, one launch (start us, length us, event | category | flops | bytes accessed | tf_op | source)
XLA Modules:
  0.0 1095.9 jit_solution(6662945658922729233)
XLA Ops:
  11.0 4.0 fusion.6
  16.0 3.0 select_add_fusion
  23.0 2.7 fusion.18
  29.3 2.1 copy.66
  31.4 2.1 copy.64
  33.5 1.9 copy.62
  37.1 18.9 %all-gather.5.cloned.1.call-done = bf16[1,1024,768]{2,1,0:T(8,128)(2,1)} async-done(((bf16[1,256,768]{2,1,0:T(8,128)(2,1)}), bf16[1,1024,768]{2,1,0:T(8,128)(2,1)}) %all-gather.5.cloned.1.call-update) | async-done | bytes 1572880 | tf_op jit(solution)/shard_map/all_gather | solution.py:156
  56.0 3.1 copy.63
  59.1 3.9 fusion.7
  63.0 4.6 copy-done.1
  67.5 4.1 fusion
  71.6 17.1 %all-gather.3.cloned.1.call-done = bf16[1,1024,768]{2,1,0:T(8,128)(2,1)} async-done(((bf16[1,256,768]{2,1,0:T(8,128)(2,1)}), bf16[1,1024,768]{2,1,0:T(8,128)(2,1)}) %all-gather.3.cloned.1.call-update) | async-done | bytes 1572880 | tf_op jit(solution)/shard_map/all_gather | solution.py:157
  88.7 2.6 copy.61
  91.3 7.1 fusion.35
  98.5 2.7 fusion.103
  105.9 2.0 fusion.106
  116.8 3.9 convert_reduce_fusion
  122.4 3.2 fusion.102
  128.5 1.9 copy.67
  130.4 3.9 fusion.27
  140.6 2.3 fusion.59
  147.7 9.5 fusion.23
  157.3 9.2 multiply_reduce_fusion
  166.6 6.8 multiply_convert_fusion
  173.4 2.9 multiply_convert_fusion.2
  176.6 3.0 fusion.109
  179.7 3.3 fusion.96
  183.1 3.0 fusion.108
  187.5 11.3 %all-reduce.12.cloned.1.call-done = (bf16[1,308,768]{1,2,0:T(8,128)(2,1)}, bf16[1,308,768]{1,2,0:T(8,128)(2,1)}) async-done(((bf16[1,308,768]{1,2,0:T(8,128)(2,1)}, bf16[1,308,768]{1,2,0:T(8,128)(2,1)}), (bf16[1,308,768]{1,2,0:T(8,128)(2,1)}, bf16[1,308,768]{1,2,0:T(8,128)(2,1)})) %all-reduce.12.cloned.1.call-update) | async-done | bytes 946192
  200.8 3.9 fusion.68
  205.0 6.1 fusion.33
  211.0 21.7 %reduce-scatter.38.cloned.1.call-done = bf16[1,256,768]{1,2,0:T(8,128)(2,1)} async-done(((bf16[1,1024,768]{1,2,0:T(8,128)(2,1)}), bf16[1,256,768]{1,2,0:T(8,128)(2,1)}) %reduce-scatter.38.cloned.1.call-update) | async-done | bytes 393232 | tf_op jit(solution)/shard_map/reduce_scatter | solution.py:210
  232.8 34.0 %reduce-scatter.36.cloned.1.call-done = bf16[1,256,768]{1,2,0:T(8,128)(2,1)} async-done(((bf16[1,1024,768]{1,2,0:T(8,128)(2,1)}), bf16[1,256,768]{1,2,0:T(8,128)(2,1)}) %reduce-scatter.36.cloned.1.call-update) | async-done | bytes 393232 | tf_op jit(solution)/shard_map/reduce_scatter | solution.py:207
  266.8 5.3 fusion.55
  272.2 7.7 fusion.62
  280.0 6.6 fusion.110
  287.4 2.9 constant_dynamic-update-slice_fusion.1
  294.1 2.5 select_reduce_fusion.3
  297.3 17.0 %all-reduce.2 = bf16[1,4,4608]{2,1,0:T(4,128)(2,1)} all-reduce(bf16[1,4,4608]{2,1,0:T(4,128)(2,1)} %pad_maximum_fusion), channel_id=6, replica_groups=mesh['seq'=4,'rows'=8] {'seq'}, use_global_device_ids=true, to_apply=%region_26.27.clone | all-reduce | flops 18432 | bytes 73728
  315.8 6.8 broadcast_multiply_fusion
  326.1 18.2 %reduce-scatter.46.cloned.1.call-done = f32[96,768]{1,0:T(8,128)} async-done(((f32[768,768]{1,0:T(8,128)}), f32[96,768]{1,0:T(8,128)}) %reduce-scatter.46.cloned.1.call-update) | async-done | bytes 294928 | tf_op jit(solution)/shard_map/reduce_scatter | solution.py:260
  347.8 34.7 %reduce-scatter.44.cloned.1.call-done = f32[96,768]{1,0:T(8,128)} async-done(((f32[768,768]{1,0:T(8,128)}), f32[96,768]{1,0:T(8,128)}) %reduce-scatter.44.cloned.1.call-update) | async-done | bytes 294928 | tf_op jit(solution)/shard_map/reduce_scatter | solution.py:258
  386.3 52.4 %reduce-scatter.48.cloned.1.call-done = f32[96,1536]{1,0:T(8,128)} async-done(((f32[768,1536]{1,0:T(8,128)}), f32[96,1536]{1,0:T(8,128)}) %reduce-scatter.48.cloned.1.call-update) | async-done | bytes 589840 | tf_op jit(solution)/shard_map/reduce_scatter | solution.py:261
  442.4 74.0 %reduce-scatter.42.cloned.1.call-done = f32[96,2304]{1,0:T(8,128)} async-done(((f32[768,2304]{1,0:T(8,128)}), f32[96,2304]{1,0:T(8,128)}) %reduce-scatter.42.cloned.1.call-update) | async-done | bytes 884752 | tf_op jit(solution)/shard_map/reduce_scatter | solution.py:257
  516.5 2.0 convert_element_type.397
  518.4 2.1 copy.79
  520.6 96.1 %reduce-scatter.56.cloned.1.call-done = f32[384,768]{1,0:T(8,128)} async-done(((f32[3072,768]{1,0:T(8,128)}), f32[384,768]{1,0:T(8,128)}) %reduce-scatter.56.cloned.1.call-update) | async-done | bytes 1179664 | tf_op jit(solution)/shard_map/reduce_scatter | solution.py:265
  616.7 2.1 convert_element_type.410
  618.8 2.1 copy.89
  621.0 95.8 %reduce-scatter.52.cloned.1.call-done = f32[96,3072]{1,0:T(8,128)} async-done(((f32[768,3072]{1,0:T(8,128)}), f32[96,3072]{1,0:T(8,128)}) %reduce-scatter.52.cloned.1.call-update) | async-done | bytes 1179664 | tf_op jit(solution)/shard_map/reduce_scatter | solution.py:263
  716.8 2.1 convert_element_type.407
  719.0 142.6 %reduce-scatter.40.cloned.1.call-done = f32[96,4608]{1,0:T(8,128)} async-done(((f32[768,4608]{1,0:T(8,128)}), f32[96,4608]{1,0:T(8,128)}) %reduce-scatter.40.cloned.1.call-update) | async-done | bytes 1769488 | tf_op jit(solution)/shard_map/reduce_scatter | solution.py:255
  861.6 2.5 convert_element_type.395
  864.1 2.3 copy.77
  870.9 2.7 convolution_bitcast_fusion.4
  874.6 27.4 %all-reduce.7 = (f32[4608]{0:T(1024)}, f32[768]{0:T(1024)}, f32[3072]{0:T(1024)}, f32[768]{0:T(1024)}) all-reduce(bf16[4608]{0:T(1024)(128)(2,1)S(1)} %dynamic-slice_reduce_fusion, f32[768]{0:T(1024)} %get-tuple-element.68, f32[3072]{0:T(1024)} %get-tuple-element.129, ...), channel_id=9, replica_groups=mesh['seq'=4,'rows'=8] {'rows'}, use_global_device_ids=true, to_apply=%region_29.30.clone | all-reduce | flops 9216 | bytes 64512
  905.1 10.8 all-reduce.8
  915.9 6.1 fusion.76
  928.0 13.3 %reduce-scatter.62.cloned.1.call-done = bf16[192,96]{1,0:T(8,128)(2,1)} async-done(((bf16[768,96]{1,0:T(8,128)(2,1)}), bf16[192,96]{1,0:T(8,128)(2,1)}) %reduce-scatter.62.cloned.1.call-update) | async-done | bytes 36880
  944.3 24.4 %reduce-scatter.66.cloned.1.call-done = bf16[384,96]{1,0:T(8,128)(2,1)} async-done(((bf16[1536,96]{1,0:T(8,128)(2,1)}), bf16[384,96]{1,0:T(8,128)(2,1)}) %reduce-scatter.66.cloned.1.call-update) | async-done | bytes 73744
  971.9 25.0 %reduce-scatter.60.cloned.1.call-done = bf16[576,96]{1,0:T(8,128)(2,1)} async-done(((bf16[2304,96]{1,0:T(8,128)(2,1)}), bf16[576,96]{1,0:T(8,128)(2,1)}) %reduce-scatter.60.cloned.1.call-update) | async-done | bytes 110608
  1000.2 25.0 %reduce-scatter.70.cloned.1.call-done = bf16[192,384]{1,0:T(8,128)(2,1)} async-done(((bf16[768,384]{1,0:T(8,128)(2,1)}), bf16[192,384]{1,0:T(8,128)(2,1)}) %reduce-scatter.70.cloned.1.call-update) | async-done | bytes 147472
  1028.6 24.7 %reduce-scatter.54.cloned.1.call-done = bf16[96,768]{1,0:T(8,128)(2,1)} async-done(((bf16[96,3072]{1,0:T(8,128)(2,1)}), bf16[96,768]{1,0:T(8,128)(2,1)}) %reduce-scatter.54.cloned.1.call-update) | async-done | bytes 147472 | tf_op jit(solution)/shard_map/reduce_scatter | solution.py:287
  1055.0 30.0 %reduce-scatter.58.cloned.1.call-done = bf16[1152,96]{1,0:T(8,128)(2,1)} async-done(((bf16[4608,96]{1,0:T(8,128)(2,1)}), bf16[1152,96]{1,0:T(8,128)(2,1)}) %reduce-scatter.58.cloned.1.call-update) | async-done | bytes 221200
  (336 shorter events, 98.0 us)
Async XLA Ops:
  7.2 12.2 %copy-start = (bf16[768,2304]{1,0:T(8,128)(2,1)S(1)}, bf16[768,2304]{1,0:T(8,128)(2,1)}, u32[]{:S(2)}) copy-start(bf16[768,2304]{1,0:T(8,128)(2,1)} %param.24) | copy-start | bytes 10616836
  7.2 48.8 %all-gather.5.cloned.1.call-start = ((), (), s32[]{:S(2)}) async-start(), calls=%async_computation.19 | async-start | bytes 1966080 | tf_op jit(solution)/shard_map/all_gather | solution.py:156
  8.5 10.5 copy-start.65
  10.3 8.7 copy-start.76
  11.0 4.9 copy-start.78
  15.9 3.1 copy-start.11
  15.9 3.4 copy-start.79
  15.9 3.4 copy-start.81
  15.9 3.4 copy-start.83
  15.9 3.4 copy-start.85
  22.2 3.6 copy-start.88
  22.2 4.2 copy-start.89
  22.2 66.4 %all-gather.3.cloned.1.call-start = ((), (), s32[]{:S(2)}) async-start(), calls=%async_computation.18 | async-start | bytes 1966080 | tf_op jit(solution)/shard_map/all_gather | solution.py:157
  23.0 175.7 %all-reduce.12.cloned.1.call-start = ((), (), s32[]{:S(2)}) async-start(), calls=%async_computation.38 | async-start | bytes 2359296
  59.0 8.5 copy-start.14
  62.9 4.6 copy-start.1
  62.9 28.3 %copy-start.49 = (f32[12,256]{1,0:T(8,128)}, f32[12,256]{1,0:T(8,128)S(1)}, u32[]{:S(2)}) copy-start(f32[12,256]{1,0:T(8,128)S(1)} %get-tuple-element.113) | copy-start | bytes 36868
  91.3 7.2 copy-start.12
  91.3 7.2 copy-start.24
  98.4 4.2 copy-start.22
  98.5 4.2 copy-start.52
  107.9 5.1 slice-start
  108.4 6.6 slice-start.2
  109.4 4.7 slice-start.1
  109.4 5.7 slice-start.3
  110.2 3.8 copy-start.16
  112.7 9.6 copy-start.9
  112.7 9.6 copy-start.62
  114.1 8.3 copy-start.68
  116.5 5.9 copy-start.20
  122.3 3.2 copy-start.36
  130.4 3.9 copy-start.3
  130.4 3.9 copy-start.27
  130.4 3.9 copy-start.40
  137.3 3.2 copy-start.31
  140.6 3.9 copy-start.50
  144.2 88.5 %reduce-scatter.38.cloned.1.call-start = ((), (), s32[]{:S(2)}) async-start(), calls=%async_computation.21 | async-start | bytes 1966080 | tf_op jit(solution)/shard_map/reduce_scatter | solution.py:210
  147.7 9.6 copy-start.51
  157.3 109.5 %reduce-scatter.36.cloned.1.call-start = ((), (), s32[]{:S(2)}) async-start(), calls=%async_computation.20 | async-start | bytes 1966080 | tf_op jit(solution)/shard_map/reduce_scatter | solution.py:207
  157.3 9.2 copy-start.15
  166.5 6.8 copy-start.19
  173.4 3.1 copy-start.4
  176.6 3.2 copy-start.54
  176.6 3.2 copy-start.58
  176.6 3.2 copy-start.61
  176.6 146.1 %reduce-scatter.50.cloned.1.call-start = ((), (), s32[]{:S(2)}) async-start(), calls=%async_computation.27 | async-start | bytes 2654208 | tf_op jit(solution)/shard_map/reduce_scatter | solution.py:262
  179.7 164.7 %reduce-scatter.46.cloned.1.call-start = ((), (), s32[]{:S(2)}) async-start(), calls=%async_computation.25 | async-start | bytes 2654208 | tf_op jit(solution)/shard_map/reduce_scatter | solution.py:260
  183.1 3.1 copy-start.90
  183.1 199.4 %reduce-scatter.44.cloned.1.call-start = ((), (), s32[]{:S(2)}) async-start(), calls=%async_computation.24 | async-start | bytes 2654208 | tf_op jit(solution)/shard_map/reduce_scatter | solution.py:258
  186.1 252.5 %reduce-scatter.48.cloned.1.call-start = ((), (), s32[]{:S(2)}) async-start(), calls=%async_computation.26 | async-start | bytes 5308416 | tf_op jit(solution)/shard_map/reduce_scatter | solution.py:261
  204.7 311.8 %reduce-scatter.42.cloned.1.call-start = ((), (), s32[]{:S(2)}) async-start(), calls=%async_computation.23 | async-start | bytes 7962624 | tf_op jit(solution)/shard_map/reduce_scatter | solution.py:257
  272.1 344.6 %reduce-scatter.56.cloned.1.call-start = ((), (), s32[]{:S(2)}) async-start(), calls=%async_computation.30 | async-start | bytes 10616832 | tf_op jit(solution)/shard_map/reduce_scatter | solution.py:265
  279.9 436.9 %reduce-scatter.52.cloned.1.call-start = ((), (), s32[]{:S(2)}) async-start(), calls=%async_computation.28 | async-start | bytes 10616832 | tf_op jit(solution)/shard_map/reduce_scatter | solution.py:263
  286.6 575.0 %reduce-scatter.40.cloned.1.call-start = ((), (), s32[]{:S(2)}) async-start(), calls=%async_computation.22 | async-start | bytes 15925248 | tf_op jit(solution)/shard_map/reduce_scatter | solution.py:255
  287.3 3.0 copy-start.13
  322.6 599.5 %reduce-scatter.68.cloned.1.call-start = ((), (), s32[]{:S(2)}) async-start(), calls=%async_computation.36 | async-start | bytes 245760
  326.1 599.0 %reduce-scatter.64.cloned.1.call-start = ((), (), s32[]{:S(2)}) async-start(), calls=%async_computation.34 | async-start | bytes 245760
  347.7 593.6 %reduce-scatter.62.cloned.1.call-start = ((), (), s32[]{:S(2)}) async-start(), calls=%async_computation.33 | async-start | bytes 245760
  385.9 582.8 %reduce-scatter.66.cloned.1.call-start = ((), (), s32[]{:S(2)}) async-start(), calls=%async_computation.35 | async-start | bytes 491520
  442.4 554.5 %reduce-scatter.60.cloned.1.call-start = ((), (), s32[]{:S(2)}) async-start(), calls=%async_computation.32 | async-start | bytes 737280
  520.6 504.6 %reduce-scatter.70.cloned.1.call-start = ((), (), s32[]{:S(2)}) async-start(), calls=%async_computation.37 | async-start | bytes 737280
  621.0 432.3 %reduce-scatter.54.cloned.1.call-start = ((), (), s32[]{:S(2)}) async-start(), calls=%async_computation.29 | async-start | bytes 737280 | tf_op jit(solution)/shard_map/reduce_scatter | solution.py:287
  719.0 366.0 %reduce-scatter.58.cloned.1.call-start = ((), (), s32[]{:S(2)}) async-start(), calls=%async_computation.31 | async-start | bytes 1474560
  864.1 10.5 copy-start.64
  (54 other events, 90.8 us)
Sparse Core Ops, SparseCore 0:
  22.4 33.5 all-gather.4
  57.8 30.8 all-gather.2
  144.3 54.3 all-reduce.11
  201.6 31.1 reduce-scatter.37
  235.6 31.1 reduce-scatter.35
  269.0 37.0 reduce-scatter.49
  308.3 35.9 reduce-scatter.45
  346.7 35.8 reduce-scatter.43
  384.8 53.7 reduce-scatter.47
  440.8 75.5 reduce-scatter.41
  518.8 97.8 reduce-scatter.55
  618.9 97.8 reduce-scatter.51
  719.1 142.4 reduce-scatter.39
  864.2 22.7 reduce-scatter.67
  889.5 24.2 reduce-scatter.63
  917.0 24.2 reduce-scatter.61
  943.9 24.7 reduce-scatter.65
  971.4 25.3 reduce-scatter.59
  999.7 25.3 reduce-scatter.69
  1027.9 25.3 reduce-scatter.53
  1056.2 28.7 reduce-scatter.57
where the time goes:
time: 1100 us
  waiting for transfers between devices  760 us (69%)
  matrix products  119 us (11%)
  local copies, waits for them, and re-layouts  71.5 us (6%)
  other arithmetic  69.4 us (6%)
  blocking collectives  55.3 us (5%)
  between operations  18.7 us (2%)
    reduce_scatter x1, waiting for transfers between devices, per_device(): lax.psum_scatter(d_w_ada, 'rows', scatter_dimension=0, tiled=True)  143 us
    unnamed x29, waiting for transfers between devices  130 us
    reduce_scatter x1, waiting for transfers between devices, per_device(): lax.psum_scatter(d_w_down, 'rows', scatter_dimension=0, tiled=True)  96.1 us
    reduce_scatter x1, waiting for transfers between devices, per_device(): lax.psum_scatter(d_w_up, 'rows', scatter_dimension=0, tiled=True)  95.8 us
    reduce_scatter x1, waiting for transfers between devices, per_device(): lax.psum_scatter(d_w_qkv, 'rows', scatter_dimension=0, tiled=True)  74 us
    reduce_scatter x1, waiting for transfers between devices, per_device(): lax.psum_scatter(d_w_ckv, 'rows', scatter_dimension=0, tiled=True)  52.4 us
    unnamed x218, local copies, waits for them, and re-layouts  49.5 us
    unnamed x2, blocking collectives  44.4 us
  transfers between devices with their start and end apart: 21, of which 18 were waited for; matrix products, arithmetic and copies ran while one was open for 16% of the time, Pallas kernels for 0%

commit v1 on v0

v1 whole, which is shorter than its diff:
```python
import functools

import jax
import jax.numpy as jnp
from jax import lax
from jax.experimental import pallas as pl
from jax.experimental.pallas import tpu as pltpu
from jax.sharding import PartitionSpec as P

HEADS = 12
HEAD = 64
TXT = 77
ITEMS = 4

EPSILON = 1e-06
NEG_FILL = -1e30
PRECISE = lax.Precision.HIGHEST
F32 = jnp.float32
BF16 = jnp.bfloat16
MESH = pl.DeviceIdType.MESH
CHUNKS = 8
VMEM_MOST = 66_000_000


def dot(left, right):
    return jnp.dot(left, right, preferred_element_type=F32)


def dot_t(left, right):
    return lax.dot_general(left, right, (((1,), (1,)), ((), ())), preferred_element_type=F32)


def t_dot(left, right):
    return lax.dot_general(left, right, (((0,), (0,)), ((), ())), preferred_element_type=F32)


def norm_parts(values):
    center = values - jnp.mean(values, axis=-1, keepdims=True)
    inverse = lax.rsqrt(jnp.mean(center * center, axis=-1, keepdims=True) + EPSILON)
    return center * inverse, inverse


def norm_back(normed, inverse, upstream):
    return inverse * (
        upstream
        - jnp.mean(upstream, axis=-1, keepdims=True)
        - normed * jnp.mean(upstream * normed, axis=-1, keepdims=True)
    )


def gelu_tanh(values):
    return jax.nn.gelu(values, approximate=True)


def split_heads(matrix):
    return matrix.reshape(matrix.shape[0], HEADS, HEAD)


def scores_of(queries, keyset, allowed):
    raw = jnp.einsum(
        "qhd,khd->hqk", split_heads(queries), split_heads(keyset), preferred_element_type=F32
    )
    raw = raw * HEAD ** (-0.5)
    return raw if allowed is None else jnp.where(allowed[None, None, :], raw, NEG_FILL)


def attend_forward(queries, keyset, valueset, allowed):
    scores = scores_of(queries, keyset, allowed)
    top_score = jnp.max(scores, axis=-1, keepdims=True)
    exp_scores = jnp.exp(scores - top_score)
    totals = jnp.sum(exp_scores, axis=-1, keepdims=True)
    probs_low = (exp_scores / totals).astype(BF16)
    mixed = jnp.einsum(
        "hqk,khd->qhd", probs_low, split_heads(valueset), preferred_element_type=F32
    )
    return mixed.reshape(queries.shape).astype(BF16), top_score + jnp.log(totals)


def attend_backward(queries, keyset, valueset, allowed, log_total, upstream):
    probs = jnp.exp(scores_of(queries, keyset, allowed) - log_total)
    up_heads = split_heads(upstream)
    grad_probs = jnp.einsum(
        "qhd,khd->hqk", up_heads, split_heads(valueset), preferred_element_type=F32
    )
    inner = jnp.sum(probs * grad_probs, axis=-1, keepdims=True)
    grad_scores = (probs * (grad_probs - inner)).astype(BF16)
    grad_query = jnp.einsum(
        "hqk,khd->qhd", grad_scores, split_heads(keyset), preferred_element_type=F32
    )
    grad_key = jnp.einsum(
        "hqk,qhd->khd", grad_scores, split_heads(queries), preferred_element_type=F32
    )
    grad_value = jnp.einsum(
        "hqk,qhd->khd", probs.astype(BF16), up_heads, preferred_element_type=F32
    )
    return (
        (grad_query.reshape(queries.shape) * HEAD ** (-0.5)).astype(BF16),
        (grad_key.reshape(keyset.shape) * HEAD ** (-0.5)).astype(BF16),
        grad_value.reshape(valueset.shape).astype(BF16),
    )


def reduce_kernel(
    act, gm_t, h3, gpre, lc, gc, text, gkv, lq, gq0, gq1,
    out,
    G, R0, R1, R2, R3,
    s0, r0, s1, r1, s2, r2, s3, r3,
):
    seq = lax.axis_index("seq")
    rows = lax.axis_index("rows")
    y, x = seq // 2, seq % 2
    z, c = rows // 2, rows % 2
    core_peer = {"rows": z * 2 + (1 - c)}
    x_peer = {"seq": y * 2 + (1 - x)}
    y_peer = {"seq": (1 - y) * 2 + x}
    z_peers = [{"rows": lax.rem(z + d, 4) * 2 + c} for d in (1, 2, 3)]

    barrier = pltpu.get_barrier_semaphore()
    for peer in [core_peer, x_peer, y_peer] + z_peers:
        pl.semaphore_signal(barrier, inc=1, device_id=peer, device_id_type=MESH)
    pl.semaphore_wait(barrier, 6)

    width = G.shape[-1]
    tall = G.shape[-2]

    def put(k, s, block):
        low = block.astype(BF16)
        for zz in range(4):
            for cc in range(2):
                at = (zz * 2 + cc) * tall
                G[k, cc, zz, s // 2, s % 2] = low[at : at + tall]

    def compute(k):
        @pl.loop(0, 4)
        def _(s):
            if k < 2:
                left = gm_t[pl.ds(pl.multiple_of(s * 2 * tall + k * tall, 16), tall), :]
                for r in range(8):
                    G[k, r % 2, r // 2, s // 2, s % 2] = dot(
                        left, act[:, r * width : (r + 1) * width]
                    ).astype(BF16)
            elif k < 4:
                at = pl.multiple_of(s * 2 * width + (k - 2) * width, 128)
                put(k, s, t_dot(h3[...], gpre[:, pl.ds(at, width)]))
            elif k == 4:
                put(k, s, t_dot(lc[...], gc[s]))
            elif k == 5:
                at = pl.multiple_of(s * width, 128)
                put(k, s, t_dot(text[...], gkv[:, pl.ds(at, width)]))
            elif k == 6:
                put(k, s, t_dot(lq[: gq0.shape[1], :], gq0[s]))
            else:
                put(k, s, t_dot(lq[...], gq1[s]))

    def remote(src, dst, send, recv, peer):
        return pltpu.make_async_remote_copy(
            src_ref=src, dst_ref=dst, send_sem=send, recv_sem=recv,
            device_id=peer, device_id_type=MESH,
        )

    def core_copy(k):
        return remote(G.at[k, 1 - c], R0.at[k], s0.at[k], r0.at[k], core_peer)

    def first_copies(k):
        return (
            remote(G.at[k, c, 0:2, :, 1 - x], R1.at[k, 0], s1.at[k, 0], r1.at[k, 0], x_peer),
            remote(G.at[k, c, 2:4, 1 - y], R1.at[k, 1], s1.at[k, 1], r1.at[k, 1], y_peer),
        )

    def second_copies(k):
        return (
            remote(G.at[k, c, 0:2, 1 - y, x], R2.at[k, 0], s2.at[k, 0], r2.at[k, 0], y_peer),
            remote(G.at[k, c, 2:4, y, 1 - x], R2.at[k, 1], s2.at[k, 1], r2.at[k, 1], x_peer),
        )

    def z_copies(k):
        return [
            remote(
                G.at[k, c, lax.rem(z + d, 4), y, x], R3.at[k, d - 1],
                s3.at[k, d - 1], r3.at[k, d - 1], z_peers[d - 1],
            )
            for d in (1, 2, 3)
        ]

    def add(one, two):
        return (one.astype(F32) + two.astype(F32)).astype(BF16)

    def phase0(k):
        compute(k)
        core_copy(k).start()

    def phase1(k):
        core_copy(k).wait_recv()

        @pl.loop(0, 4)
        def _(zz):
            for yy in range(2):
                for xx in range(2):
                    G[k, c, zz, yy, xx] = add(G[k, c, zz, yy, xx], R0[k, zz, yy, xx])

        for copy in first_copies(k):
            copy.start()

    def phase2(k):
        for copy in first_copies(k):
            copy.wait_recv()
        for zz in range(2):
            for other in range(2):
                G[k, c, zz, other, x] = add(G[k, c, zz, other, x], R1[k, 0, zz, other])
                G[k, c, 2 + zz, y, other] = add(G[k, c, 2 + zz, y, other], R1[k, 1, zz, other])
        for copy in second_copies(k):
            copy.start()

    def phase3(k):
        for copy in second_copies(k):
            copy.wait_recv()
        for zz in range(2):
            G[k, c, zz, y, x] = add(G[k, c, zz, y, x], R2[k, 0, zz])
            G[k, c, 2 + zz, y, x] = add(G[k, c, 2 + zz, y, x], R2[k, 1, zz])
        for copy in z_copies(k):
            copy.start()

    def phase4(k):
        for copy in z_copies(k):
            copy.wait_recv()
        total = G[k, c, z, y, x].astype(F32)
        for d in range(3):
            total = total + R3[k, d].astype(F32)
        out[k] = total

    phases = (phase0, phase1, phase2, phase3, phase4)
    for wave in range(CHUNKS + 4):
        for depth in (4, 3, 2, 1, 0):
            if 0 <= wave - depth < CHUNKS:
                phases[depth](wave - depth)
    for k in range(CHUNKS):
        core_copy(k).wait_send()
        for copy in (*first_copies(k), *second_copies(k), *z_copies(k)):
            copy.wait_send()


def reduce_weights(ops, model):
    tall, width = model // 8, model // 2
    block = (CHUNKS, 2, 4, 2, 2, tall, width)
    dma = pltpu.SemaphoreType.DMA
    return pl.pallas_call(
        reduce_kernel,
        out_shape=jax.ShapeDtypeStruct((CHUNKS, tall, width), F32),
        in_specs=[pl.BlockSpec(memory_space=pltpu.VMEM)] * len(ops),
        out_specs=pl.BlockSpec(memory_space=pltpu.VMEM),
        scratch_shapes=[
            pltpu.VMEM(block, BF16),
            pltpu.VMEM((CHUNKS, 4, 2, 2, tall, width), BF16),
            pltpu.VMEM((CHUNKS, 2, 2, 2, tall, width), BF16),
            pltpu.VMEM((CHUNKS, 2, 2, tall, width), BF16),
            pltpu.VMEM((CHUNKS, 3, tall, width), BF16),
            dma((CHUNKS,)), dma((CHUNKS,)),
            dma((CHUNKS, 2)), dma((CHUNKS, 2)),
            dma((CHUNKS, 2)), dma((CHUNKS, 2)),
            dma((CHUNKS, 3)), dma((CHUNKS, 3)),
        ],
        compiler_params=pltpu.CompilerParams(
            collective_id=0, has_side_effects=True, vmem_limit_bytes=VMEM_MOST
        ),
        name="reduce_weights",
    )(*ops)


def scatter_plain(matrix):
    part = lax.psum_scatter(matrix.astype(BF16), "rows", scatter_dimension=0, tiled=True)
    part = lax.psum_scatter(part, "seq", scatter_dimension=1, tiled=True)
    return part.astype(F32)


def per_device(
    frames, text_tokens, step_embed, segments, cotangent,
    w_ada, b_ada, w_qkv, w_out, g_cross, w_cq, w_ckv, w_co, w_up, b_up, w_down, b_down,
):
    seq_count = lax.axis_size("seq")
    rows_count = lax.axis_size("rows")
    seq_index = lax.axis_index("seq")
    rows_index = lax.axis_index("rows")
    frames, text_tokens, step_embed = frames[0], text_tokens[0], step_embed[0]
    segments, cotangent = segments[0], cotangent[0]
    here, model = frames.shape
    length = segments.shape[0]
    assert (length // ITEMS) % here == 0
    block_slots = segments[::here]
    slot = lax.dynamic_index_in_dim(block_slots, seq_index, 0, keepdims=False)
    allowed = segments == slot
    text_mine = lax.dynamic_slice_in_dim(text_tokens, slot * TXT, TXT, axis=0)

    frames_all = lax.all_gather(frames, "seq", axis=0, tiled=True)
    ada_in = jax.nn.silu(step_embed.astype(F32)).astype(BF16)
    item_mod = dot(ada_in, w_ada) + b_ada.astype(F32)
    mine = lax.dynamic_slice_in_dim(item_mod, slot, 1, axis=0)
    shift_a, scale_a, gate_a, shift_b, scale_b, gate_b = jnp.split(mine, 6, axis=-1)

    normed_all, inverse_all = norm_parts(frames_all.astype(F32))
    hot = (block_slots[:, None] == jnp.arange(ITEMS)[None, :]).astype(F32)
    block_mod = jnp.dot(hot, item_mod[:, : 2 * model], precision=PRECISE)
    frame_mod = jnp.repeat(block_mod, here, axis=0)
    h_all = (normed_all * (1.0 + frame_mod[:, model:]) + frame_mod[:, :model]).astype(BF16)
    frames_f32 = frames.astype(F32)
    normed_0, inverse_0 = norm_parts(frames_f32)
    h_one = (normed_0 * (1.0 + scale_a) + shift_a).astype(BF16)
    query_a = dot(h_one, w_qkv[:, :model]).astype(BF16)
    kv_all = dot(h_all, w_qkv[:, model:]).astype(BF16)
    key_all, value_all = kv_all[:, :model], kv_all[:, model:]
    attn_low, lse_self = attend_forward(query_a, key_all, value_all, allowed)
    branch_a = dot(attn_low, w_out)
    x_one = frames_f32 + gate_a * branch_a
    gain = g_cross.astype(F32)[None]
    normed_1, inverse_1 = norm_parts(x_one)
    h_two = (normed_1 * gain).astype(BF16)
    query_c = dot(h_two, w_cq).astype(BF16)
    text_kv = dot(text_mine, w_ckv).astype(BF16)
    key_c, value_c = text_kv[:, :model], text_kv[:, model:]
    cross_low, lse_cross = attend_forward(query_c, key_c, value_c, None)
    x_two = x_one + dot(cross_low, w_co)
    normed_2, inverse_2 = norm_parts(x_two)
    h_three = (normed_2 * (1.0 + scale_b) + shift_b).astype(BF16)
    pre_act = dot(h_three, w_up) + b_up.astype(F32)
    act_low = gelu_tanh(pre_act).astype(BF16)
    branch_m = dot(act_low, w_down) + b_down.astype(F32)
    output = (x_two + gate_b * branch_m).astype(BF16)

    grad_out = cotangent.astype(F32)
    grad_m = (gate_b * grad_out).astype(BF16)
    grad_act = dot_t(grad_m, w_down)
    unused_act, gelu_back = jax.vjp(gelu_tanh, pre_act)
    grad_pre = gelu_back(grad_act)[0].astype(BF16)
    up_three = dot_t(grad_pre, w_up)
    grad_x2 = grad_out + norm_back(normed_2, inverse_2, up_three * (1.0 + scale_b))
    grad_c = grad_x2.astype(BF16)
    grad_cross = dot_t(grad_c, w_co).astype(BF16)
    grad_qc, grad_kc, grad_vc = attend_backward(
        query_c, key_c, value_c, None, lse_cross, grad_cross
    )
    grad_kvc = jnp.concatenate([grad_kc, grad_vc], axis=-1)
    up_two = dot_t(grad_qc, w_cq)
    grad_x1 = grad_x2 + norm_back(normed_1, inverse_1, up_two * gain)
    grad_a = (gate_a * grad_x1).astype(BF16)
    grad_attn = dot_t(grad_a, w_out).astype(BF16)
    grad_qa, grad_ka, grad_va = attend_backward(
        query_a, key_all, value_all, allowed, lse_self, grad_attn
    )
    grad_kva = jnp.concatenate([grad_ka, grad_va], axis=-1)
    up_kv = dot_t(grad_kva, w_qkv[:, model:]).astype(BF16)
    up_one = dot_t(grad_qa, w_qkv[:, :model]) + lax.psum_scatter(
        up_kv, "seq", scatter_dimension=0, tiled=True
    ).astype(F32)
    d_frames = grad_x1 + norm_back(normed_0, inverse_0, up_one * (1.0 + scale_a))

    small = jnp.concatenate(
        [
            jnp.sum(up_one, axis=0),
            jnp.sum(up_one * normed_0, axis=0),
            jnp.sum(grad_x1 * branch_a, axis=0),
            jnp.sum(up_three, axis=0),
            jnp.sum(up_three * normed_2, axis=0),
            jnp.sum(grad_out * branch_m, axis=0),
            jnp.sum(up_two * normed_1, axis=0),
            jnp.sum(grad_pre.astype(F32), axis=0),
            jnp.sum(grad_m.astype(F32), axis=0),
            lax.dynamic_index_in_dim(ada_in, slot, 0, keepdims=False).astype(F32),
        ]
    )
    small_all = lax.all_gather(small, ("rows", "seq"), axis=0, tiled=False)
    small_all = small_all.reshape(rows_count * seq_count, -1)
    item_all = small_all[:, : 6 * model]
    bias_all = small_all[:, 6 * model : -model]
    ada_all = small_all[:, -model:]

    def share(table, count, index):
        size = table.shape[-1] // count
        return lax.dynamic_slice_in_dim(table, index * size, size, axis=-1)

    def bias_sum(table):
        return jnp.sum(share(table, rows_count, rows_index), axis=0)

    d_b_ada = bias_sum(item_all)
    d_g_cross = bias_sum(bias_all[:, :model])
    d_b_up = bias_sum(bias_all[:, model:-model])
    d_b_down = bias_sum(bias_all[:, -model:])
    d_w_ada = lax.dot_general(
        share(ada_all, rows_count, rows_index),
        share(item_all, seq_count, seq_index),
        (((0,), (0,)), ((), ())),
        precision=PRECISE,
        preferred_element_type=F32,
    )
    item_share = ITEMS // seq_count
    row_items = lax.dynamic_slice_in_dim(item_all, rows_index * seq_count, seq_count, axis=0)
    owned = seq_index * item_share + jnp.arange(item_share)
    pick = (owned[:, None] == block_slots[None, :]).astype(F32)
    item_mine = jnp.dot(pick, row_items, precision=PRECISE)
    d_ada = lax.dot_general(
        item_mine, w_ada.astype(F32), (((1,), (1,)), ((), ())), precision=PRECISE
    )
    my_step = lax.dynamic_slice_in_dim(
        step_embed, seq_index * item_share, item_share, axis=0
    ).astype(F32)
    unused_step, silu_back = jax.vjp(jax.nn.silu, my_step)
    d_step = silu_back(d_ada)[0]
    text_part = dot_t(grad_kvc, w_ckv).astype(BF16)
    text_full = lax.dynamic_update_slice_in_dim(
        jnp.zeros(text_tokens.shape, BF16), text_part, slot * TXT, axis=0
    )
    d_text = lax.psum_scatter(text_full, "seq", scatter_dimension=0, tiled=True).astype(F32)

    if rows_count == 8 and seq_count == 4:
        half = model // 2

        def by_seq(table):
            return table.reshape(table.shape[0], 4, -1).transpose(1, 0, 2)

        pad_text = (-TXT) % 16
        zero_c = jnp.zeros((4, here, model // 4), BF16)
        gc = jnp.concatenate(
            [
                jnp.concatenate([by_seq(grad_qc), zero_c], axis=2),
                jnp.concatenate([zero_c, by_seq(grad_c)], axis=2),
            ],
            axis=1,
        )
        query_full = lax.dynamic_update_slice_in_dim(
            jnp.zeros((length, model), BF16), grad_qa, seq_index * here, axis=0
        )
        gqkv = by_seq(jnp.concatenate([query_full, grad_kva], axis=1))
        rest = gqkv[:, :, half:]
        gq1 = jnp.concatenate(
            [
                jnp.pad(rest, ((0, 0), (0, 0), (0, half - rest.shape[2]))),
                jnp.pad(by_seq(grad_a), ((0, 0), (0, 0), (rest.shape[2], 0))),
            ],
            axis=1,
        )
        ops = (
            act_low, grad_m.T, h_three, grad_pre,
            jnp.concatenate([h_two, cross_low], axis=0), gc,
            jnp.pad(text_mine, ((0, pad_text), (0, 0))),
            jnp.pad(grad_kvc, ((0, pad_text), (0, 0))),
            jnp.concatenate([h_all, attn_low], axis=0), gqkv[:, :, :half], gq1,
        )
        done = reduce_weights(ops, model)
        d_w_down = jnp.concatenate([done[0], done[1]], axis=0).T
        d_w_up = jnp.concatenate([done[2], done[3]], axis=1)
        d_w_cq, d_w_co = done[4][:, : model // 4], done[4][:, model // 4 :]
        d_w_ckv = done[5]
        last = done[7]
        d_w_qkv = jnp.concatenate([done[6], last[:, : rest.shape[2]]], axis=1)
        d_w_out = last[:, rest.shape[2] :]
    else:
        d_w_down = scatter_plain(t_dot(act_low, grad_m))
        d_w_up = scatter_plain(t_dot(h_three, grad_pre))
        d_w_cq = scatter_plain(t_dot(h_two, grad_qc))
        d_w_co = scatter_plain(t_dot(cross_low, grad_c))
        d_w_ckv = scatter_plain(t_dot(text_mine, grad_kvc))
        d_w_out = scatter_plain(t_dot(attn_low, grad_a))
        d_w_qkv = scatter_plain(
            jnp.concatenate([t_dot(h_one, grad_qa), t_dot(h_all, grad_kva)], axis=1)
        )
    return (
        output[None], d_frames[None], d_text[None], d_step[None],
        d_w_ada, d_b_ada, d_w_qkv, d_w_out, d_g_cross, d_w_cq, d_w_ckv, d_w_co,
        d_w_up, d_b_up, d_w_down, d_b_down,
    )


def solution(mesh):
    row_seq = P("rows", "seq", None)
    in_specs = (
        row_seq, P("rows", None, None), P("rows", None, None), P("rows", None), row_seq,
    ) + (P(),) * 12
    out_specs = (row_seq,) * 4 + (
        P("rows", "seq"), P("rows"), P("rows", "seq"), P("rows", "seq"), P("rows"),
        P("rows", "seq"), P("rows", "seq"), P("rows", "seq"), P("rows", "seq"), P("rows"),
        P("rows", "seq"), P("rows"),
    )
    return jax.shard_map(
        per_device, mesh=mesh, in_specs=in_specs, out_specs=out_specs, check_vma=False
    )
```

time: 1100 us -> 363 us (0.33)
  waiting for transfers between devices: 760 us -> 16.6 us
  Pallas kernels: 0 us -> 109 us
  matrix products: 119 us -> 81.3 us
  other arithmetic: 69.4 us -> 38.7 us
  blocking collectives: 55.3 us -> 24.8 us
    reduce_scatter x11 -> x1, waiting for transfers between devices: 594 us -> 0.02 us  [per_device(): lax.psum_scatter(up_kv, 'seq', scatter_dimension=0, tiled=True).astype(F32)]
    unnamed x29 -> x4, waiting for transfers between devices: 130 us -> 0.72 us
    pallas_call x0 -> x1, Pallas kernels: none -> 109 us  [reduce_weights(): pl.pallas_call(reduce_kernel, out_shape=jax.ShapeDtypeStruct((CHUNKS, tal...]
    dot_general x35 -> x33, matrix products: 119 us -> 81.3 us  [the longest x8 18.1 us: dot_t(): lax.dot_general(left, right, (((1,), (1,)), ((), ())), preferred_element_...]
    unnamed x218 -> x189, local copies, waits for them, and re-layouts: 49.5 us -> 15.9 us
    convert_element_type x23 -> x13, other arithmetic: 38.6 us -> 11 us  [the longest x2 7.63 us: attend_backward(): grad_scores = (probs * (grad_probs - inner)).astype(BF16)]
    all_gather x2, waiting for transfers between devices: 35.9 us -> 15.9 us  [the longest x1 15.9 us: per_device(): frames_all = lax.all_gather(frames, 'seq', axis=0, tiled=True)]
    unnamed x2 -> x1, blocking collectives: 44.4 us -> 24.8 us
  transfers between devices with their start and end apart: 21 -> 4, of which waited for: 18 -> 1; matrix products, arithmetic and copies ran while one was open for 16% -> 29% of each run, Pallas kernels for 0% -> 30%
where the time goes in v1:
time: 363 us; the launch traced here: 358 us
  Pallas kernels  109 us (30%)
  matrix products  81.3 us (22%)
  local copies, waits for them, and re-layouts  66.4 us (18%)
  other arithmetic  38.7 us (11%)
  blocking collectives  24.8 us (7%)
  between operations  18.8 us (5%)
  waiting for transfers between devices  16.6 us (5%)
    pallas_call x1, Pallas kernels, reduce_weights(): pl.pallas_call(reduce_kernel, out_shape=jax.ShapeDtypeStruct((CHUNKS, tal...  109 us
    unnamed x1, blocking collectives  24.8 us
    dot_general x8, matrix products, dot_t(): lax.dot_general(left, right, (((1,), (1,)), ((), ())), preferred_element_...  18.1 us
    dot_general x9, matrix products, dot(): return jnp.dot(left, right, preferred_element_type=F32)  18 us
    unnamed x189, local copies, waits for them, and re-layouts  15.9 us
    all_gather x1, waiting for transfers between devices, per_device(): frames_all = lax.all_gather(frames, 'seq', axis=0, tiled=True)  15.9 us
    dot_general x2, matrix products, attend_backward(): jnp.einsum('qhd,khd->hqk', up_heads, split_heads(valueset), preferred_ele...  12.4 us
    reshape x3, local copies, waits for them, and re-layouts, by_seq(): return table.reshape(table.shape[0], 4, -1).transpose(1, 0, 2)  11.9 us
  transfers between devices with their start and end apart: 4, of which 1 were waited for; matrix products, arithmetic and copies ran while one was open for 29% of the time, Pallas kernels for 30%

profile of v1, /device:TPU:0, one launch (start us, length us, event | category | flops | bytes accessed | tf_op | source)
XLA Modules:
  0.0 358.5 jit_solution(10334969078234439965)
XLA Ops:
  12.0 4.1 %convolution_add_fusion = f32[4,4608]{1,0:T(4,128)S(1)} fusion(bf16[768,4608]{1,0:T(8,128)(2,1)} %param.22, f32[4608]{0:T(1024)S(1)} %convert_element_type.220, bf16[1,4,768]{2,1,0:T(4,128)(2,1)} %param.19), kind=kOutput, calls=%fused_computation.15 | convolution fusion | flops 28348416 | bytes 7176192 | tf_op jit(solution)/shard_map/dot_general | solution.py:26
  17.2 2.6 convolution_convert_fusion.5
  19.9 2.0 copy.74
  23.3 0.8 copy.76
  27.6 15.9 %all-gather.6.cloned.1.call-done = bf16[1,1024,768]{2,1,0:T(8,128)(2,1)} async-done(((bf16[1,256,768]{2,1,0:T(8,128)(2,1)}), bf16[1,1024,768]{2,1,0:T(8,128)(2,1)}) %all-gather.6.cloned.1.call-update) | async-done | bytes 1572880 | tf_op jit(solution)/shard_map/all_gather | solution.py:293
  43.5 1.7 convert_reduce_fusion
  45.1 2.0 fusion.14
  48.6 1.6 fusion.17
  50.6 2.8 convolution_convert_fusion
  53.4 2.0 fusion.111
  55.4 1.8 copy.75
  57.2 2.0 fusion.9
  59.2 3.1 fusion.1
  62.3 1.6 copy-done.2
  64.0 1.6 copy.73
  65.6 6.9 %fusion.44 = bf16[12,64,256]{2,1,0:T(8,128)(2,1)S(1)} fusion(bf16[1024,12,64]{0,2,1:T(8,128)(2,1)} %bitcast.216, f32[12,256]{1,0:T(8,128)S(1)} %fusion.1, f32[12,256]{1,0:T(8,128)S(1)} %get-tuple-element.80, f32[12,256,1024]{2,1,0:T(8,128)} %copy-done.2, pred[1024]{0:T(1024)(128)(4,1)S(1)} %broadcast_compare_fusion), kind=kOutput, calls=%fused_computation.73 | convolution fusion | flops 418578432 | bytes 14574592 | tf_op jit(solution)/shard_map/hqk,khd->qhd/dot_general | solution.py:73
  72.5 1.4 fusion.109
  78.8 2.1 multiply_convert_fusion.2
  81.0 3.9 %convert_reduce_fusion.1 = (f32[3072]{0:T(1024)}, bf16[256,3072]{1,0:T(8,128)(2,1)S(1)}) fusion(f32[256,3072]{1,0:T(8,128)S(1)} %get-tuple-element.88, bf16[3072,768]{1,0:T(8,128)(2,1)S(1)} %bitcast.255, bf16[1,256,768]{2,1,0:T(8,128)(2,1)S(1)} %copy-done.79, f32[768]{0:T(1024)S(1)} %get-tuple-element.45), kind=kOutput, calls=%fused_computation.47 | convolution fusion | flops 1225847808 | bytes 9845760 | tf_op jit(solution)/shard_map/dot_general | solution.py:30
  84.9 2.2 multiply_reduce_fusion.3
  87.1 3.4 convert_reduce_fusion.3
  91.3 1.2 convolution_convert_fusion.3
  92.5 1.2 copy.79
  93.8 1.5 multiply_reduce_fusion.1
  95.8 1.2 multiply_reduce_fusion.2
  98.8 1.0 copy.80
  99.8 11.0 %multiply_reduce_fusion = (f32[12,256]{1,0:T(8,128)S(1)}, f32[12,256,1024]{2,1,0:T(8,128)}) fusion(f32[12,256]{1,0:T(8,128)S(1)} %log_add_fusion, f32[12,256,1024]{2,1,0:T(8,128)} %copy-done.2, pred[1024]{0:T(1024)(128)(4,1)S(1)} %broadcast_compare_fusion, bf16[256,12,64]{0,2,1:T(8,128)(2,1)} %bitcast.244, bf16[1024,12,64]{0,2,1:T(8,128)(2,1)} %bitcast.217), kind=kOutput, calls=%fused_computation.1 | convolution fusion | flops 418378752 | bytes 27157504 | tf_op jit(solution)/shard_map/qhd,khd->hqk/dot_general | solution.py:82
  110.8 6.6 %fusion.38 = bf16[12,64,1024]{2,1,0:T(8,128)(2,1)S(1)} fusion(bf16[256,12,64]{0,2,1:T(8,128)(2,1)S(1)} %bitcast.245, f32[12,256]{1,0:T(8,128)S(1)} %log_add_fusion, f32[12,256,1024]{2,1,0:T(8,128)} %copy-done.2, pred[1024]{0:T(1024)(128)(4,1)S(1)} %broadcast_compare_fusion), kind=kOutput, calls=%fused_computation.57 | convolution fusion | flops 416022528 | bytes 14562304 | tf_op jit(solution)/shard_map/hqk,qhd->khd/dot_general | solution.py:93
  117.4 7.4 %multiply_convert_fusion = bf16[12,256,1024]{2,1,0:T(8,128)(2,1)S(1)} fusion(f32[12,256,1024]{2,1,0:T(8,128)} %get-tuple-element.94, f32[12,256]{1,0:T(8,128)S(1)} %get-tuple-element.93, f32[12,256]{1,0:T(8,128)S(1)} %log_add_fusion, f32[12,256,1024]{2,1,0:T(8,128)S(1)} %bitcast.207, pred[1024]{0:T(1024)(128)(4,1)S(1)} %broadcast_compare_fusion), kind=kLoop, calls=%fused_computation | loop fusion | flops 18874368 | bytes 31482880 | tf_op jit(solution)/shard_map/convert_element_type | solution.py:86
  124.9 1.2 multiply_convert_fusion.1
  126.1 2.0 copy-done.3
  128.0 1.1 copy-done.7
  129.4 3.9 %fusion.33 = bf16[1024,768]{1,0:T(8,128)(2,1)} fusion(bf16[768,2304]{1,0:T(8,128)(2,1)S(1)} %copy-done.78, bf16[1024,768]{0,1:T(8,128)(2,1)S(1)} %bitcast.234, bf16[1024,768]{0,1:T(8,128)(2,1)S(1)} %bitcast.214), kind=kOutput, calls=%fused_computation.56 | convolution fusion | flops 2422996992 | bytes 7077888 | tf_op jit(solution)/shard_map/dot_general | solution.py:30
  133.4 0.9 copy.89
  134.9 5.0 %fusion.43 = bf16[12,64,256]{2,1,0:T(8,128)(2,1)S(1)} fusion(bf16[1024,12,64]{0,2,1:T(8,128)(2,1)S(1)} %bitcast.213, bf16[12,256,1024]{2,1,0:T(8,128)(2,1)} %copy-done.3), kind=kOutput, calls=%fused_computation.67 | convolution fusion | flops 403046400 | bytes 8257536 | tf_op jit(solution)/shard_map/hqk,khd->qhd/dot_general | solution.py:87
  140.1 1.3 copy-done.8
  141.4 2.5 pad_maximum_fusion
  143.9 7.9 %copy.88 = bf16[1024,4,576]{2,0,1:T(8,128)(2,1)} copy(bf16[1024,4,576]{0,2,1:T(8,128)(2,1)} %bitcast.211) | data formatting | bytes 9437184 | tf_op jit(solution)/shard_map/reshape | solution.py:416
  151.8 3.1 slice.133
  154.9 3.9 %slice.132.gq0 = bf16[4,1024,384]{2,1,0:T(8,128)(2,1)} slice(bf16[4,1024,576]{2,1,0:T(8,128)(2,1)} %bitcast.210), slice={[0:4], [0:1024], [0:384]} | slice | bytes 6291456 | tf_op jit(solution)/shard_map/slice | solution.py:444
  158.8 2.0 copy.85
  160.8 1.9 copy.83
  162.7 0.9 copy.87
  163.7 2.0 copy.90
  167.4 2.1 copy.84
  169.4 2.0 copy.86
  171.4 1.9 copy.91.gm_t
  173.3 1.5 convolution_convert_fusion.8
  174.8 0.8 broadcast_in_dim.38
  175.7 1.8 dynamic_update_slice.6
  177.5 24.8 %fusion = bf16[80,768]{1,0:T(8,128)(2,1)S(1)} fusion(bf16[308,768]{1,0:T(8,128)(2,1)} %dynamic_update_slice.6), kind=kCustom, calls=%all-reduce-scatter | all-reduce-scatter fusion | flops 245761 | bytes 596480
  202.4 2.5 collective-permute-start
  204.8 1.9 pad_maximum_fusion.2.lc
  206.8 2.5 fusion.41.gc
  209.3 2.4 pad_maximum_fusion.1.lq
  211.8 3.6 %fusion.64 = (f32[768]{0:T(1024)S(1)}, f32[256]{0:T(256)}, f32[256]{0:T(256)}, f32[768]{0:T(1024)S(1)}, f32[256,768]{1,0:T(8,128)}) fusion(bf16[1,256,768]{2,1,0:T(8,128)(2,1)S(1)} %copy-done.9, f32[256]{0:T(256)S(1)} %copy-done.62, f32[256]{0:T(256)S(1)} %copy-done.59, f32[768]{0:T(1024)S(1)} %get-tuple-element.48, ...), kind=kOutput, calls=%fused_computation.107 | convolution fusion | flops 304347136 | bytes 3159040 | tf_op jit(solution)/shard_map/dot_general | solution.py:30
  216.4 3.5 fusion.10.gq1
  219.8 109.2 %reduce_weights.1 = f32[8,96,384]{2,1,0:T(8,128)} custom-call(bf16[256,3072]{1,0:T(8,128)(2,1)} %copy-done.46, bf16[768,256]{1,0:T(8,128)(2,1)} %copy.91.gm_t, bf16[256,768]{1,0:T(8,128)(2,1)} %copy-done.48, bf16[256,3072]{1,0:T(8,128)(2,1)} %copy-done.47, bf16[512,768]{1,0:T(8,128)(2,1)} %pad_maximum_fusion.2.lc, bf16[4,512,384]{2,1,0:T(8,128)(2,1)} %fusion.41.gc, ...), custom_call_target="tpu_custom_call" | custom-call | tf_op jit(solution)/shard_map/reduce_weights/pallas_call | solution.py:246
  329.1 2.2 slice_bitcast_fusion.1
  335.3 0.9 copy.92
  336.3 1.2 fusion.63
  337.5 1.4 copy.95
  339.2 7.8 %convolution_reduce_fusion = f32[768]{0:T(1024)S(1)} fusion(f32[4608,1]{0,1:T(1,128)S(1)} %convolution_bitcast_fusion, bf16[768,4608]{1,0:T(8,128)(2,1)} %param.22), kind=kOutput, calls=%fused_computation.81 | convolution fusion | flops 42467328 | bytes 7099392 | tf_op jit(solution)/shard_map/dot_general | solution.py:398
  349.5 1.4 fusion.82
  (271 shorter events, 28.0 us)
Async XLA Ops:
  7.2 15.3 %copy-start = (bf16[1,308,768]{2,1,0:T(8,128)(2,1)S(1)}, bf16[1,308,768]{2,1,0:T(8,128)(2,1)}, u32[]{:S(2)}) copy-start(bf16[1,308,768]{2,1,0:T(8,128)(2,1)} %param.18) | copy-start | bytes 1419268
  7.2 36.3 %all-gather.6.cloned.1.call-start = ((), (), s32[]{:S(2)}) async-start(), calls=%async_computation.2 | async-start | bytes 1966080 | tf_op jit(solution)/shard_map/all_gather | solution.py:293
  7.9 203.9 %reduce-scatter.4.cloned.1.call-start = ((), (), s32[]{:S(2)}) async-start(), calls=%async_computation.1 | async-start | bytes 1966080 | tf_op jit(solution)/shard_map/reduce_scatter | solution.py:350
  8.8 18.6 %copy-start.74 = (s32[4]{0:T(128)}, s32[4]{0:T(128)S(1)}, u32[]{:S(2)}) copy-start(s32[4]{0:T(128)S(1)} %slice.94) | copy-start | bytes 52
  12.0 4.2 %copy-start.9 = (bf16[1,256,768]{2,1,0:T(8,128)(2,1)S(1)}, bf16[1,256,768]{2,1,0:T(8,128)(2,1)}, u32[]{:S(2)}) copy-start(bf16[1,256,768]{2,1,0:T(8,128)(2,1)} %param.17) | copy-start | bytes 1179652
  16.1 5.7 %copy-start.70 = (bf16[768]{0:T(1024)(128)(2,1)S(1)}, bf16[768]{0:T(1024)(128)(2,1)}, u32[]{:S(2)}) copy-start(bf16[768]{0:T(1024)(128)(2,1)} %param.26) | copy-start | bytes 4612
  16.1 6.4 %copy-start.10 = (bf16[768,1536]{1,0:T(8,128)(2,1)S(1)}, bf16[768,1536]{1,0:T(8,128)(2,1)}, u32[]{:S(2)}) copy-start(bf16[768,1536]{1,0:T(8,128)(2,1)} %param.28) | copy-start | bytes 7077892
  16.4 3.4 copy-start.58
  19.8 4.3 %copy-start.60 = (bf16[3072]{0:T(1024)(128)(2,1)S(1)}, bf16[3072]{0:T(1024)(128)(2,1)}, u32[]{:S(2)}) copy-start(bf16[3072]{0:T(1024)(128)(2,1)} %param.31) | copy-start | bytes 18436
  19.8 4.3 %copy-start.71 = (bf16[768]{0:T(1024)(128)(2,1)S(1)}, bf16[768]{0:T(1024)(128)(2,1)}, u32[]{:S(2)}) copy-start(bf16[768]{0:T(1024)(128)(2,1)} %param.33) | copy-start | bytes 4612
  19.8 5.0 %copy-start.76 = (u32[32]{0:T(128)S(1)}, u32[32]{0:T(128)}, u32[]{:S(2)}) copy-start(u32[32]{0:T(128)} %constant.120) | copy-start | bytes 388
  19.8 6.2 %copy-start.55 = (bf16[1,4,768]{2,1,0:T(4,128)(2,1)S(1)}, bf16[1,4,768]{2,1,0:T(4,128)(2,1)}, u32[]{:S(2)}) copy-start(bf16[1,4,768]{2,1,0:T(4,128)(2,1)} %param.19) | copy-start | bytes 18436
  19.8 6.8 %copy-start.64 = (s32[1,1024]{1,0:T(1,128)S(1)}, s32[1,1024]{1,0:T(1,128)}, u32[]{:S(2)}) copy-start(s32[1,1024]{1,0:T(1,128)} %param.20) | copy-start | bytes 12292
  23.3 52.5 %copy-start.34 = (bf16[77,768]{0,1:T(8,128)(2,1)}, bf16[77,768]{0,1:T(8,128)(2,1)S(1)}, u32[]{:S(2)}) copy-start(bf16[77,768]{0,1:T(8,128)(2,1)S(1)} %copy.78) | copy-start | bytes 354820
  50.6 2.8 copy-start.16
  59.2 4.7 %copy-start.2 = (f32[12,256,1024]{2,1,0:T(8,128)}, f32[12,256,1024]{2,1,0:T(8,128)S(1)}, u32[]{:S(2)}) copy-start(f32[12,256,1024]{2,1,0:T(8,128)S(1)} %get-tuple-element.81) | copy-start | bytes 37748740
  59.2 4.7 %copy-start.15 = (bf16[1024,768]{1,0:T(8,128)(2,1)S(1)}, bf16[1024,768]{1,0:T(8,128)(2,1)}, u32[]{:S(2)}) copy-start(bf16[1024,768]{1,0:T(8,128)(2,1)} %get-tuple-element.58) | copy-start | bytes 4718596
  65.6 6.9 %copy-start.19 = (bf16[768,768]{1,0:T(8,128)(2,1)S(1)}, bf16[768,768]{1,0:T(8,128)(2,1)}, u32[]{:S(2)}) copy-start(bf16[768,768]{1,0:T(8,128)(2,1)} %param.25) | copy-start | bytes 3538948
  72.5 2.6 copy-start.49
  75.8 2.8 slice-start.3
  76.4 2.4 slice-start.4
  78.1 2.9 slice-start.5
  81.0 6.2 %copy-start.46 = (bf16[256,3072]{1,0:T(8,128)(2,1)}, bf16[256,3072]{1,0:T(8,128)(2,1)S(1)}, u32[]{:S(2)}) copy-start(bf16[256,3072]{1,0:T(8,128)(2,1)S(1)} %get-tuple-element.87.act) | copy-start | bytes 4718596
  92.5 3.0 copy-start.35
  97.4 13.3 %copy-start.13 = (f32[256,768]{1,0:T(8,128)}, f32[256,768]{1,0:T(8,128)S(1)}, u32[]{:S(2)}) copy-start(f32[256,768]{1,0:T(8,128)S(1)} %get-tuple-element.52) | copy-start | bytes 2359300
  98.3 12.5 %copy-start.28 = (bf16[256,768]{1,0:T(8,128)(2,1)}, bf16[256,768]{1,0:T(8,128)(2,1)S(1)}, u32[]{:S(2)}) copy-start(bf16[256,768]{1,0:T(8,128)(2,1)S(1)} %multiply_convert_fusion.4) | copy-start | bytes 1179652
  99.7 11.0 %copy-start.45 = (bf16[256,768]{0,1:T(8,128)(2,1)S(1)}, bf16[256,768]{0,1:T(8,128)(2,1)}, u32[]{:S(2)}) copy-start(bf16[256,768]{0,1:T(8,128)(2,1)} %copy.80) | copy-start | bytes 1179652
  99.8 17.6 %slice-start = ((s8[12582912]{0:T(1024)(128)(4,1)}), s8[4194304]{0:T(1024)(128)(4,1)S(1)}, s32[]{:S(2)}) async-start(s8[12582912]{0:T(1024)(128)(4,1)} %bitcast.206), calls=%async_computation.4 | async-start | bytes 8388608
  99.8 17.6 %slice-start.1 = ((s8[12582912]{0:T(1024)(128)(4,1)}), s8[4194304]{0:T(1024)(128)(4,1)S(1)}, s32[]{:S(2)}) async-start(s8[12582912]{0:T(1024)(128)(4,1)} %bitcast.206), calls=%async_computation.5 | async-start | bytes 8388608
  110.7 6.7 %slice-start.2 = ((s8[12582912]{0:T(1024)(128)(4,1)}), s8[4194304]{0:T(1024)(128)(4,1)S(1)}, s32[]{:S(2)}) async-start(s8[12582912]{0:T(1024)(128)(4,1)} %bitcast.206), calls=%async_computation.6 | async-start | bytes 8388608
  117.4 10.7 %copy-start.38 = (bf16[12,64,1024]{2,1,0:T(8,128)(2,1)}, bf16[12,64,1024]{2,1,0:T(8,128)(2,1)S(1)}, u32[]{:S(2)}) copy-start(bf16[12,64,1024]{2,1,0:T(8,128)(2,1)S(1)} %fusion.38) | copy-start | bytes 4718596
  124.8 3.2 copy-start.3
  124.8 4.6 %copy-start.78 = (bf16[768,2304]{1,0:T(8,128)(2,1)S(1)}, bf16[768,2304]{1,0:T(8,128)(2,1)}, u32[]{:S(2)}) copy-start(bf16[768,2304]{1,0:T(8,128)(2,1)} %param.24) | copy-start | bytes 10616836
  129.4 4.0 %copy-start.29 = (bf16[256,768]{1,0:T(8,128)(2,1)S(1)}, bf16[256,768]{1,0:T(8,128)(2,1)}, u32[]{:S(2)}) copy-start(bf16[256,768]{1,0:T(8,128)(2,1)} %copy-done.28) | copy-start | bytes 1179652
  133.3 204.1 %all-gather.8.cloned.1.call-start = ((), (), s32[]{:S(2)}) async-start(), calls=%async_computation.3 | async-start | bytes 1317888 | tf_op jit(solution)/shard_map/all_gather | solution.py:369
  134.9 5.2 %copy-start.39 = (bf16[12,64,1024]{2,1,0:T(8,128)(2,1)S(1)}, bf16[12,64,1024]{2,1,0:T(8,128)(2,1)}, u32[]{:S(2)}) copy-start(bf16[12,64,1024]{2,1,0:T(8,128)(2,1)} %copy-done.38) | copy-start | bytes 4718596
  139.8 4.1 %copy-start.36 = (bf16[12,64,256]{2,1,0:T(8,128)(2,1)}, bf16[12,64,256]{2,1,0:T(8,128)(2,1)S(1)}, u32[]{:S(2)}) copy-start(bf16[12,64,256]{2,1,0:T(8,128)(2,1)S(1)} %fusion.43) | copy-start | bytes 1179652
  154.9 7.9 %copy-start.41 = (bf16[12,64,256]{2,1,0:T(8,128)(2,1)S(1)}, bf16[12,64,256]{2,1,0:T(8,128)(2,1)}, u32[]{:S(2)}) copy-start(bf16[12,64,256]{2,1,0:T(8,128)(2,1)} %copy-done.40) | copy-start | bytes 1179652
  158.8 6.9 %copy-start.23 = (bf16[12,256,77]{1,2,0:T(8,128)(2,1)S(1)}, bf16[12,256,77]{1,2,0:T(8,128)(2,1)}, u32[]{:S(2)}) copy-start(bf16[12,256,77]{1,2,0:T(8,128)(2,1)} %copy-done.22) | copy-start | bytes 1419268
  158.8 6.9 %copy-start.25 = (bf16[256,768]{0,1:T(8,128)(2,1)S(1)}, bf16[256,768]{0,1:T(8,128)(2,1)}, u32[]{:S(2)}) copy-start(bf16[256,768]{0,1:T(8,128)(2,1)} %copy-done.24) | copy-start | bytes 1179652
  158.8 7.3 %copy-start.27 = (bf16[256,768]{0,1:T(8,128)(2,1)S(1)}, bf16[256,768]{0,1:T(8,128)(2,1)}, u32[]{:S(2)}) copy-start(bf16[256,768]{0,1:T(8,128)(2,1)} %copy-done.26) | copy-start | bytes 1179652
  166.4 6.9 %copy-start.11 = (bf16[768,1536]{1,0:T(8,128)(2,1)S(1)}, bf16[768,1536]{1,0:T(8,128)(2,1)}, u32[]{:S(2)}) copy-start(bf16[768,1536]{1,0:T(8,128)(2,1)} %param.28) | copy-start | bytes 7077892
  167.3 37.5 %copy-start.31 = (bf16[256,768]{1,0:T(8,128)(2,1)S(1)}, bf16[256,768]{1,0:T(8,128)(2,1)}, u32[]{:S(2)}) copy-start(bf16[256,768]{1,0:T(8,128)(2,1)} %copy-done.30) | copy-start | bytes 1179652
  174.8 32.0 %copy-start.33 = (bf16[256,4,192]{2,0,1:T(8,128)(2,1)S(1)}, bf16[256,4,192]{2,0,1:T(8,128)(2,1)}, u32[]{:S(2)}) copy-start(bf16[256,4,192]{2,0,1:T(8,128)(2,1)} %copy.84) | copy-start | bytes 1179652
  174.8 34.5 %copy-start.17 = (bf16[1024,768]{1,0:T(8,128)(2,1)S(1)}, bf16[1024,768]{1,0:T(8,128)(2,1)}, u32[]{:S(2)}) copy-start(bf16[1024,768]{1,0:T(8,128)(2,1)} %copy-done.16) | copy-start | bytes 4718596
  202.4 132.6 %collective-permute-start = (bf16[9,768]{1,0:T(8,128)(2,1)S(1)}, bf16[9,768]{1,0:T(8,128)(2,1)S(1)}, u32[]{:S(2)}, u32[]{:S(2)}) collective-permute-start(bf16[9,768]{1,0:T(8,128)(2,1)S(1)} %slice.141), channel_id=1, source_target_pairs={{0,8},{8,16},{16,24},{1,9},{9,17},{17,25},{2,10},{10,18},{18,26},{... | collective-permute-start | bytes 41480
  206.8 5.0 %copy-start.37 = (bf16[12,64,256]{2,1,0:T(8,128)(2,1)S(1)}, bf16[12,64,256]{2,1,0:T(8,128)(2,1)}, u32[]{:S(2)}) copy-start(bf16[12,64,256]{2,1,0:T(8,128)(2,1)} %copy-done.36) | copy-start | bytes 1179652
  206.8 5.0 %copy-start.59 = (f32[256]{0:T(256)S(1)}, f32[256]{0:T(256)}, u32[]{:S(2)}) copy-start(f32[256]{0:T(256)} %copy-done.58) | copy-start | bytes 3076
  206.8 5.0 %copy-start.62 = (f32[256]{0:T(256)S(1)}, f32[256]{0:T(256)}, u32[]{:S(2)}) copy-start(f32[256]{0:T(256)} %copy-done.61) | copy-start | bytes 3076
  211.7 3.8 %copy-start.54 = (f32[9984]{0:T(1024)S(1)}, f32[9984]{0:T(1024)}, u32[]{:S(2)}) copy-start(f32[9984]{0:T(1024)} %custom-call) | copy-start | bytes 119812
  211.7 3.8 %copy-start.67 = (f32[768]{0:T(1024)S(1)}, f32[768]{0:T(1024)}, u32[]{:S(2)}) copy-start(f32[768]{0:T(1024)} %get-tuple-element.41) | copy-start | bytes 9220
  211.7 3.8 %copy-start.66 = (f32[768]{0:T(1024)S(1)}, f32[768]{0:T(1024)}, u32[]{:S(2)}) copy-start(f32[768]{0:T(1024)} %get-tuple-element.34) | copy-start | bytes 9220
  211.7 3.8 %copy-start.68 = (f32[768]{0:T(1024)S(1)}, f32[768]{0:T(1024)}, u32[]{:S(2)}) copy-start(f32[768]{0:T(1024)} %get-tuple-element.44) | copy-start | bytes 9220
  211.7 3.9 %copy-start.69 = (f32[768]{0:T(1024)S(1)}, f32[768]{0:T(1024)}, u32[]{:S(2)}) copy-start(f32[768]{0:T(1024)} %get-tuple-element.32) | copy-start | bytes 9220
  211.8 3.9 %copy-start.57 = (f32[3072]{0:T(1024)S(1)}, f32[3072]{0:T(1024)}, u32[]{:S(2)}) copy-start(f32[3072]{0:T(1024)} %get-tuple-element.96) | copy-start | bytes 36868
  211.8 3.9 %copy-start.65 = (f32[768]{0:T(1024)S(1)}, f32[768]{0:T(1024)}, u32[]{:S(2)}) copy-start(f32[768]{0:T(1024)} %get-tuple-element.43) | copy-start | bytes 9220
  211.8 4.6 %copy-start.12 = (bf16[4,1024,192]{2,1,0:T(8,128)(2,1)S(1)}, bf16[4,1024,192]{2,1,0:T(8,128)(2,1)}, u32[]{:S(2)}) copy-start(bf16[4,1024,192]{2,1,0:T(8,128)(2,1)} %slice.133) | copy-start | bytes 4718596
  329.1 7.2 %copy-start.73 = (f32[256]{0:T(256)S(1)}, f32[256]{0:T(256)}, u32[]{:S(2)}) copy-start(f32[256]{0:T(256)} %get-tuple-element.37) | copy-start | bytes 3076
  329.1 7.1 %copy-start.72 = (f32[256]{0:T(256)S(1)}, f32[256]{0:T(256)}, u32[]{:S(2)}) copy-start(f32[256]{0:T(256)} %get-tuple-element.38) | copy-start | bytes 3076
  329.1 7.1 %copy-start.14 = (f32[256,768]{1,0:T(8,128)S(1)}, f32[256,768]{1,0:T(8,128)}, u32[]{:S(2)}) copy-start(f32[256,768]{1,0:T(8,128)} %copy-done.13) | copy-start | bytes 2359300
  329.1 7.1 %copy-start.52 = (f32[256,768]{1,0:T(8,128)S(1)}, f32[256,768]{1,0:T(8,128)}, u32[]{:S(2)}) copy-start(f32[256,768]{1,0:T(8,128)} %get-tuple-element.95) | copy-start | bytes 2359300
  329.1 7.1 %copy-start.63 = (f32[256]{0:T(256)S(1)}, f32[256]{0:T(256)}, u32[]{:S(2)}) copy-start(f32[256]{0:T(256)} %copy-done.61) | copy-start | bytes 3076
  339.0 12.5 %copy-start.1 = (bf16[1,308,768]{2,1,0:T(8,128)(2,1)S(1)}, bf16[1,308,768]{2,1,0:T(8,128)(2,1)}, u32[]{:S(2)}) copy-start(bf16[1,308,768]{2,1,0:T(8,128)(2,1)} %param.18) | copy-start | bytes 1419268
  339.2 7.8 %copy-start.56 = (f32[768]{0:T(1024)S(1)}, f32[768]{0:T(1024)}, u32[]{:S(2)}) copy-start(f32[768]{0:T(1024)} %convert_reduce_fusion.4) | copy-start | bytes 9220
  (27 other events, 42.1 us)
Sparse Core Ops, SparseCore 0:
  9.8 33.5 all-gather.5
  133.5 31.1 reduce-scatter.3
  216.5 59.1 all-gather.7

commit v2 on v1

--- a/solution.py
+++ b/solution.py
@@ -19,7 +19,7 @@
 BF16 = jnp.bfloat16
 MESH = pl.DeviceIdType.MESH
 CHUNKS = 8
-VMEM_MOST = 66_000_000
+VMEM_MOST = 67_043_328
 
 
 def dot(left, right):
@@ -100,179 +100,13 @@
     )
 
 
-def reduce_kernel(
-    act, gm_t, h3, gpre, lc, gc, text, gkv, lq, gq0, gq1,
-    out,
-    G, R0, R1, R2, R3,
-    s0, r0, s1, r1, s2, r2, s3, r3,
-):
-    seq = lax.axis_index("seq")
-    rows = lax.axis_index("rows")
-    y, x = seq // 2, seq % 2
-    z, c = rows // 2, rows % 2
-    core_peer = {"rows": z * 2 + (1 - c)}
-    x_peer = {"seq": y * 2 + (1 - x)}
-    y_peer = {"seq": (1 - y) * 2 + x}
-    z_peers = [{"rows": lax.rem(z + d, 4) * 2 + c} for d in (1, 2, 3)]
-
-    barrier = pltpu.get_barrier_semaphore()
-    for peer in [core_peer, x_peer, y_peer] + z_peers:
-        pl.semaphore_signal(barrier, inc=1, device_id=peer, device_id_type=MESH)
-    pl.semaphore_wait(barrier, 6)
-
-    width = G.shape[-1]
-    tall = G.shape[-2]
-
-    def put(k, s, block):
-        low = block.astype(BF16)
-        for zz in range(4):
-            for cc in range(2):
-                at = (zz * 2 + cc) * tall
-                G[k, cc, zz, s // 2, s % 2] = low[at : at + tall]
-
-    def compute(k):
-        @pl.loop(0, 4)
-        def _(s):
-            if k < 2:
-                left = gm_t[pl.ds(pl.multiple_of(s * 2 * tall + k * tall, 16), tall), :]
-                for r in range(8):
-                    G[k, r % 2, r // 2, s // 2, s % 2] = dot(
-                        left, act[:, r * width : (r + 1) * width]
-                    ).astype(BF16)
-            elif k < 4:
-                at = pl.multiple_of(s * 2 * width + (k - 2) * width, 128)
-                put(k, s, t_dot(h3[...], gpre[:, pl.ds(at, width)]))
-            elif k == 4:
-                put(k, s, t_dot(lc[...], gc[s]))
-            elif k == 5:
-                at = pl.multiple_of(s * width, 128)
-                put(k, s, t_dot(text[...], gkv[:, pl.ds(at, width)]))
-            elif k == 6:
-                put(k, s, t_dot(lq[: gq0.shape[1], :], gq0[s]))
-            else:
-                put(k, s, t_dot(lq[...], gq1[s]))
-
-    def remote(src, dst, send, recv, peer):
-        return pltpu.make_async_remote_copy(
-            src_ref=src, dst_ref=dst, send_sem=send, recv_sem=recv,
-            device_id=peer, device_id_type=MESH,
-        )
-
-    def core_copy(k):
-        return remote(G.at[k, 1 - c], R0.at[k], s0.at[k], r0.at[k], core_peer)
-
-    def first_copies(k):
-        return (
-            remote(G.at[k, c, 0:2, :, 1 - x], R1.at[k, 0], s1.at[k, 0], r1.at[k, 0], x_peer),
-            remote(G.at[k, c, 2:4, 1 - y], R1.at[k, 1], s1.at[k, 1], r1.at[k, 1], y_peer),
-        )
-
-    def second_copies(k):
-        return (
-            remote(G.at[k, c, 0:2, 1 - y, x], R2.at[k, 0], s2.at[k, 0], r2.at[k, 0], y_peer),
-            remote(G.at[k, c, 2:4, y, 1 - x], R2.at[k, 1], s2.at[k, 1], r2.at[k, 1], x_peer),
-        )
-
-    def z_copies(k):
-        return [
-            remote(
-                G.at[k, c, lax.rem(z + d, 4), y, x], R3.at[k, d - 1],
-                s3.at[k, d - 1], r3.at[k, d - 1], z_peers[d - 1],
-            )
-            for d in (1, 2, 3)
-        ]
-
-    def add(one, two):
-        return (one.astype(F32) + two.astype(F32)).astype(BF16)
-
-    def phase0(k):
-        compute(k)
-        core_copy(k).start()
-
-    def phase1(k):
-        core_copy(k).wait_recv()
-
-        @pl.loop(0, 4)
-        def _(zz):
-            for yy in range(2):
-                for xx in range(2):
-                    G[k, c, zz, yy, xx] = add(G[k, c, zz, yy, xx], R0[k, zz, yy, xx])
-
-        for copy in first_copies(k):
-            copy.start()
-
-    def phase2(k):
-        for copy in first_copies(k):
-            copy.wait_recv()
-        for zz in range(2):
-            for other in range(2):
-                G[k, c, zz, other, x] = add(G[k, c, zz, other, x], R1[k, 0, zz, other])
-                G[k, c, 2 + zz, y, other] = add(G[k, c, 2 + zz, y, other], R1[k, 1, zz, other])
-        for copy in second_copies(k):
-            copy.start()
-
-    def phase3(k):
-        for copy in second_copies(k):
-            copy.wait_recv()
-        for zz in range(2):
-            G[k, c, zz, y, x] = add(G[k, c, zz, y, x], R2[k, 0, zz])
-            G[k, c, 2 + zz, y, x] = add(G[k, c, 2 + zz, y, x], R2[k, 1, zz])
-        for copy in z_copies(k):
-            copy.start()
-
-    def phase4(k):
-        for copy in z_copies(k):
-            copy.wait_recv()
-        total = G[k, c, z, y, x].astype(F32)
-        for d in range(3):
-            total = total + R3[k, d].astype(F32)
-        out[k] = total
-
-    phases = (phase0, phase1, phase2, phase3, phase4)
-    for wave in range(CHUNKS + 4):
-        for depth in (4, 3, 2, 1, 0):
-            if 0 <= wave - depth < CHUNKS:
-                phases[depth](wave - depth)
-    for k in range(CHUNKS):
-        core_copy(k).wait_send()
-        for copy in (*first_copies(k), *second_copies(k), *z_copies(k)):
-            copy.wait_send()
-
-
-def reduce_weights(ops, model):
-    tall, width = model // 8, model // 2
-    block = (CHUNKS, 2, 4, 2, 2, tall, width)
-    dma = pltpu.SemaphoreType.DMA
-    return pl.pallas_call(
-        reduce_kernel,
-        out_shape=jax.ShapeDtypeStruct((CHUNKS, tall, width), F32),
-        in_specs=[pl.BlockSpec(memory_space=pltpu.VMEM)] * len(ops),
-        out_specs=pl.BlockSpec(memory_space=pltpu.VMEM),
-        scratch_shapes=[
-            pltpu.VMEM(block, BF16),
-            pltpu.VMEM((CHUNKS, 4, 2, 2, tall, width), BF16),
-            pltpu.VMEM((CHUNKS, 2, 2, 2, tall, width), BF16),
-            pltpu.VMEM((CHUNKS, 2, 2, tall, width), BF16),
-            pltpu.VMEM((CHUNKS, 3, tall, width), BF16),
-            dma((CHUNKS,)), dma((CHUNKS,)),
-            dma((CHUNKS, 2)), dma((CHUNKS, 2)),
-            dma((CHUNKS, 2)), dma((CHUNKS, 2)),
-            dma((CHUNKS, 3)), dma((CHUNKS, 3)),
-        ],
-        compiler_params=pltpu.CompilerParams(
-            collective_id=0, has_side_effects=True, vmem_limit_bytes=VMEM_MOST
-        ),
-        name="reduce_weights",
-    )(*ops)
-
-
 def scatter_plain(matrix):
     part = lax.psum_scatter(matrix.astype(BF16), "rows", scatter_dimension=0, tiled=True)
     part = lax.psum_scatter(part, "seq", scatter_dimension=1, tiled=True)
     return part.astype(F32)
 
 
-def per_device(
+def per_device_plain(
     frames, text_tokens, step_embed, segments, cotangent,
     w_ada, b_ada, w_qkv, w_out, g_cross, w_cq, w_ckv, w_co, w_up, b_up, w_down, b_down,
 ):
@@ -409,60 +243,750 @@
     )
     d_text = lax.psum_scatter(text_full, "seq", scatter_dimension=0, tiled=True).astype(F32)
 
-    if rows_count == 8 and seq_count == 4:
-        half = model // 2
-
-        def by_seq(table):
-            return table.reshape(table.shape[0], 4, -1).transpose(1, 0, 2)
-
-        pad_text = (-TXT) % 16
-        zero_c = jnp.zeros((4, here, model // 4), BF16)
-        gc = jnp.concatenate(
-            [
-                jnp.concatenate([by_seq(grad_qc), zero_c], axis=2),
-                jnp.concatenate([zero_c, by_seq(grad_c)], axis=2),
-            ],
-            axis=1,
-        )
-        query_full = lax.dynamic_update_slice_in_dim(
-            jnp.zeros((length, model), BF16), grad_qa, seq_index * here, axis=0
-        )
-        gqkv = by_seq(jnp.concatenate([query_full, grad_kva], axis=1))
-        rest = gqkv[:, :, half:]
-        gq1 = jnp.concatenate(
-            [
-                jnp.pad(rest, ((0, 0), (0, 0), (0, half - rest.shape[2]))),
-                jnp.pad(by_seq(grad_a), ((0, 0), (0, 0), (rest.shape[2], 0))),
-            ],
-            axis=1,
-        )
-        ops = (
-            act_low, grad_m.T, h_three, grad_pre,
-            jnp.concatenate([h_two, cross_low], axis=0), gc,
-            jnp.pad(text_mine, ((0, pad_text), (0, 0))),
-            jnp.pad(grad_kvc, ((0, pad_text), (0, 0))),
-            jnp.concatenate([h_all, attn_low], axis=0), gqkv[:, :, :half], gq1,
-        )
-        done = reduce_weights(ops, model)
-        d_w_down = jnp.concatenate([done[0], done[1]], axis=0).T
-        d_w_up = jnp.concatenate([done[2], done[3]], axis=1)
-        d_w_cq, d_w_co = done[4][:, : model // 4], done[4][:, model // 4 :]
-        d_w_ckv = done[5]
-        last = done[7]
-        d_w_qkv = jnp.concatenate([done[6], last[:, : rest.shape[2]]], axis=1)
-        d_w_out = last[:, rest.shape[2] :]
-    else:
-        d_w_down = scatter_plain(t_dot(act_low, grad_m))
-        d_w_up = scatter_plain(t_dot(h_three, grad_pre))
-        d_w_cq = scatter_plain(t_dot(h_two, grad_qc))
-        d_w_co = scatter_plain(t_dot(cross_low, grad_c))
-        d_w_ckv = scatter_plain(t_dot(text_mine, grad_kvc))
-        d_w_out = scatter_plain(t_dot(attn_low, grad_a))
-        d_w_qkv = scatter_plain(
-            jnp.concatenate([t_dot(h_one, grad_qa), t_dot(h_all, grad_kva)], axis=1)
-        )
+    d_w_down = scatter_plain(t_dot(act_low, grad_m))
+    d_w_up = scatter_plain(t_dot(h_three, grad_pre))
+    d_w_cq = scatter_plain(t_dot(h_two, grad_qc))
+    d_w_co = scatter_plain(t_dot(cross_low, grad_c))
+    d_w_ckv = scatter_plain(t_dot(text_mine, grad_kvc))
+    d_w_out = scatter_plain(t_dot(attn_low, grad_a))
+    d_w_qkv = scatter_plain(
+        jnp.concatenate([t_dot(h_one, grad_qa), t_dot(h_all, grad_kva)], axis=1)
+    )
     return (
         output[None], d_frames[None], d_text[None], d_step[None],
+        d_w_ada, d_b_ada, d_w_qkv, d_w_out, d_g_cross, d_w_cq, d_w_ckv, d_w_co,
+        d_w_up, d_b_up, d_w_down, d_b_down,
+    )
+
+
+def remote(src, dst, send, recv, peer):
+    return pltpu.make_async_remote_copy(
+        src_ref=src, dst_ref=dst, send_sem=send, recv_sem=recv,
+        device_id=peer, device_id_type=MESH,
+    )
+
+
+def enter(peers):
+    barrier = pltpu.get_barrier_semaphore()
+    for peer in peers:
+        pl.semaphore_signal(barrier, inc=1, device_id=peer, device_id_type=MESH)
+    pl.semaphore_wait(barrier, len(peers))
+
+
+def low_half(shape):
+    return lax.broadcasted_iota(jnp.int32, shape, len(shape) - 1) < HEAD
+
+
+def pick_half(pair, half):
+    lower = low_half(pair.shape)
+    return jnp.where(lower if half == 0 else ~lower, pair, jnp.zeros_like(pair))
+
+
+def join_halves(first, second):
+    return jnp.where(low_half(first.shape), first, second)
+
+
+def lanes(index, count=1):
+    return pl.ds(pl.multiple_of(index * 128, 128), 128 * count)
+
+
+def col_sum(values):
+    return jnp.sum(values, axis=0, keepdims=True)
+
+
+def softmax_rows(scores):
+    top = jnp.max(scores, axis=-1, keepdims=True)
+    raised = jnp.exp(scores - top)
+    total = jnp.sum(raised, axis=-1, keepdims=True)
+    return raised / total, top + jnp.log(total)
+
+
+def forward_kernel(
+    frames, cot, text, step, picks, mask,
+    w_ada, b_ada, w_qkv, w_out, g_cross, w_cq, w_ckv, w_co, w_up, b_up, w_down, b_down,
+    output, act, gm_t, h3, gpre, h2, cross, gqc, gc, gkvc, attn, ga, gattn, gx1, query,
+    kv, h_all, lse, mods, text_part, early,
+    fr, ada_v, qkv_v, out_v, cq_v, ckv_v, co_v, up_v, down_v, prob_c, acc_m, acc_u,
+    item, local, send, recv,
+):
+    seq = lax.axis_index("seq")
+    y, x = seq // 2, seq % 2
+    x_id, y_id, d_id = y * 2 + 1 - x, (1 - y) * 2 + x, (1 - y) * 2 + 1 - x
+    x_peer, y_peer = {"seq": x_id}, {"seq": y_id}
+    model = frames.shape[1]
+    here = frames.shape[0]
+    part = here // 2
+    loads = [
+        pltpu.make_async_copy(src, dst, local.at[i])
+        for i, (src, dst) in enumerate(
+            [
+                (frames, fr.at[seq]), (w_ada, ada_v), (w_qkv, qkv_v), (w_out, out_v),
+                (w_ckv, ckv_v), (w_cq, cq_v), (w_co, co_v), (w_up, up_v), (w_down, down_v),
+            ]
+        )
+    ]
+    for load in loads:
+        load.start()
+    enter([x_peer, y_peer])
+    to_x = remote(frames, fr.at[seq], send.at[0], recv.at[0], x_peer)
+    to_y = remote(frames, fr.at[seq], send.at[1], recv.at[1], y_peer)
+    to_x.start()
+    to_y.start()
+
+    def row(at):
+        return mods[at : at + 1, :]
+
+    step_f32 = step[...].astype(F32)
+    ada = (step_f32 / (1.0 + jnp.exp(-step_f32))).astype(BF16)
+    loads[1].wait()
+    item[...] = dot(ada, ada_v[...]) + b_ada[...].astype(F32)
+    for part_at in range(6):
+        mods[part_at : part_at + 1, :] = col_sum(
+            item[:, part_at * model : (part_at + 1) * model] * picks[4]
+        )
+    early[10:11, :] = col_sum(ada.astype(F32) * picks[4])
+
+    def take(block):
+        chosen = picks[block]
+        shift = col_sum(item[:, :model] * chosen)
+        scale = col_sum(item[:, model : 2 * model] * chosen)
+        normed, unused = norm_parts(fr[block].astype(F32))
+        rows_at = pl.ds(pl.multiple_of(block * here, here), here)
+        h_block = (normed * (1.0 + scale) + shift).astype(BF16)
+        h_all[rows_at, :] = h_block
+        kv[rows_at, :] = dot(h_block, qkv_v[:, model:]).astype(BF16)
+        return h_block
+
+    loads[0].wait()
+    loads[2].wait()
+    h_one = take(seq)
+    query[...] = dot(h_one, qkv_v[:, :model]).astype(BF16)
+    to_x.wait_recv()
+    fwd_y = remote(
+        fr.at[x_id, pl.ds(0, part)], fr.at[x_id, pl.ds(0, part)], send.at[2], recv.at[2], y_peer
+    )
+    fwd_y.start()
+    to_y.wait_recv()
+    fwd_x = remote(
+        fr.at[y_id, pl.ds(part, part)], fr.at[y_id, pl.ds(part, part)],
+        send.at[3], recv.at[3], x_peer,
+    )
+    fwd_x.start()
+    take(x_id)
+    take(y_id)
+    loads[4].wait()
+    text_kv = dot(text[...], ckv_v[...]).astype(BF16)
+    gkvc[...] = text_kv
+    fwd_y.wait_recv()
+    fwd_x.wait_recv()
+    take(d_id)
+
+    lse[...] = jnp.zeros_like(lse)
+    lane_of = lax.broadcasted_iota(jnp.int32, lse.shape, 1)
+
+    @pl.loop(0, HEADS // 2)
+    def _(p):
+        at = lanes(p)
+        value_at = lanes(p + HEADS // 2)
+        pair = query[:, at] * jnp.asarray(HEAD ** (-0.5), BF16)
+        outs = []
+        for half in range(2):
+            scores = dot_t(pick_half(pair, half), kv[:, at])
+            scores = jnp.where(mask[...] > 0.5, scores, NEG_FILL)
+            probs, log_total = softmax_rows(scores)
+            lse[...] = jnp.where(lane_of == 2 * p + half, log_total, lse[...])
+            outs.append(dot(probs.astype(BF16), kv[:, value_at]))
+        attn[:, at] = join_halves(*outs).astype(BF16)
+
+    loads[3].wait()
+    branch_a = dot(attn[...], out_v[...])
+    x_one = frames_f32(fr[seq]) + row(2) * branch_a
+    gx1[...] = branch_a
+    gain = g_cross[...].astype(F32)
+    normed_1, inverse_1 = norm_parts(x_one)
+    h2[...] = (normed_1 * gain).astype(BF16)
+    loads[5].wait()
+    query_c = dot(h2[...], cq_v[...]).astype(BF16)
+    gqc[...] = query_c
+
+    text_rows = text.shape[0]
+    key_lane = lax.broadcasted_iota(jnp.int32, (here, text_rows), 1)
+
+    @pl.loop(0, HEADS // 2)
+    def _(p):
+        at = lanes(p)
+        value_at = lanes(p + HEADS // 2)
+        pair = gqc[:, at] * jnp.asarray(HEAD ** (-0.5), BF16)
+        outs = []
+        for half in range(2):
+            scores = dot_t(pick_half(pair, half), gkvc[:, at])
+            probs, unused = softmax_rows(jnp.where(key_lane < TXT, scores, NEG_FILL))
+            prob_c[2 * p + half] = probs
+            outs.append(dot(probs.astype(BF16), gkvc[:, value_at]))
+        cross[:, at] = join_halves(*outs).astype(BF16)
+
+    loads[6].wait()
+    x_two = x_one + dot(cross[...], co_v[...])
+    normed_2, inverse_2 = norm_parts(x_two)
+    h3[...] = (normed_2 * (1.0 + row(4)) + row(3)).astype(BF16)
+    grad_out = cot[...].astype(F32)
+    grad_m = row(5) * grad_out
+    gm_low = grad_m.astype(BF16)
+    gm_t[...] = gm_low.astype(F32).T.astype(BF16)
+    early[9:10, :] = col_sum(gm_low.astype(F32))
+    gc[...] = gm_low
+    acc_m[...] = jnp.zeros_like(acc_m)
+    acc_u[...] = jnp.zeros_like(acc_u)
+    loads[7].wait()
+    loads[8].wait()
+    slab = model // 2
+
+    @pl.loop(0, w_up.shape[1] // slab)
+    def _(j):
+        at = pl.ds(pl.multiple_of(j * slab, slab), slab)
+        pre = dot(h3[...], up_v[:, at]) + b_up[:, at].astype(F32)
+        inner = GELU_SCALE * (pre + 0.044715 * pre * pre * pre)
+        tanh = jnp.tanh(inner)
+        act_low = (0.5 * pre * (1.0 + tanh)).astype(BF16)
+        act[:, at] = act_low
+        acc_m[...] += dot(act_low, down_v[at, :])
+        slope = 0.5 * (1.0 + tanh) + 0.5 * pre * (1.0 - tanh * tanh) * (
+            GELU_SCALE * (1.0 + 3.0 * 0.044715 * pre * pre)
+        )
+        grad_pre = (dot_t(gc[...], down_v[at, :]) * slope).astype(BF16)
+        gpre[:, at] = grad_pre
+        acc_u[...] += dot_t(grad_pre, up_v[:, at])
+
+    for quarter in range(4):
+        at = slice(quarter * model, (quarter + 1) * model)
+        early[5 + quarter : 6 + quarter, :] = col_sum(gpre[:, at].astype(F32))
+    branch_m = acc_m[...] + b_down[...].astype(F32)
+    output[...] = (x_two + row(5) * branch_m).astype(BF16)
+    early[3:4, :] = col_sum(grad_out * branch_m)
+    up_three = acc_u[...]
+    early[1:2, :] = col_sum(up_three)
+    early[2:3, :] = col_sum(up_three * normed_2)
+    grad_x2 = grad_out + norm_back(normed_2, inverse_2, up_three * (1.0 + row(4)))
+    acc_m[...] = grad_x2
+    gc[...] = grad_x2.astype(BF16)
+    ga[...] = dot_t(gc[...], co_v[...]).astype(BF16)
+
+    @pl.loop(0, HEADS // 2)
+    def _(p):
+        at = lanes(p)
+        value_at = lanes(p + HEADS // 2)
+        key_pair, value_pair = gkvc[:, at], gkvc[:, value_at]
+        query_pair, up_pair = gqc[:, at], ga[:, at]
+        d_q, d_k, d_v = [], [], []
+        for half in range(2):
+            probs = prob_c[2 * p + half]
+            grad_probs = dot_t(pick_half(up_pair, half), value_pair)
+            inner = jnp.sum(probs * grad_probs, axis=-1, keepdims=True)
+            grad_scores = (probs * (grad_probs - inner)).astype(BF16)
+            d_q.append(dot(grad_scores, key_pair))
+            d_k.append(t_dot(grad_scores, query_pair))
+            d_v.append(t_dot(probs.astype(BF16), up_pair))
+        gqc[:, at] = (join_halves(*d_q) * HEAD ** (-0.5)).astype(BF16)
+        gkvc[:, at] = (join_halves(*d_k) * HEAD ** (-0.5)).astype(BF16)
+        gkvc[:, value_at] = join_halves(*d_v).astype(BF16)
+
+    text_part[...] = dot_t(gkvc[...], ckv_v[...]).astype(BF16)
+    up_two = dot_t(gqc[...], cq_v[...])
+    early[4:5, :] = col_sum(up_two * normed_1)
+    grad_x1 = acc_m[...] + norm_back(normed_1, inverse_1, up_two * gain)
+    early[0:1, :] = col_sum(grad_x1 * gx1[...])
+    early[11:16, :] = jnp.zeros((5, model), F32)
+    gx1[...] = grad_x1
+    ga[...] = (row(2) * grad_x1).astype(BF16)
+    gattn[...] = dot_t(ga[...], out_v[...]).astype(BF16)
+    for copy in (to_x, to_y, fwd_x, fwd_y):
+        copy.wait_send()
+
+
+def frames_f32(block):
+    return block.astype(F32)
+
+
+GELU_SCALE = 0.7978845608028654
+
+
+def backward_kernel(
+    act, gm_t, h3, gpre, h2, cross, gqc, gc, gkvc, attn, ga, gattn, gx1, query,
+    kv, h_all, lse, mods, text_part, early, text, mask, frames, w_qkv, text_pick,
+    out, d_frames, d_text, e_all, l_all,
+    G, R0, R1, R2, R3, R4, dqkv, up_low, T, late,
+    s0, r0, s1, r1, s2, r2, s3, r3, s4, r4, se, re, sl, rl, st, rt, free,
+):
+    seq = lax.axis_index("seq")
+    rows = lax.axis_index("rows")
+    y, x = seq // 2, seq % 2
+    z, c = rows // 2, rows % 2
+    core_peer = {"rows": z * 2 + (1 - c)}
+    x_id, y_id, d_id = y * 2 + 1 - x, (1 - y) * 2 + x, (1 - y) * 2 + 1 - x
+    x_peer, y_peer, d_peer = {"seq": x_id}, {"seq": y_id}, {"seq": d_id}
+    z_peers = [{"rows": lax.rem(z + d, 4) * 2 + c} for d in (1, 2, 3)]
+    enter([core_peer, x_peer, y_peer, d_peer] + z_peers)
+
+    tall, width = G.shape[-2:]
+    here, model = frames.shape
+
+    def gather_copies(table, send, recv):
+        mine = table.at[c, z, y, x]
+        pair = table.at[c, z, y]
+        plane = table.at[c, z]
+        return (
+            [remote(mine, mine, send.at[0], recv.at[0], x_peer)],
+            [remote(pair, pair, send.at[1], recv.at[1], y_peer)],
+            [
+                remote(plane, plane, send.at[1 + d], recv.at[1 + d], z_peers[d - 1])
+                for d in (1, 2, 3)
+            ],
+            [remote(table.at[c], table.at[c], send.at[5], recv.at[5], core_peer)],
+        )
+
+    early_steps = gather_copies(e_all, se, re)
+    late_steps = gather_copies(l_all, sl, rl)
+    text_steps = (
+        [remote(T.at[y, x], T.at[y, x], st.at[0], rt.at[0], x_peer)],
+        [remote(T.at[y], T.at[y], st.at[1], rt.at[1], y_peer)],
+    )
+
+    def advance(steps, at):
+        if at:
+            for copy in steps[at - 1]:
+                copy.wait_recv()
+        if at < len(steps):
+            for copy in steps[at]:
+                copy.start()
+
+    def put(k, s, block):
+        low = block.astype(BF16)
+        for zz in range(4):
+            for cc in range(2):
+                at = (zz * 2 + cc) * tall
+                G[k, cc, zz, s // 2, s % 2] = low[at : at + tall]
+
+    def put_lanes(k, s, lane, block):
+        low = block.astype(BF16)
+        for zz in range(4):
+            for cc in range(2):
+                at = (zz * 2 + cc) * tall
+                G[k, cc, zz, s // 2, s % 2, :, lane : lane + 128] = low[at : at + tall]
+
+    def shared(s, first_left, first, second_left, second):
+        parity = s % 2
+        half_of = (~low_half(first.shape)).astype(jnp.int32)
+        first = jnp.where(half_of == parity, first, jnp.zeros_like(first))
+        turned = pltpu.roll(second.astype(F32), HEAD, 1)
+        half_of = (~low_half(turned.shape)).astype(jnp.int32)
+        turned = jnp.where(half_of == parity, 0.0, turned).astype(BF16)
+        return t_dot(first_left, first) + t_dot(second_left, turned)
+
+    def compute(k):
+        @pl.loop(0, 4)
+        def _(s):
+            full = s + (s + 1) // 2
+            split = 1 + 3 * (s // 2)
+            wide = 4 * s + (s + 1) // 2
+            if k < 2:
+                left = gm_t[pl.ds(pl.multiple_of(s * 2 * tall + k * tall, 16), tall), :]
+                for r in range(8):
+                    G[k, r % 2, r // 2, s // 2, s % 2] = dot(
+                        left, act[:, r * width : (r + 1) * width]
+                    ).astype(BF16)
+            elif k < 4:
+                put(k, s, t_dot(h3[...], gpre[:, lanes(s * 6 + (k - 2) * 3, 3)]))
+            elif k == 4:
+                put_lanes(k, s, 0, t_dot(h2[...], gqc[:, lanes(full)]))
+                put_lanes(k, s, 128, t_dot(cross[...], gc[:, lanes(full)]))
+                put_lanes(
+                    k, s, 256,
+                    shared(s, h2[...], gqc[:, lanes(split)], cross[...], gc[:, lanes(split)]),
+                )
+            elif k == 5:
+                put(k, s, t_dot(text[...], gkvc[:, lanes(s * 3, 3)]))
+            elif k == 6:
+                put(k, s, t_dot(h_all[...], dqkv[:, lanes(wide, 3)]))
+            else:
+                put_lanes(k, s, 0, t_dot(h_all[...], dqkv[:, lanes(wide + 3)]))
+                put_lanes(
+                    k, s, 128,
+                    shared(
+                        s, h_all[...], dqkv[:, lanes(4 + 9 * (s // 2))],
+                        attn[...], ga[:, lanes(split)],
+                    ),
+                )
+                put_lanes(k, s, 256, t_dot(attn[...], ga[:, lanes(full)]))
+
+    def core_copy(k):
+        slot = k % 2
+        return remote(G.at[k, 1 - c], R0.at[slot], s0.at[k], r0.at[k], core_peer)
+
+    def first_copies(k):
+        return (
+            remote(G.at[k, c, 0:2, :, 1 - x], R1.at[k, 0], s1.at[k, 0], r1.at[k, 0], x_peer),
+            remote(G.at[k, c, 2:4, 1 - y], R1.at[k, 1], s1.at[k, 1], r1.at[k, 1], y_peer),
+        )
+
+    def second_copies(k):
+        return (
+            remote(G.at[k, c, 0:2, 1 - y, x], R2.at[k, 0], s2.at[k, 0], r2.at[k, 0], y_peer),
+            remote(G.at[k, c, 2:4, y, 1 - x], R2.at[k, 1], s2.at[k, 1], r2.at[k, 1], x_peer),
+        )
+
+    def z_copies(k):
+        return [
+            remote(
+                G.at[k, c, lax.rem(z + d, 4), y, x], R3.at[k, d - 1],
+                s3.at[k, d - 1], r3.at[k, d - 1], z_peers[d - 1],
+            )
+            for d in (1, 2, 3)
+        ]
+
+    def add(one, two):
+        return (one.astype(F32) + two.astype(F32)).astype(BF16)
+
+    def phase0(k):
+        compute(k)
+        if k >= 2:
+            pl.semaphore_wait(free, 1)
+        core_copy(k).start()
+
+    def phase1(k):
+        core_copy(k).wait_recv()
+
+        @pl.loop(0, 4)
+        def _(zz):
+            for yy in range(2):
+                for xx in range(2):
+                    G[k, c, zz, yy, xx] = add(G[k, c, zz, yy, xx], R0[k % 2, zz, yy, xx])
+
+        if k < CHUNKS - 2:
+            pl.semaphore_signal(free, inc=1, device_id=core_peer, device_id_type=MESH)
+        for copy in first_copies(k):
+            copy.start()
+
+    def phase2(k):
+        for copy in first_copies(k):
+            copy.wait_recv()
+        for zz in range(2):
+            for other in range(2):
+                G[k, c, zz, other, x] = add(G[k, c, zz, other, x], R1[k, 0, zz, other])
+                G[k, c, 2 + zz, y, other] = add(G[k, c, 2 + zz, y, other], R1[k, 1, zz, other])
+        for copy in second_copies(k):
+            copy.start()
+
+    def phase3(k):
+        for copy in second_copies(k):
+            copy.wait_recv()
+        for zz in range(2):
+            G[k, c, zz, y, x] = add(G[k, c, zz, y, x], R2[k, 0, zz])
+            G[k, c, 2 + zz, y, x] = add(G[k, c, 2 + zz, y, x], R2[k, 1, zz])
+        for copy in z_copies(k):
+            copy.start()
+
+    def phase4(k):
+        for copy in z_copies(k):
+            copy.wait_recv()
+        total = G[k, c, z, y, x].astype(F32)
+        for d in range(3):
+            total = total + R3[k, d].astype(F32)
+        out[k] = total
+
+    e_all[c, z, y, x] = early[...]
+    T[y, x] = text_part[...]
+    phase0(0)
+    advance(early_steps, 0)
+    advance(text_steps, 0)
+    phase0(1)
+    phase1(0)
+    phase0(2)
+    phase1(1)
+    phase0(3)
+    phase1(2)
+    phase0(4)
+    phase1(3)
+    phase0(5)
+    phase1(4)
+    phase1(5)
+    advance(early_steps, 1)
+    advance(text_steps, 1)
+
+    own = pl.ds(pl.multiple_of(seq * here, here), here)
+    dqkv[:, :model] = jnp.zeros((dqkv.shape[0], model), BF16)
+    lane_of = lax.broadcasted_iota(jnp.int32, lse.shape, 1)
+
+    @pl.loop(0, HEADS // 2)
+    def _(p):
+        at = lanes(p)
+        key_at = lanes(p + HEADS // 2)
+        value_at = lanes(p + HEADS)
+        key_pair, value_pair = kv[:, at], kv[:, key_at]
+        query_pair, up_pair = query[:, at], gattn[:, at]
+        scaled = query_pair * jnp.asarray(HEAD ** (-0.5), BF16)
+        d_q, d_k, d_v = [], [], []
+        for half in range(2):
+            scores = dot_t(pick_half(scaled, half), key_pair)
+            log_total = jnp.sum(
+                jnp.where(lane_of == 2 * p + half, lse[...], 0.0), axis=-1, keepdims=True
+            )
+            scores = jnp.where(mask[...] > 0.5, scores, NEG_FILL)
+            probs = jnp.exp(scores - log_total)
+            grad_probs = dot_t(pick_half(up_pair, half), value_pair)
+            inner = jnp.sum(probs * grad_probs, axis=-1, keepdims=True)
+            grad_scores = (probs * (grad_probs - inner)).astype(BF16)
+            d_q.append(dot(grad_scores, key_pair))
+            d_k.append(t_dot(grad_scores, query_pair))
+            d_v.append(t_dot(probs.astype(BF16), up_pair))
+        dqkv[own, at] = (join_halves(*d_q) * HEAD ** (-0.5)).astype(BF16)
+        dqkv[:, key_at] = (join_halves(*d_k) * HEAD ** (-0.5)).astype(BF16)
+        dqkv[:, value_at] = join_halves(*d_v).astype(BF16)
+        phase2(p)
+
+    def up_block(block):
+        rows_at = pl.ds(pl.multiple_of(block * here, here), here)
+        return dot_t(dqkv[rows_at, model:], w_qkv[:, model:])
+
+    up_copies = []
+    for i, (block, peer) in enumerate(((d_id, d_peer), (x_id, x_peer), (y_id, y_peer))):
+        up_low[i] = up_block(block).astype(BF16)
+        copy = remote(up_low.at[i], R4.at[i], s4.at[i], r4.at[i], peer)
+        copy.start()
+        up_copies.append(copy)
+    phase0(6)
+    phase0(7)
+    phase1(6)
+    phase1(7)
+    advance(early_steps, 2)
+    advance(text_steps, 2)
+
+    @pl.loop(0, 6)
+    def _(k):
+        phase3(k)
+
+    for copy in up_copies:
+        copy.wait_recv()
+    up_one = dot_t(dqkv[own, :], w_qkv[...])
+    for i in range(3):
+        up_one = up_one + R4[i].astype(F32)
+    normed, inverse = norm_parts(frames[...].astype(F32))
+    late[0:1, :] = col_sum(up_one)
+    late[1:2, :] = col_sum(up_one * normed)
+    late[2:8, :] = jnp.zeros((6, model), F32)
+    d_frames[...] = gx1[...] + norm_back(normed, inverse, up_one * (1.0 + mods[1:2, :]))
+    l_all[c, z, y, x] = late[...]
+    advance(late_steps, 0)
+    total = jnp.zeros(d_text.shape, F32)
+    for i in range(4):
+        total = total + T[i // 2, i % 2].astype(F32) * text_pick[i]
+    d_text[...] = total
+    phase2(6)
+    advance(late_steps, 1)
+    phase2(7)
+    advance(early_steps, 3)
+
+    @pl.loop(0, 6)
+    def _(k):
+        phase4(k)
+
+    advance(late_steps, 2)
+    phase3(6)
+    phase3(7)
+    advance(late_steps, 3)
+    phase4(6)
+    phase4(7)
+    advance(early_steps, 4)
+    advance(late_steps, 4)
+
+    @pl.loop(0, CHUNKS)
+    def _(k):
+        core_copy(k).wait_send()
+        for copy in (*first_copies(k), *second_copies(k), *z_copies(k)):
+            copy.wait_send()
+
+    for copy in up_copies:
+        copy.wait_send()
+    for steps in (early_steps, late_steps, text_steps):
+        for step in steps:
+            for copy in step:
+                copy.wait_send()
+
+
+def in_vmem(count):
+    return [pl.BlockSpec(memory_space=pltpu.VMEM)] * count
+
+
+def in_any(count):
+    return [pl.BlockSpec(memory_space=pl.ANY)] * count
+
+
+def per_device(
+    frames, text_tokens, step_embed, segments, cotangent,
+    w_ada, b_ada, w_qkv, w_out, g_cross, w_cq, w_ckv, w_co, w_up, b_up, w_down, b_down,
+):
+    seq_count = lax.axis_size("seq")
+    rows_count = lax.axis_size("rows")
+    seq_index = lax.axis_index("seq")
+    rows_index = lax.axis_index("rows")
+    frames, text_tokens, step_embed = frames[0], text_tokens[0], step_embed[0]
+    segments, cotangent = segments[0], cotangent[0]
+    here, model = frames.shape
+    length = segments.shape[0]
+    hidden = w_up.shape[1]
+    assert (length // ITEMS) % here == 0
+    block_slots = segments[::here]
+    slot = lax.dynamic_index_in_dim(block_slots, seq_index, 0, keepdims=False)
+    mask = (segments == slot).astype(F32)[None]
+    text_rows = 128
+    text_mine = jnp.pad(
+        lax.dynamic_slice_in_dim(text_tokens, slot * TXT, TXT, axis=0),
+        ((0, text_rows - TXT), (0, 0)),
+    )
+    step_rows = 16
+    step_pad = jnp.pad(step_embed, ((0, step_rows - ITEMS), (0, 0)))
+    wanted = jnp.concatenate([block_slots, slot[None]])
+    picks = (wanted[:, None] == jnp.arange(step_rows)[None, :]).astype(F32)[:, :, None]
+    text_pick = (block_slots == seq_index).astype(F32)[:, None, None]
+
+    def like(shape, dtype=BF16):
+        return jax.ShapeDtypeStruct(shape, dtype)
+
+    square = like((here, model))
+    dma = pltpu.SemaphoreType.DMA
+    vmem = pltpu.VMEM
+    (
+        output, act, gm_t, h3, gpre, h2, cross, gqc, gc, gkvc, attn, ga, gattn, gx1, query,
+        kv, h_all, lse, mods, text_part, early,
+    ) = pl.pallas_call(
+        forward_kernel,
+        out_shape=(
+            square, like((here, hidden)), like((model, here)), square, like((here, hidden)),
+            square, square, square, square, like((text_rows, 2 * model)), square, square,
+            square, like((here, model), F32), square, like((length, 2 * model)),
+            like((length, model)), like((here, 128), F32), like((8, model), F32),
+            like((text_rows, model)), like((16, model), F32),
+        ),
+        in_specs=in_any(1) + in_vmem(5)
+        + in_any(1) + in_vmem(1) + in_any(2) + in_vmem(1) + in_any(4) + in_vmem(1)
+        + in_any(1) + in_vmem(1),
+        out_specs=tuple(in_vmem(21)),
+        scratch_shapes=[
+            vmem((seq_count, here, model), BF16),
+            vmem(w_ada.shape, BF16), vmem(w_qkv.shape, BF16), vmem(w_out.shape, BF16),
+            vmem(w_cq.shape, BF16), vmem(w_ckv.shape, BF16), vmem(w_co.shape, BF16),
+            vmem(w_up.shape, BF16), vmem(w_down.shape, BF16),
+            vmem((HEADS, here, text_rows), F32),
+            vmem((here, model), F32), vmem((here, model), F32),
+            vmem((step_rows, 6 * model), F32),
+            dma((9,)), dma((4,)), dma((4,)),
+        ],
+        compiler_params=pltpu.CompilerParams(
+            collective_id=0, has_side_effects=True, vmem_limit_bytes=VMEM_MOST
+        ),
+        name="forward_layer",
+    )(
+        frames, cotangent, text_mine, step_pad, picks, mask,
+        w_ada, b_ada[None], w_qkv, w_out, g_cross[None], w_cq, w_ckv, w_co, w_up,
+        b_up[None], w_down, b_down[None],
+    )
+
+    tall, width = model // rows_count, model // 2
+    table = (2, 4, 2, 2)
+    done, d_frames, d_text, e_all, l_all = pl.pallas_call(
+        backward_kernel,
+        out_shape=(
+            like((CHUNKS, tall, width), F32), like((here, model), F32),
+            like((text_rows, model), F32), like(table + (16, model), F32),
+            like(table + (8, model), F32),
+        ),
+        in_specs=in_vmem(25),
+        out_specs=tuple(in_vmem(5)),
+        scratch_shapes=[
+            vmem((CHUNKS,) + table + (tall, width), BF16),
+            vmem((2, 4, 2, 2, tall, width), BF16),
+            vmem((CHUNKS, 2, 2, 2, tall, width), BF16),
+            vmem((CHUNKS, 2, 2, tall, width), BF16),
+            vmem((CHUNKS, 3, tall, width), BF16),
+            vmem((3, here, model), BF16),
+            vmem((length, 3 * model), BF16),
+            vmem((3, here, model), BF16),
+            vmem((2, 2, text_rows, model), BF16),
+            vmem((8, model), F32),
+            dma((CHUNKS,)), dma((CHUNKS,)),
+            dma((CHUNKS, 2)), dma((CHUNKS, 2)),
+            dma((CHUNKS, 2)), dma((CHUNKS, 2)),
+            dma((CHUNKS, 3)), dma((CHUNKS, 3)),
+            dma((3,)), dma((3,)), dma((6,)), dma((6,)), dma((6,)), dma((6,)),
+            dma((2,)), dma((2,)), pltpu.SemaphoreType.REGULAR,
+        ],
+        compiler_params=pltpu.CompilerParams(
+            collective_id=1, has_side_effects=True, vmem_limit_bytes=VMEM_MOST
+        ),
+        name="backward_layer",
+    )(
+        act, gm_t, h3, gpre, h2, cross, gqc, gc, gkvc, attn, ga, gattn, gx1, query,
+        kv, h_all, lse, mods, text_part, early, text_mine, mask, frames, w_qkv, text_pick,
+    )
+
+    def by_device(entries):
+        return entries.transpose(1, 0, 2, 3, 4, 5).reshape(
+            (rows_count * seq_count,) + entries.shape[4:]
+        )
+
+    e_all, l_all = by_device(e_all), by_device(l_all)
+    item_all = jnp.concatenate([l_all[:, :2], e_all[:, :4]], axis=1).reshape(
+        rows_count * seq_count, 6 * model
+    )
+    ada_all = e_all[:, 10]
+
+    def share(vector, count, index):
+        size = vector.shape[-1] // count
+        return lax.dynamic_slice_in_dim(vector, index * size, size, axis=-1)
+
+    d_b_ada = share(jnp.sum(item_all, axis=0), rows_count, rows_index)
+    d_g_cross = share(jnp.sum(e_all[:, 4], axis=0), rows_count, rows_index)
+    d_b_up = share(jnp.sum(e_all[:, 5:9], axis=0).reshape(-1), rows_count, rows_index)
+    d_b_down = share(jnp.sum(e_all[:, 9], axis=0), rows_count, rows_index)
+    d_w_ada = lax.dot_general(
+        share(ada_all, rows_count, rows_index),
+        share(item_all, seq_count, seq_index),
+        (((0,), (0,)), ((), ())),
+        precision=PRECISE,
+        preferred_element_type=F32,
+    )
+    row_items = lax.dynamic_slice_in_dim(item_all, rows_index * seq_count, seq_count, axis=0)
+    item_mine = jnp.sum(row_items * text_pick[:, 0], axis=0, keepdims=True)
+    item_high = item_mine.astype(BF16)
+    item_low = (item_mine - item_high.astype(F32)).astype(BF16)
+    d_ada = jnp.sum(
+        dot_t(jnp.concatenate([item_high, item_low], axis=0), w_ada), axis=0, keepdims=True
+    )
+    my_step = lax.dynamic_slice_in_dim(step_embed, seq_index, 1, axis=0).astype(F32)
+    unused_step, silu_back = jax.vjp(jax.nn.silu, my_step)
+    d_step = silu_back(d_ada)[0]
+
+    odd = seq_index % 2 == 1
+
+    def place(full, mixed, first):
+        even = mixed[:, :HEAD] if first else mixed[:, HEAD:]
+        other = mixed[:, HEAD:] if first else mixed[:, :HEAD]
+        return jnp.where(
+            odd,
+            jnp.concatenate([other, full], axis=1),
+            jnp.concatenate([full, even], axis=1),
+        )
+
+    d_w_down = jnp.concatenate([done[0], done[1]], axis=0).T
+    d_w_up = jnp.concatenate([done[2], done[3]], axis=1)
+    d_w_cq = place(done[4][:, :128], done[4][:, 256:], True)
+    d_w_co = place(done[4][:, 128:256], done[4][:, 256:], False)
+    d_w_ckv = done[5]
+    d_w_qkv = place(
+        jnp.concatenate([done[6], done[7][:, :128]], axis=1), done[7][:, 128:256], True
+    )
+    d_w_out = place(done[7][:, 256:], done[7][:, 128:256], False)
+    return (
+        output[None], d_frames[None], d_text[None, :TXT], d_step[None],
         d_w_ada, d_b_ada, d_w_qkv, d_w_out, d_g_cross, d_w_cq, d_w_ckv, d_w_co,
         d_w_up, d_b_up, d_w_down, d_b_down,
     )
@@ -478,6 +1002,7 @@
         P("rows", "seq"), P("rows", "seq"), P("rows", "seq"), P("rows", "seq"), P("rows"),
         P("rows", "seq"), P("rows"),
     )
+    fused = mesh.shape["rows"] == 8 and mesh.shape["seq"] == 4
     return jax.shard_map(
-        per_device, mesh=mesh, in_specs=in_specs, out_specs=out_specs, check_vma=False
-    )
+        per_device if fused else per_device_plain, mesh=mesh, in_specs=in_specs, out_specs=out_specs, check_vma=False
+    )

time: 363 us -> 247 us (0.68); the launches traced: 358 us -> 246 us
  Pallas kernels: 109 us -> 210 us
  matrix products: 81.3 us -> 6.36 us
  local copies, waits for them, and re-layouts: 66.4 us -> 19.2 us
  other arithmetic: 38.7 us -> 9.19 us
  blocking collectives: 24.8 us -> 0 us
  between operations: 18.8 us -> 1.5 us
  waiting for transfers between devices: 16.6 us -> 0 us
    pallas_call x1 -> x2, Pallas kernels: 109 us -> 210 us  [the longest x1 151 us: per_device(): pl.pallas_call(backward_kernel, out_shape=(like((CHUNKS, tall, width), F3...]
    dot_general x24 -> x0, matrix products: 61.8 us -> none  [the longest x9 18 us: dot(): return jnp.dot(left, right, preferred_element_type=F32)]
    unnamed x1 -> x0, blocking collectives: 24.8 us -> none
    all_gather x2 -> x0, waiting for transfers between devices: 15.9 us -> none  [the longest x1 15.9 us: per_device(): frames_all = lax.all_gather(frames, 'seq', axis=0, tiled=True)]
    slice x13 -> x4, local copies, waits for them, and re-layouts: 15 us -> 0.16 us  [the longest x1 0.09 us: place(): even = mixed[:, :HEAD] if first else mixed[:, HEAD:]]
    dot_general x8 -> x1, matrix products: 18.1 us -> 5.04 us  [dot_t(): lax.dot_general(left, right, (((1,), (1,)), ((), ())), preferred_element_...]
    unnamed x189 -> x18, local copies, waits for them, and re-layouts: 15.9 us -> 2.96 us
    concatenate x7 -> x1, other arithmetic: 13.6 us -> 0.72 us  [per_device(): wanted = jnp.concatenate([block_slots, slot[None]])]
  transfers between devices with their start and end apart: 4 -> 0, of which waited for: 1 -> 0; matrix products, arithmetic and copies ran while one was open for 29% -> 0% of each run, Pallas kernels for 30% -> 0%
where the time goes in v2:
time: 247 us; the launch traced here: 246 us
  Pallas kernels  210 us (85%)
  local copies, waits for them, and re-layouts  19.2 us (8%)
  other arithmetic  9.19 us (4%)
  matrix products  6.36 us (3%)
    pallas_call x1, Pallas kernels, per_device(): pl.pallas_call(backward_kernel, out_shape=(like((CHUNKS, tall, width), F3...  151 us
    pallas_call x1, Pallas kernels, per_device(): pl.pallas_call(forward_kernel, out_shape=(square, like((here, hidden)), l...  59 us
    dot_general x1, matrix products, dot_t(): lax.dot_general(left, right, (((1,), (1,)), ((), ())), preferred_element_...  5.04 us

profile of v2, /device:TPU:0, one launch (start us, length us, event | category | flops | bytes accessed | tf_op | source)
XLA Modules:
  0.0 246.5 jit_solution(421105203526810859)
XLA Ops:
  0.6 0.8 slice.93
  1.4 0.0 copy-start.5
  1.4 0.6 dynamic_slice.35
  2.7 0.9 dynamic-slice_bitcast_fusion
  3.6 0.7 pad.8.text
  4.3 1.3 pad.9.step
  5.6 0.7 pad_add_fusion
  6.3 0.7 fusion.2.picks
  7.0 0.0 copy-done.5
  7.0 1.9 compare_convert_fusion.mask
  9.0 1.3 broadcast_in_dim.32.b_ada
  10.3 1.3 broadcast_in_dim.33.g_cross
  11.5 1.3 broadcast_in_dim.34.b_up
  12.8 1.3 broadcast_in_dim.35.b_down
  14.1 59.0 %forward_layer.1 = (bf16[256,768]{1,0:T(8,128)(2,1)}, bf16[256,3072]{1,0:T(8,128)(2,1)}, bf16[768,256]{1,0:T(8,128)(2,1)}, bf16[256,768]{1,0:T(8,128)(2,1)}, bf1...) custom-call(bf16[256,768]{1,0:T(8,128)(2,1)} %bitcast.44, ...), custom_call_target="tpu_custom_call" | custom-call | tf_op jit(solution)/shard_map/forward_layer/pallas_call | solution.py:860
  73.1 0.7 fusion.17
  73.7 0.7 copy.35.text_pick
  74.4 151.3 %backward_layer.1 = (f32[8,96,384]{2,1,0:T(8,128)}, f32[256,768]{1,0:T(8,128)}, f32[128,768]{1,0:T(8,128)}, f32[2,4,2,2,16,768]{5,4,3,2,1,0:T(8,128)}, f32[2,4,2,2,8,768]{5,4,3,2,1,0:T(8,128)}) custom-call(bf16[256,3072]{1,0:T(8,128)(2,1)} %get-tuple-element.43.act, bf16[768,256]{1,0:T(8,128)(2,1)} %get-tuple-element.44.gm_t, ...), custom_call_target="tpu_custom_call" | custom-call | tf_op jit(solution)/shard_map/backward_layer/pallas_call | solution.py:895
  225.7 1.0 slice_bitcast_fusion
  226.6 0.9 copy.38
  227.6 0.0 copy-start.2
  227.6 1.6 copy.37
  229.2 0.1 slice_reduce_fusion
  229.3 0.0 copy-done.2
  229.3 0.1 copy.36
  229.4 0.0 copy-start.6
  229.4 0.1 slice.118
  229.4 0.2 fusion.10
  229.7 0.2 copy.39
  229.8 0.2 copy-done.6
  230.0 0.1 multiply_reduce_fusion
  230.2 0.0 copy-start.4
  230.2 0.0 copy-start
  230.2 5.0 %convolution_reduce_fusion = f32[768]{0:T(1024)S(1)} fusion(bf16[768,4608]{1,0:T(8,128)(2,1)} %w_ada.1, bf16[1,4608]{1,0:T(2,128)(2,1)S(1)} %subtract_convert_fusion, bf16[1,4608]{1,0:T(2,128)(2,1)S(1)} %reduce_sum.80), kind=kOutput, calls=%fused_computation | convolution fusion | flops 14193408 | bytes 7099392 | tf_op jit(solution)/shard_map/dot_general | solution.py:30
  235.3 0.0 copy-done.4
  235.3 0.6 fusion.7
  235.9 0.3 slice_reduce_fusion.1
  236.2 0.1 constant_dynamic-slice_fusion
  236.3 1.3 fusion
  237.6 0.7 dynamic_slice.43
  238.3 0.0 copy-done
  238.3 0.7 slice_bitcast_fusion.2
  239.0 0.0 copy-start.3
  239.0 0.1 fusion.12
  239.2 0.0 copy-start.1
  239.2 0.8 maximum_select_fusion
  240.0 0.7 maximum_select_fusion.1
  240.7 0.6 dynamic_slice.44
  241.3 0.8 maximum_select_fusion.3
  242.1 0.7 pad_maximum_fusion.1
  242.9 0.7 dynamic_slice.45
  243.5 0.7 maximum_bitcast_fusion
  244.3 0.6 dynamic_slice.46
  244.8 0.0 copy-done.3
  244.8 0.7 copy.42
  245.6 0.0 copy-done.1
  245.6 0.9 copy.43
  (7 shorter events, 0.1 us)
Async XLA Ops:
  1.4 5.6 %copy-start.5 = (s32[4]{0:T(128)}, s32[4]{0:T(128)S(1)}, u32[]{:S(2)}) copy-start(s32[4]{0:T(128)S(1)} %slice.93) | copy-start | bytes 52
  227.6 1.8 copy-start.2
  229.4 0.7 copy-start.6
  230.2 5.1 %copy-start.4 = (bf16[1,4,768]{2,1,0:T(4,128)(2,1)S(1)}, bf16[1,4,768]{2,1,0:T(4,128)(2,1)}, u32[]{:S(2)}) copy-start(bf16[1,4,768]{2,1,0:T(4,128)(2,1)} %param.19) | copy-start | bytes 18436
  230.2 8.1 %copy-start = (f32[8,96,384]{2,1,0:T(8,128)S(1)}, f32[8,96,384]{2,1,0:T(8,128)}, u32[]{:S(2)}) copy-start(f32[8,96,384]{2,1,0:T(8,128)} %get-tuple-element.67) | copy-start | bytes 3538948
  239.0 5.8 %copy-start.3 = (bf16[256,768]{1,0:T(8,128)(2,1)S(1)}, bf16[256,768]{1,0:T(8,128)(2,1)}, u32[]{:S(2)}) copy-start(bf16[256,768]{1,0:T(8,128)(2,1)} %get-tuple-element.42) | copy-start | bytes 1179652
  239.2 6.4 %copy-start.1 = (f32[256,768]{1,0:T(8,128)S(1)}, f32[256,768]{1,0:T(8,128)}, u32[]{:S(2)}) copy-start(f32[256,768]{1,0:T(8,128)} %get-tuple-element.63) | copy-start | bytes 2359300

commit v3 on v2

--- a/solution.py
+++ b/solution.py
@@ -302,20 +302,22 @@
 
 
 def forward_kernel(
-    frames, cot, text, step, picks, mask,
+    frames, cot, text, step, seg_s, seg,
     w_ada, b_ada, w_qkv, w_out, g_cross, w_cq, w_ckv, w_co, w_up, b_up, w_down, b_down,
     output, act, gm_t, h3, gpre, h2, cross, gqc, gc, gkvc, attn, ga, gattn, gx1, query,
-    kv, h_all, lse, mods, text_part, early,
+    kv, h_all, lse, mods, text_part, early, text_mine,
     fr, ada_v, qkv_v, out_v, cq_v, ckv_v, co_v, up_v, down_v, prob_c, acc_m, acc_u,
-    item, local, send, recv,
+    item, up_bias, local, send, recv,
 ):
     seq = lax.axis_index("seq")
     y, x = seq // 2, seq % 2
     x_id, y_id, d_id = y * 2 + 1 - x, (1 - y) * 2 + x, (1 - y) * 2 + 1 - x
     x_peer, y_peer = {"seq": x_id}, {"seq": y_id}
-    model = frames.shape[1]
-    here = frames.shape[0]
+    frames = frames.at[0]
+    here, model = frames.shape
     part = here // 2
+    slot = seg_s[0, seq * here]
+    mask = seg[...] == slot
     loads = [
         pltpu.make_async_copy(src, dst, local.at[i])
         for i, (src, dst) in enumerate(
@@ -336,18 +338,23 @@
     def row(at):
         return mods[at : at + 1, :]
 
-    step_f32 = step[...].astype(F32)
+    step_f32 = jnp.concatenate(
+        [step[0].astype(F32), jnp.zeros((item.shape[0] - ITEMS, model), F32)], axis=0
+    )
     ada = (step_f32 / (1.0 + jnp.exp(-step_f32))).astype(BF16)
     loads[1].wait()
-    item[...] = dot(ada, ada_v[...]) + b_ada[...].astype(F32)
+    item[...] = dot(ada, ada_v[...]) + b_ada[...].astype(F32)[None]
+    slot_row = lax.broadcasted_iota(jnp.int32, (item.shape[0], model), 0)
+    chosen_mine = (slot_row == slot).astype(F32)
     for part_at in range(6):
         mods[part_at : part_at + 1, :] = col_sum(
-            item[:, part_at * model : (part_at + 1) * model] * picks[4]
+            item[:, part_at * model : (part_at + 1) * model] * chosen_mine
         )
-    early[10:11, :] = col_sum(ada.astype(F32) * picks[4])
+    early[10:11, :] = col_sum(ada.astype(F32) * chosen_mine)
+    up_bias[...] = b_up[...].astype(F32)[None]
 
     def take(block):
-        chosen = picks[block]
+        chosen = (slot_row == seg_s[0, block * here]).astype(F32)
         shift = col_sum(item[:, :model] * chosen)
         scale = col_sum(item[:, model : 2 * model] * chosen)
         normed, unused = norm_parts(fr[block].astype(F32))
@@ -375,7 +382,12 @@
     take(x_id)
     take(y_id)
     loads[4].wait()
-    text_kv = dot(text[...], ckv_v[...]).astype(BF16)
+    picked = (text_mine.shape[0], text.shape[1])
+    text_at = lax.broadcasted_iota(jnp.int32, picked, 0)
+    token = lax.broadcasted_iota(jnp.int32, picked, 1)
+    hot = jnp.where((token == text_at + TXT * slot) & (text_at < TXT), 1.0, 0.0).astype(BF16)
+    text_mine[...] = dot(hot, text[0]).astype(BF16)
+    text_kv = dot(text_mine[...], ckv_v[...]).astype(BF16)
     gkvc[...] = text_kv
     fwd_y.wait_recv()
     fwd_x.wait_recv()
@@ -392,7 +404,7 @@
         outs = []
         for half in range(2):
             scores = dot_t(pick_half(pair, half), kv[:, at])
-            scores = jnp.where(mask[...] > 0.5, scores, NEG_FILL)
+            scores = jnp.where(mask, scores, NEG_FILL)
             probs, log_total = softmax_rows(scores)
             lse[...] = jnp.where(lane_of == 2 * p + half, log_total, lse[...])
             outs.append(dot(probs.astype(BF16), kv[:, value_at]))
@@ -402,14 +414,14 @@
     branch_a = dot(attn[...], out_v[...])
     x_one = frames_f32(fr[seq]) + row(2) * branch_a
     gx1[...] = branch_a
-    gain = g_cross[...].astype(F32)
+    gain = g_cross[...].astype(F32)[None]
     normed_1, inverse_1 = norm_parts(x_one)
     h2[...] = (normed_1 * gain).astype(BF16)
     loads[5].wait()
     query_c = dot(h2[...], cq_v[...]).astype(BF16)
     gqc[...] = query_c
 
-    text_rows = text.shape[0]
+    text_rows = text_mine.shape[0]
     key_lane = lax.broadcasted_iota(jnp.int32, (here, text_rows), 1)
 
     @pl.loop(0, HEADS // 2)
@@ -429,7 +441,7 @@
     x_two = x_one + dot(cross[...], co_v[...])
     normed_2, inverse_2 = norm_parts(x_two)
     h3[...] = (normed_2 * (1.0 + row(4)) + row(3)).astype(BF16)
-    grad_out = cot[...].astype(F32)
+    grad_out = cot[0].astype(F32)
     grad_m = row(5) * grad_out
     gm_low = grad_m.astype(BF16)
     gm_t[...] = gm_low.astype(F32).T.astype(BF16)
@@ -444,7 +456,7 @@
     @pl.loop(0, w_up.shape[1] // slab)
     def _(j):
         at = pl.ds(pl.multiple_of(j * slab, slab), slab)
-        pre = dot(h3[...], up_v[:, at]) + b_up[:, at].astype(F32)
+        pre = dot(h3[...], up_v[:, at]) + up_bias[:, at]
         inner = GELU_SCALE * (pre + 0.044715 * pre * pre * pre)
         tanh = jnp.tanh(inner)
         act_low = (0.5 * pre * (1.0 + tanh)).astype(BF16)
@@ -460,7 +472,7 @@
     for quarter in range(4):
         at = slice(quarter * model, (quarter + 1) * model)
         early[5 + quarter : 6 + quarter, :] = col_sum(gpre[:, at].astype(F32))
-    branch_m = acc_m[...] + b_down[...].astype(F32)
+    branch_m = acc_m[...] + b_down[...].astype(F32)[None]
     output[...] = (x_two + row(5) * branch_m).astype(BF16)
     early[3:4, :] = col_sum(grad_out * branch_m)
     up_three = acc_u[...]
@@ -511,10 +523,11 @@
 
 
 def backward_kernel(
-    act, gm_t, h3, gpre, h2, cross, gqc, gc, gkvc, attn, ga, gattn, gx1, query,
-    kv, h_all, lse, mods, text_part, early, text, mask, frames, w_qkv, text_pick,
+    act, gm_t, h3, gpre, h2, cross, gqc, gc, gkvc, attn, ga, mods, text_part, early, text,
+    seg_s, seg, gattn_h, gx1_h, query_h, kv_h, h_all_h, lse_h, frames_h, w_qkv_h,
     out, d_frames, d_text, e_all, l_all,
     G, R0, R1, R2, R3, R4, dqkv, up_low, T, late,
+    gattn, gx1, query, kv, h_all, lse, frames, w_qkv, local,
     s0, r0, s1, r1, s2, r2, s3, r3, s4, r4, se, re, sl, rl, st, rt, free,
 ):
     seq = lax.axis_index("seq")
@@ -525,10 +538,22 @@
     x_id, y_id, d_id = y * 2 + 1 - x, (1 - y) * 2 + x, (1 - y) * 2 + 1 - x
     x_peer, y_peer, d_peer = {"seq": x_id}, {"seq": y_id}, {"seq": d_id}
     z_peers = [{"rows": lax.rem(z + d, 4) * 2 + c} for d in (1, 2, 3)]
+    loads = [
+        pltpu.make_async_copy(src, dst, local.at[i])
+        for i, (src, dst) in enumerate(
+            [
+                (query_h, query), (kv_h, kv), (gattn_h, gattn), (lse_h, lse),
+                (w_qkv_h, w_qkv), (h_all_h, h_all), (gx1_h, gx1), (frames_h.at[0], frames),
+            ]
+        )
+    ]
+    for load in loads:
+        load.start()
     enter([core_peer, x_peer, y_peer, d_peer] + z_peers)
 
     tall, width = G.shape[-2:]
     here, model = frames.shape
+    mask = seg[...] == seg_s[0, seq * here]
 
     def gather_copies(table, send, recv):
         mine = table.at[c, z, y, x]
@@ -693,8 +718,8 @@
             total = total + R3[k, d].astype(F32)
         out[k] = total
 
-    e_all[c, z, y, x] = early[...]
-    T[y, x] = text_part[...]
+    e_all[c, z, y, x] = early[...].astype(BF16)
+    T[y, x] = text_part[: T.shape[2], :]
     phase0(0)
     advance(early_steps, 0)
     advance(text_steps, 0)
@@ -702,19 +727,22 @@
     phase1(0)
     phase0(2)
     phase1(1)
+    advance(early_steps, 1)
+    advance(text_steps, 1)
     phase0(3)
     phase1(2)
     phase0(4)
     phase1(3)
+    advance(early_steps, 2)
     phase0(5)
     phase1(4)
     phase1(5)
-    advance(early_steps, 1)
-    advance(text_steps, 1)
 
     own = pl.ds(pl.multiple_of(seq * here, here), here)
     dqkv[:, :model] = jnp.zeros((dqkv.shape[0], model), BF16)
     lane_of = lax.broadcasted_iota(jnp.int32, lse.shape, 1)
+    for load in loads:
+        load.wait()
 
     @pl.loop(0, HEADS // 2)
     def _(p):
@@ -730,7 +758,7 @@
             log_total = jnp.sum(
                 jnp.where(lane_of == 2 * p + half, lse[...], 0.0), axis=-1, keepdims=True
             )
-            scores = jnp.where(mask[...] > 0.5, scores, NEG_FILL)
+            scores = jnp.where(mask, scores, NEG_FILL)
             probs = jnp.exp(scores - log_total)
             grad_probs = dot_t(pick_half(up_pair, half), value_pair)
             inner = jnp.sum(probs * grad_probs, axis=-1, keepdims=True)
@@ -741,7 +769,6 @@
         dqkv[own, at] = (join_halves(*d_q) * HEAD ** (-0.5)).astype(BF16)
         dqkv[:, key_at] = (join_halves(*d_k) * HEAD ** (-0.5)).astype(BF16)
         dqkv[:, value_at] = join_halves(*d_v).astype(BF16)
-        phase2(p)
 
     def up_block(block):
         rows_at = pl.ds(pl.multiple_of(block * here, here), here)
@@ -754,15 +781,21 @@
         copy.start()
         up_copies.append(copy)
     phase0(6)
+    phase2(0)
     phase0(7)
+    phase2(1)
     phase1(6)
+    phase3(0)
+    phase2(2)
     phase1(7)
-    advance(early_steps, 2)
+    phase3(1)
+    advance(early_steps, 3)
     advance(text_steps, 2)
 
-    @pl.loop(0, 6)
+    @pl.loop(3, 6)
     def _(k):
-        phase3(k)
+        phase2(k)
+        phase3(k - 1)
 
     for copy in up_copies:
         copy.wait_recv()
@@ -770,31 +803,33 @@
     for i in range(3):
         up_one = up_one + R4[i].astype(F32)
     normed, inverse = norm_parts(frames[...].astype(F32))
-    late[0:1, :] = col_sum(up_one)
-    late[1:2, :] = col_sum(up_one * normed)
-    late[2:8, :] = jnp.zeros((6, model), F32)
+    for i, total in enumerate((col_sum(up_one), col_sum(up_one * normed))):
+        for j in range(model // 128):
+            at = i * (model // 128) + j
+            late[at : at + 1, :] = total[:, j * 128 : (j + 1) * 128]
+    late[2 * (model // 128) :, :] = jnp.zeros((16 - 2 * (model // 128), 128), F32)
     d_frames[...] = gx1[...] + norm_back(normed, inverse, up_one * (1.0 + mods[1:2, :]))
-    l_all[c, z, y, x] = late[...]
+    l_all[c, z, y, x] = late[...].astype(BF16)
     advance(late_steps, 0)
     total = jnp.zeros(d_text.shape, F32)
     for i in range(4):
-        total = total + T[i // 2, i % 2].astype(F32) * text_pick[i]
+        total = total + T[i // 2, i % 2].astype(F32) * jnp.where(
+            seg_s[0, i * here] == seq, 1.0, 0.0
+        )
     d_text[...] = total
     phase2(6)
+    phase3(5)
     advance(late_steps, 1)
     phase2(7)
-    advance(early_steps, 3)
-
-    @pl.loop(0, 6)
+    phase3(6)
+    advance(late_steps, 2)
+    phase3(7)
+    advance(late_steps, 3)
+
+    @pl.loop(0, CHUNKS)
     def _(k):
         phase4(k)
 
-    advance(late_steps, 2)
-    phase3(6)
-    phase3(7)
-    advance(late_steps, 3)
-    phase4(6)
-    phase4(7)
     advance(early_steps, 4)
     advance(late_steps, 4)
 
@@ -820,33 +855,115 @@
     return [pl.BlockSpec(memory_space=pl.ANY)] * count
 
 
+def finish_kernel(
+    done, d_frames_in, d_text_in, output_in, e_all, l_all, step, seg_s, w_ada,
+    output, d_frames, d_text, d_step, d_w_ada, d_b_ada, d_w_qkv, d_w_out, d_g_cross,
+    d_w_cq, d_w_ckv, d_w_co, d_w_up, d_b_up, d_w_down, d_b_down,
+    item, ada, ada_t,
+):
+    seq = lax.axis_index("seq")
+    rows = lax.axis_index("rows")
+    here, model = output_in.shape
+    parts = model // 128
+    output[0] = output_in[...]
+    d_frames[0] = d_frames_in[...]
+    d_text[0] = d_text_in[: d_text.shape[1], :]
+    bias_sum = jnp.zeros((16, model), F32)
+    for r in range(8):
+        for s in range(4):
+            entry = e_all[r % 2, r // 2, s // 2, s % 2].astype(F32)
+            tail = l_all[r % 2, r // 2, s // 2, s % 2].astype(F32)
+            bias_sum = bias_sum + entry
+            at = slice(r * 4 + s, r * 4 + s + 1)
+            ada[at, :] = entry[10:11]
+            for j in range(4):
+                item[at, (2 + j) * model : (3 + j) * model] = entry[j : j + 1]
+            for j in range(2 * parts):
+                item[at, j * 128 : (j + 1) * 128] = tail[j : j + 1]
+    item_sum = jnp.sum(item[...], axis=0, keepdims=True)
+
+    def share(pieces):
+        total = jnp.zeros_like(pieces[0])
+        for r, piece in enumerate(pieces):
+            total = total + jnp.where(rows == r, piece, jnp.zeros_like(piece))
+        return total
+
+    def cut(row, size):
+        return [row[:, at * size : (at + 1) * size] for at in range(row.shape[1] // size)]
+
+    d_b_ada[...] = share(cut(item_sum, 6 * model // 8)).reshape(6 * model // 8)
+    d_g_cross[...] = share(cut(bias_sum[4:5], model // 8)).reshape(model // 8)
+    d_b_down[...] = share(cut(bias_sum[9:10], model // 8)).reshape(model // 8)
+    d_b_up[...] = share(
+        [piece for at in range(5, 9) for piece in cut(bias_sum[at : at + 1], model // 2)]
+    ).reshape(model // 2)
+    ada_t[...] = ada[...].T
+    tall = model // 8
+    share_at = pl.ds(pl.multiple_of(seq * 9 * 128, 128), 9 * 128)
+    d_w_ada[...] = jnp.dot(
+        ada_t[pl.ds(pl.multiple_of(rows * tall, 8), tall), :],
+        item[:, share_at],
+        precision=PRECISE,
+        preferred_element_type=F32,
+    )
+    near = item[pl.ds(pl.multiple_of(rows // 2 * 8, 8), 8), :]
+    total = jnp.zeros((1, 6 * model), F32)
+    for j in range(8):
+        wanted = jnp.where(seg_s[0, j % 4 * here] == seq, 1.0, 0.0)
+        wanted = jnp.where(rows % 2 == j // 4, wanted, 0.0)
+        total = total + near[j : j + 1] * wanted
+    high = total.astype(BF16)
+    low = (total - high.astype(F32)).astype(BF16)
+    both = jnp.concatenate(
+        [high.astype(F32), low.astype(F32), jnp.zeros((6, 6 * model), F32)], axis=0
+    ).astype(BF16)
+    d_ada = jnp.sum(dot_t(both, w_ada[...]), axis=0, keepdims=True)
+    all_steps = step[0].astype(F32)
+    my_step = jnp.zeros((1, model), F32)
+    for j in range(4):
+        my_step = my_step + all_steps[j : j + 1] * jnp.where(seq == j, 1.0, 0.0)
+    gate = 1.0 / (1.0 + jnp.exp(-my_step))
+    d_step[0] = d_ada * gate * (1.0 + my_step * (1.0 - gate))
+    odd = seq % 2 == 1
+
+    def place(full, mixed, first):
+        even = mixed[:, :HEAD] if first else mixed[:, HEAD:]
+        other = mixed[:, HEAD:] if first else mixed[:, :HEAD]
+        return jnp.where(
+            odd,
+            jnp.concatenate([other, full], axis=1),
+            jnp.concatenate([full, even], axis=1),
+        )
+
+    width = model // 2
+    d_w_down[...] = jnp.concatenate([done[0], done[1]], axis=0).T
+    d_w_up[:, :width] = done[2]
+    d_w_up[:, width:] = done[3]
+    cross, last = done[4], done[7]
+    d_w_cq[...] = place(cross[:, :128], cross[:, 256:], True)
+    d_w_co[...] = place(cross[:, 128:256], cross[:, 256:], False)
+    d_w_ckv[...] = done[5]
+    d_w_qkv[...] = place(
+        jnp.concatenate([done[6], last[:, :128]], axis=1), last[:, 128:256], True
+    )
+    d_w_out[...] = place(last[:, 256:], last[:, 128:256], False)
+
+
+def smem(count):
+    return [pl.BlockSpec(memory_space=pltpu.SMEM)] * count
+
+
 def per_device(
     frames, text_tokens, step_embed, segments, cotangent,
     w_ada, b_ada, w_qkv, w_out, g_cross, w_cq, w_ckv, w_co, w_up, b_up, w_down, b_down,
 ):
     seq_count = lax.axis_size("seq")
     rows_count = lax.axis_size("rows")
-    seq_index = lax.axis_index("seq")
-    rows_index = lax.axis_index("rows")
-    frames, text_tokens, step_embed = frames[0], text_tokens[0], step_embed[0]
-    segments, cotangent = segments[0], cotangent[0]
-    here, model = frames.shape
-    length = segments.shape[0]
+    here, model = frames.shape[1:]
+    length = segments.shape[1]
     hidden = w_up.shape[1]
     assert (length // ITEMS) % here == 0
-    block_slots = segments[::here]
-    slot = lax.dynamic_index_in_dim(block_slots, seq_index, 0, keepdims=False)
-    mask = (segments == slot).astype(F32)[None]
-    text_rows = 128
-    text_mine = jnp.pad(
-        lax.dynamic_slice_in_dim(text_tokens, slot * TXT, TXT, axis=0),
-        ((0, text_rows - TXT), (0, 0)),
-    )
-    step_rows = 16
-    step_pad = jnp.pad(step_embed, ((0, step_rows - ITEMS), (0, 0)))
-    wanted = jnp.concatenate([block_slots, slot[None]])
-    picks = (wanted[:, None] == jnp.arange(step_rows)[None, :]).astype(F32)[:, :, None]
-    text_pick = (block_slots == seq_index).astype(F32)[:, None, None]
+    text_rows, text_kept, step_rows = 128, 80, 16
 
     def like(shape, dtype=BF16):
         return jax.ShapeDtypeStruct(shape, dtype)
@@ -856,7 +973,7 @@
     vmem = pltpu.VMEM
     (
         output, act, gm_t, h3, gpre, h2, cross, gqc, gc, gkvc, attn, ga, gattn, gx1, query,
-        kv, h_all, lse, mods, text_part, early,
+        kv, h_all, lse, mods, text_part, early, text_mine,
     ) = pl.pallas_call(
         forward_kernel,
         out_shape=(
@@ -864,12 +981,12 @@
             square, square, square, square, like((text_rows, 2 * model)), square, square,
             square, like((here, model), F32), square, like((length, 2 * model)),
             like((length, model)), like((here, 128), F32), like((8, model), F32),
-            like((text_rows, model)), like((16, model), F32),
+            like((text_rows, model)), like((16, model), F32), like((text_rows, model)),
         ),
-        in_specs=in_any(1) + in_vmem(5)
+        in_specs=in_any(1) + in_vmem(3) + smem(1) + in_vmem(1)
         + in_any(1) + in_vmem(1) + in_any(2) + in_vmem(1) + in_any(4) + in_vmem(1)
         + in_any(1) + in_vmem(1),
-        out_specs=tuple(in_vmem(21)),
+        out_specs=tuple(in_vmem(22)),
         scratch_shapes=[
             vmem((seq_count, here, model), BF16),
             vmem(w_ada.shape, BF16), vmem(w_qkv.shape, BF16), vmem(w_out.shape, BF16),
@@ -878,6 +995,7 @@
             vmem((HEADS, here, text_rows), F32),
             vmem((here, model), F32), vmem((here, model), F32),
             vmem((step_rows, 6 * model), F32),
+            vmem((1, hidden), F32),
             dma((9,)), dma((4,)), dma((4,)),
         ],
         compiler_params=pltpu.CompilerParams(
@@ -885,9 +1003,8 @@
         ),
         name="forward_layer",
     )(
-        frames, cotangent, text_mine, step_pad, picks, mask,
-        w_ada, b_ada[None], w_qkv, w_out, g_cross[None], w_cq, w_ckv, w_co, w_up,
-        b_up[None], w_down, b_down[None],
+        frames, cotangent, text_tokens, step_embed, segments, segments,
+        w_ada, b_ada, w_qkv, w_out, g_cross, w_cq, w_ckv, w_co, w_up, b_up, w_down, b_down,
     )
 
     tall, width = model // rows_count, model // 2
@@ -896,10 +1013,10 @@
         backward_kernel,
         out_shape=(
             like((CHUNKS, tall, width), F32), like((here, model), F32),
-            like((text_rows, model), F32), like(table + (16, model), F32),
-            like(table + (8, model), F32),
+            like((text_kept, model), F32), like(table + (16, model)),
+            like(table + (16, 128)),
         ),
-        in_specs=in_vmem(25),
+        in_specs=in_vmem(15) + smem(1) + in_vmem(1) + in_any(8),
         out_specs=tuple(in_vmem(5)),
         scratch_shapes=[
             vmem((CHUNKS,) + table + (tall, width), BF16),
@@ -910,8 +1027,12 @@
             vmem((3, here, model), BF16),
             vmem((length, 3 * model), BF16),
             vmem((3, here, model), BF16),
-            vmem((2, 2, text_rows, model), BF16),
-            vmem((8, model), F32),
+            vmem((2, 2, text_kept, model), BF16),
+            vmem((16, 128), F32),
+            vmem((here, model), BF16), vmem((here, model), F32), vmem((here, model), BF16),
+            vmem((length, 2 * model), BF16), vmem((length, model), BF16),
+            vmem((here, 128), F32), vmem((here, model), BF16), vmem(w_qkv.shape, BF16),
+            dma((8,)),
             dma((CHUNKS,)), dma((CHUNKS,)),
             dma((CHUNKS, 2)), dma((CHUNKS, 2)),
             dma((CHUNKS, 2)), dma((CHUNKS, 2)),
@@ -924,72 +1045,32 @@
         ),
         name="backward_layer",
     )(
-        act, gm_t, h3, gpre, h2, cross, gqc, gc, gkvc, attn, ga, gattn, gx1, query,
-        kv, h_all, lse, mods, text_part, early, text_mine, mask, frames, w_qkv, text_pick,
-    )
-
-    def by_device(entries):
-        return entries.transpose(1, 0, 2, 3, 4, 5).reshape(
-            (rows_count * seq_count,) + entries.shape[4:]
-        )
-
-    e_all, l_all = by_device(e_all), by_device(l_all)
-    item_all = jnp.concatenate([l_all[:, :2], e_all[:, :4]], axis=1).reshape(
-        rows_count * seq_count, 6 * model
-    )
-    ada_all = e_all[:, 10]
-
-    def share(vector, count, index):
-        size = vector.shape[-1] // count
-        return lax.dynamic_slice_in_dim(vector, index * size, size, axis=-1)
-
-    d_b_ada = share(jnp.sum(item_all, axis=0), rows_count, rows_index)
-    d_g_cross = share(jnp.sum(e_all[:, 4], axis=0), rows_count, rows_index)
-    d_b_up = share(jnp.sum(e_all[:, 5:9], axis=0).reshape(-1), rows_count, rows_index)
-    d_b_down = share(jnp.sum(e_all[:, 9], axis=0), rows_count, rows_index)
-    d_w_ada = lax.dot_general(
-        share(ada_all, rows_count, rows_index),
-        share(item_all, seq_count, seq_index),
-        (((0,), (0,)), ((), ())),
-        precision=PRECISE,
-        preferred_element_type=F32,
-    )
-    row_items = lax.dynamic_slice_in_dim(item_all, rows_index * seq_count, seq_count, axis=0)
-    item_mine = jnp.sum(row_items * text_pick[:, 0], axis=0, keepdims=True)
-    item_high = item_mine.astype(BF16)
-    item_low = (item_mine - item_high.astype(F32)).astype(BF16)
-    d_ada = jnp.sum(
-        dot_t(jnp.concatenate([item_high, item_low], axis=0), w_ada), axis=0, keepdims=True
-    )
-    my_step = lax.dynamic_slice_in_dim(step_embed, seq_index, 1, axis=0).astype(F32)
-    unused_step, silu_back = jax.vjp(jax.nn.silu, my_step)
-    d_step = silu_back(d_ada)[0]
-
-    odd = seq_index % 2 == 1
-
-    def place(full, mixed, first):
-        even = mixed[:, :HEAD] if first else mixed[:, HEAD:]
-        other = mixed[:, HEAD:] if first else mixed[:, :HEAD]
-        return jnp.where(
-            odd,
-            jnp.concatenate([other, full], axis=1),
-            jnp.concatenate([full, even], axis=1),
-        )
-
-    d_w_down = jnp.concatenate([done[0], done[1]], axis=0).T
-    d_w_up = jnp.concatenate([done[2], done[3]], axis=1)
-    d_w_cq = place(done[4][:, :128], done[4][:, 256:], True)
-    d_w_co = place(done[4][:, 128:256], done[4][:, 256:], False)
-    d_w_ckv = done[5]
-    d_w_qkv = place(
-        jnp.concatenate([done[6], done[7][:, :128]], axis=1), done[7][:, 128:256], True
-    )
-    d_w_out = place(done[7][:, 256:], done[7][:, 128:256], False)
-    return (
-        output[None], d_frames[None], d_text[None, :TXT], d_step[None],
-        d_w_ada, d_b_ada, d_w_qkv, d_w_out, d_g_cross, d_w_cq, d_w_ckv, d_w_co,
-        d_w_up, d_b_up, d_w_down, d_b_down,
-    )
+        act, gm_t, h3, gpre, h2, cross, gqc, gc, gkvc, attn, ga, mods, text_part, early,
+        text_mine, segments, segments, gattn, gx1, query, kv, h_all, lse, frames, w_qkv,
+    )
+
+    def shard(*shape):
+        return like(shape, F32)
+
+    seq_share = model // seq_count
+    return pl.pallas_call(
+        finish_kernel,
+        out_shape=(
+            like((1, here, model)), shard(1, here, model), shard(1, TXT, model),
+            shard(1, 1, model), shard(tall, 6 * seq_share), shard(6 * tall),
+            shard(tall, 3 * seq_share), shard(tall, seq_share), shard(tall),
+            shard(tall, seq_share), shard(tall, 2 * seq_share), shard(tall, seq_share),
+            shard(tall, hidden // seq_count), shard(hidden // rows_count),
+            shard(hidden // rows_count, seq_share), shard(tall),
+        ),
+        in_specs=in_vmem(7) + smem(1) + in_vmem(1),
+        out_specs=tuple(in_vmem(16)),
+        scratch_shapes=[
+            vmem((32, 6 * model), F32), vmem((32, model), F32), vmem((model, 32), F32),
+        ],
+        compiler_params=pltpu.CompilerParams(vmem_limit_bytes=VMEM_MOST),
+        name="finish_layer",
+    )(done, d_frames, d_text, output, e_all, l_all, step_embed, segments, w_ada)
 
 
 def solution(mesh):

time: 247 us -> 208 us (0.84)
  local copies, waits for them, and re-layouts: 19.2 us -> 3.74 us
  other arithmetic: 9.19 us -> 0 us
  Pallas kernels: 210 us -> 203 us
  matrix products: 6.36 us -> 0 us
    pallas_call x1, Pallas kernels: 151 us -> 136 us  [per_device(): pl.pallas_call(backward_kernel, out_shape=(like((CHUNKS, tall, width), F3...]
    pallas_call x0 -> x1, Pallas kernels: none -> 8.44 us  [per_device(): pl.pallas_call(finish_kernel, out_shape=(like((1, here, model)), shard(1,...]
    broadcast_in_dim x6 -> x0, local copies, waits for them, and re-layouts: 6.77 us -> none  [the longest x1 1.32 us: per_device(): b_ada[None]]
    dot_general x2 -> x0, matrix products: 6.36 us -> none  [the longest x1 5.04 us: dot_t(): lax.dot_general(left, right, (((1,), (1,)), ((), ())), preferred_element_...]
    dynamic_slice x7 -> x0, local copies, waits for them, and re-layouts: 4.11 us -> none  [the longest x5 2.58 us: share(): return lax.dynamic_slice_in_dim(vector, index * size, size, axis=-1)]
    pallas_call x0 -> x2, local copies, waits for them, and re-layouts: none -> 3.74 us  [per_device(): pl.pallas_call(finish_kernel, out_shape=(like((1, here, model)), shard(1,...]
    unnamed x18 -> x0, local copies, waits for them, and re-layouts: 2.96 us -> none
    convert_element_type x4 -> x0, other arithmetic: 2.64 us -> none  [the longest x1 1.93 us: per_device(): mask = (segments == slot).astype(F32)[None]]
where the time goes in v3:
time: 208 us
  Pallas kernels  203 us (98%)
  local copies, waits for them, and re-layouts  3.74 us (2%)
    pallas_call x1, Pallas kernels, per_device(): pl.pallas_call(backward_kernel, out_shape=(like((CHUNKS, tall, width), F3...  136 us
    pallas_call x1, Pallas kernels, per_device(): pl.pallas_call(forward_kernel, out_shape=(square, like((here, hidden)), l...  59 us
    pallas_call x1, Pallas kernels, per_device(): pl.pallas_call(finish_kernel, out_shape=(like((1, here, model)), shard(1,...  8.44 us

profile of v3, /device:TPU:0, one launch (start us, length us, event | category | flops | bytes accessed | tf_op | source)
XLA Modules:
  0.0 207.5 jit_solution(2064184339133104979)
XLA Ops:
  0.7 59.0 %forward_layer.1 = (bf16[256,768]{1,0:T(8,128)(2,1)}, bf16[256,3072]{1,0:T(8,128)(2,1)}, bf16[768,256]{1,0:T(8,128)(2,1)}, bf16[256,768]{1,0:T(8,128)(2,1)}, bf1...) custom-call(bf16[1,256,768]{2,1,0:T(8,128)(2,1)} %frames_h.1, ...), custom_call_target="tpu_custom_call" | custom-call | tf_op jit(solution)/shard_map/forward_layer/pallas_call | solution.py:977
  59.7 135.6 %backward_layer.1 = (f32[8,96,384]{2,1,0:T(8,128)}, f32[256,768]{1,0:T(8,128)}, f32[80,768]{1,0:T(8,128)}, bf16[2,4,2,2,16,768]{5,4,3,2,1,0:T(8,128)(2,1)}, bf16[2,4,2,2,16,128]{5,4,3,2,1,0:T(8,128)(2,1)}) custom-call(bf16[256,3072]{1,0:T(8,128)(2,1)} %get-tuple-element.43.act, bf16[768,256]{1,0:T(8,128)(2,1)} %get-tuple-element.44.gm_t, ...), custom_call_target="tpu_custom_call" | custom-call | tf_op jit(solution)/shard_map/backward_layer/pallas_call | solution.py:1012
  195.3 8.4 %finish_layer.1 = (bf16[1,256,768]{2,1,0:T(8,128)(2,1)}, f32[1,256,768]{2,1,0:T(8,128)}, f32[1,77,768]{2,1,0:T(8,128)}, f32[1,1,768]{2,1,0:T(1,128)}, f32[96,115...) custom-call(f32[8,96,384]{2,1,0:T(8,128)} %get-tuple-element.64.done, ...), custom_call_target="tpu_custom_call" | custom-call | tf_op jit(solution)/shard_map/finish_layer/pallas_call | solution.py:1056
  203.8 1.9 copy.33
  205.7 1.9 copy.34

commit v4 on v3

--- a/solution.py
+++ b/solution.py
@@ -327,13 +327,15 @@
             ]
         )
     ]
-    for load in loads:
-        load.start()
+    for i in (0, 1):
+        loads[i].start()
     enter([x_peer, y_peer])
     to_x = remote(frames, fr.at[seq], send.at[0], recv.at[0], x_peer)
     to_y = remote(frames, fr.at[seq], send.at[1], recv.at[1], y_peer)
     to_x.start()
     to_y.start()
+    loads[2].start()
+    loads[4].start()
 
     def row(at):
         return mods[at : at + 1, :]
@@ -344,6 +346,8 @@
     ada = (step_f32 / (1.0 + jnp.exp(-step_f32))).astype(BF16)
     loads[1].wait()
     item[...] = dot(ada, ada_v[...]) + b_ada[...].astype(F32)[None]
+    for i in (3, 5, 6, 7, 8):
+        loads[i].start()
     slot_row = lax.broadcasted_iota(jnp.int32, (item.shape[0], model), 0)
     chosen_mine = (slot_row == slot).astype(F32)
     for part_at in range(6):
@@ -368,19 +372,6 @@
     loads[2].wait()
     h_one = take(seq)
     query[...] = dot(h_one, qkv_v[:, :model]).astype(BF16)
-    to_x.wait_recv()
-    fwd_y = remote(
-        fr.at[x_id, pl.ds(0, part)], fr.at[x_id, pl.ds(0, part)], send.at[2], recv.at[2], y_peer
-    )
-    fwd_y.start()
-    to_y.wait_recv()
-    fwd_x = remote(
-        fr.at[y_id, pl.ds(part, part)], fr.at[y_id, pl.ds(part, part)],
-        send.at[3], recv.at[3], x_peer,
-    )
-    fwd_x.start()
-    take(x_id)
-    take(y_id)
     loads[4].wait()
     picked = (text_mine.shape[0], text.shape[1])
     text_at = lax.broadcasted_iota(jnp.int32, picked, 0)
@@ -389,6 +380,19 @@
     text_mine[...] = dot(hot, text[0]).astype(BF16)
     text_kv = dot(text_mine[...], ckv_v[...]).astype(BF16)
     gkvc[...] = text_kv
+    to_x.wait_recv()
+    fwd_y = remote(
+        fr.at[x_id, pl.ds(0, part)], fr.at[x_id, pl.ds(0, part)], send.at[2], recv.at[2], y_peer
+    )
+    fwd_y.start()
+    to_y.wait_recv()
+    fwd_x = remote(
+        fr.at[y_id, pl.ds(part, part)], fr.at[y_id, pl.ds(part, part)],
+        send.at[3], recv.at[3], x_peer,
+    )
+    fwd_x.start()
+    take(x_id)
+    take(y_id)
     fwd_y.wait_recv()
     fwd_x.wait_recv()
     take(d_id)
@@ -424,7 +428,7 @@
     text_rows = text_mine.shape[0]
     key_lane = lax.broadcasted_iota(jnp.int32, (here, text_rows), 1)
 
-    @pl.loop(0, HEADS // 2)
+    @pl.loop(0, HEADS // 2, unroll=True)
     def _(p):
         at = lanes(p)
         value_at = lanes(p + HEADS // 2)
@@ -483,7 +487,7 @@
     gc[...] = grad_x2.astype(BF16)
     ga[...] = dot_t(gc[...], co_v[...]).astype(BF16)
 
-    @pl.loop(0, HEADS // 2)
+    @pl.loop(0, HEADS // 2, unroll=True)
     def _(p):
         at = lanes(p)
         value_at = lanes(p + HEADS // 2)
@@ -522,6 +526,10 @@
 GELU_SCALE = 0.7978845608028654
 
 
+ORDER = (2, 0, 3, 1, 4, 5, 6, 7)
+DEEP = (0, 1)
+
+
 def backward_kernel(
     act, gm_t, h3, gpre, h2, cross, gqc, gc, gkvc, attn, ga, mods, text_part, early, text,
     seg_s, seg, gattn_h, gx1_h, query_h, kv_h, h_all_h, lse_h, frames_h, w_qkv_h,
@@ -535,9 +543,12 @@
     y, x = seq // 2, seq % 2
     z, c = rows // 2, rows % 2
     core_peer = {"rows": z * 2 + (1 - c)}
-    x_id, y_id, d_id = y * 2 + 1 - x, (1 - y) * 2 + x, (1 - y) * 2 + 1 - x
-    x_peer, y_peer, d_peer = {"seq": x_id}, {"seq": y_id}, {"seq": d_id}
+    x_id, y_id = y * 2 + 1 - x, (1 - y) * 2 + x
+    x_peer, y_peer = {"seq": x_id}, {"seq": y_id}
     z_peers = [{"rows": lax.rem(z + d, 4) * 2 + c} for d in (1, 2, 3)]
+    zh, zl = z // 2, z % 2
+    near_peer = {"rows": (zh * 2 + 1 - zl) * 2 + c}
+    far_peer = {"rows": ((1 - zh) * 2 + zl) * 2 + c}
     loads = [
         pltpu.make_async_copy(src, dst, local.at[i])
         for i, (src, dst) in enumerate(
@@ -549,7 +560,7 @@
     ]
     for load in loads:
         load.start()
-    enter([core_peer, x_peer, y_peer, d_peer] + z_peers)
+    enter([core_peer, x_peer, y_peer] + z_peers)
 
     tall, width = G.shape[-2:]
     here, model = frames.shape
@@ -644,8 +655,7 @@
                 put_lanes(k, s, 256, t_dot(attn[...], ga[:, lanes(full)]))
 
     def core_copy(k):
-        slot = k % 2
-        return remote(G.at[k, 1 - c], R0.at[slot], s0.at[k], r0.at[k], core_peer)
+        return remote(G.at[k, 1 - c], R0.at[ORDER.index(k) % 2], s0.at[k], r0.at[k], core_peer)
 
     def first_copies(k):
         return (
@@ -668,26 +678,106 @@
             for d in (1, 2, 3)
         ]
 
+    def near_copies(k):
+        return [
+            remote(
+                G.at[k, c, h * 2 + 1 - zl], R1.at[k, h], s3.at[k, h], r3.at[k, h], near_peer
+            )
+            for h in range(2)
+        ]
+
+    def far_copy(k):
+        return remote(
+            G.at[k, c, (1 - zh) * 2 + zl], R2.at[k], s3.at[k, 2], r3.at[k, 2], far_peer
+        )
+
+    def pair_copies(k):
+        if k % 2 == 0:
+            return [
+                remote(
+                    G.at[k, c, z, other, 1 - x], R3.at[k, other],
+                    s1.at[k, other], r1.at[k, other], x_peer,
+                )
+                for other in range(2)
+            ]
+        return [
+            remote(
+                G.at[k, c, z, 1 - y, other], R3.at[k, other],
+                s1.at[k, other], r1.at[k, other], y_peer,
+            )
+            for other in range(2)
+        ]
+
+    def last_copy(k):
+        if k % 2 == 0:
+            return remote(
+                G.at[k, c, z, 1 - y, x], R3.at[k, 2], s2.at[k, 0], r2.at[k, 0], y_peer
+            )
+        return remote(G.at[k, c, z, y, 1 - x], R3.at[k, 2], s2.at[k, 0], r2.at[k, 0], x_peer)
+
     def add(one, two):
         return (one.astype(F32) + two.astype(F32)).astype(BF16)
 
+    def deep1(k):
+        core_add(k)
+        for copy in near_copies(k):
+            copy.start()
+
+    def deep2(k):
+        for copy in near_copies(k):
+            copy.wait_recv()
+        for h in range(2):
+            for yy in range(2):
+                for xx in range(2):
+                    at = h * 2 + zl
+                    G[k, c, at, yy, xx] = add(G[k, c, at, yy, xx], R1[k, h, yy, xx])
+        far_copy(k).start()
+
+    def deep3(k):
+        far_copy(k).wait_recv()
+        for yy in range(2):
+            for xx in range(2):
+                G[k, c, z, yy, xx] = add(G[k, c, z, yy, xx], R2[k, yy, xx])
+        for copy in pair_copies(k):
+            copy.start()
+
+    def deep4(k):
+        for copy in pair_copies(k):
+            copy.wait_recv()
+        for other in range(2):
+            if k % 2 == 0:
+                G[k, c, z, other, x] = add(G[k, c, z, other, x], R3[k, other])
+            else:
+                G[k, c, z, y, other] = add(G[k, c, z, y, other], R3[k, other])
+        last_copy(k).start()
+
+    def deep5(k):
+        last_copy(k).wait_recv()
+        out[k] = G[k, c, z, y, x].astype(F32) + R3[k, 2].astype(F32)
+
+    def deep_copies(k):
+        return near_copies(k) + [far_copy(k)] + pair_copies(k) + [last_copy(k)]
+
     def phase0(k):
         compute(k)
-        if k >= 2:
+        if ORDER.index(k) >= 2:
             pl.semaphore_wait(free, 1)
         core_copy(k).start()
 
-    def phase1(k):
+    def core_add(k):
         core_copy(k).wait_recv()
 
         @pl.loop(0, 4)
         def _(zz):
             for yy in range(2):
                 for xx in range(2):
-                    G[k, c, zz, yy, xx] = add(G[k, c, zz, yy, xx], R0[k % 2, zz, yy, xx])
-
-        if k < CHUNKS - 2:
+                    G[k, c, zz, yy, xx] = add(G[k, c, zz, yy, xx], R0[ORDER.index(k) % 2, zz, yy, xx])
+
+        if ORDER.index(k) < CHUNKS - 2:
             pl.semaphore_signal(free, inc=1, device_id=core_peer, device_id_type=MESH)
+
+    def phase1(k):
+        core_add(k)
         for copy in first_copies(k):
             copy.start()
 
@@ -720,23 +810,23 @@
 
     e_all[c, z, y, x] = early[...].astype(BF16)
     T[y, x] = text_part[: T.shape[2], :]
+    phase0(2)
     phase0(0)
+    phase1(2)
     advance(early_steps, 0)
     advance(text_steps, 0)
+    phase0(3)
+    deep1(0)
     phase0(1)
-    phase1(0)
-    phase0(2)
-    phase1(1)
+    phase1(3)
+    phase0(4)
+    deep1(1)
     advance(early_steps, 1)
     advance(text_steps, 1)
-    phase0(3)
-    phase1(2)
-    phase0(4)
-    phase1(3)
-    advance(early_steps, 2)
     phase0(5)
     phase1(4)
     phase1(5)
+    advance(early_steps, 2)
 
     own = pl.ds(pl.multiple_of(seq * here, here), here)
     dqkv[:, :model] = jnp.zeros((dqkv.shape[0], model), BF16)
@@ -774,34 +864,50 @@
         rows_at = pl.ds(pl.multiple_of(block * here, here), here)
         return dot_t(dqkv[rows_at, model:], w_qkv[:, model:])
 
-    up_copies = []
-    for i, (block, peer) in enumerate(((d_id, d_peer), (x_id, x_peer), (y_id, y_peer))):
-        up_low[i] = up_block(block).astype(BF16)
-        copy = remote(up_low.at[i], R4.at[i], s4.at[i], r4.at[i], peer)
+    part = here // 2
+    up_first = (
+        remote(up_low.at[:, 1 - x, :part], R4.at[0:2], s4.at[0], r4.at[0], x_peer),
+        remote(up_low.at[1 - y, :, part:], R4.at[2:4], s4.at[1], r4.at[1], y_peer),
+    )
+    up_second = (
+        remote(up_low.at[1 - y, x, :part], R4.at[4], s4.at[2], r4.at[2], y_peer),
+        remote(up_low.at[y, 1 - x, part:], R4.at[5], s4.at[3], r4.at[3], x_peer),
+    )
+    deep2(0)
+    for block in range(4):
+        up_low[block // 2, block % 2] = up_block(block).astype(BF16)
+    for copy in up_first:
         copy.start()
-        up_copies.append(copy)
     phase0(6)
-    phase2(0)
+    phase2(2)
+    deep2(1)
     phase0(7)
-    phase2(1)
     phase1(6)
-    phase3(0)
-    phase2(2)
+    phase2(3)
     phase1(7)
-    phase3(1)
+    phase3(2)
+    deep3(0)
+    for copy in up_first:
+        copy.wait_recv()
+    for i in range(2):
+        up_low[i, x, :part] = add(up_low[i, x, :part], R4[i])
+        up_low[y, i, part:] = add(up_low[y, i, part:], R4[2 + i])
+    for copy in up_second:
+        copy.start()
     advance(early_steps, 3)
     advance(text_steps, 2)
-
-    @pl.loop(3, 6)
-    def _(k):
-        phase2(k)
-        phase3(k - 1)
-
-    for copy in up_copies:
+    phase2(4)
+    phase3(3)
+    deep3(1)
+    deep4(0)
+    phase2(5)
+    phase3(4)
+    deep4(1)
+    deep5(0)
+    for copy in up_second:
         copy.wait_recv()
-    up_one = dot_t(dqkv[own, :], w_qkv[...])
-    for i in range(3):
-        up_one = up_one + R4[i].astype(F32)
+    up_one = dot_t(dqkv[own, :model], w_qkv[:, :model]) + up_low[y, x].astype(F32)
+    up_one = up_one + jnp.concatenate([R4[4], R4[5]], axis=0).astype(F32)
     normed, inverse = norm_parts(frames[...].astype(F32))
     for i, total in enumerate((col_sum(up_one), col_sum(up_one * normed))):
         for j in range(model // 128):
@@ -820,26 +926,31 @@
     phase2(6)
     phase3(5)
     advance(late_steps, 1)
+    deep5(1)
     phase2(7)
     phase3(6)
     advance(late_steps, 2)
     phase3(7)
     advance(late_steps, 3)
 
-    @pl.loop(0, CHUNKS)
+    @pl.loop(len(DEEP), CHUNKS)
     def _(k):
         phase4(k)
 
     advance(early_steps, 4)
     advance(late_steps, 4)
-
-    @pl.loop(0, CHUNKS)
+    for k in range(CHUNKS):
+        core_copy(k).wait_send()
+    for k in DEEP:
+        for copy in deep_copies(k):
+            copy.wait_send()
+
+    @pl.loop(len(DEEP), CHUNKS)
     def _(k):
-        core_copy(k).wait_send()
         for copy in (*first_copies(k), *second_copies(k), *z_copies(k)):
             copy.wait_send()
 
-    for copy in up_copies:
+    for copy in (*up_first, *up_second):
         copy.wait_send()
     for steps in (early_steps, late_steps, text_steps):
         for step in steps:
@@ -867,7 +978,7 @@
     parts = model // 128
     output[0] = output_in[...]
     d_frames[0] = d_frames_in[...]
-    d_text[0] = d_text_in[: d_text.shape[1], :]
+    d_text[:, 0, :] = d_text_in[: d_text.shape[0], :]
     bias_sum = jnp.zeros((16, model), F32)
     for r in range(8):
         for s in range(4):
@@ -936,7 +1047,8 @@
         )
 
     width = model // 2
-    d_w_down[...] = jnp.concatenate([done[0], done[1]], axis=0).T
+    d_w_down[: model // 8] = done[0]
+    d_w_down[model // 8 :] = done[1]
     d_w_up[:, :width] = done[2]
     d_w_up[:, width:] = done[3]
     cross, last = done[4], done[7]
@@ -1024,9 +1136,9 @@
             vmem((CHUNKS, 2, 2, 2, tall, width), BF16),
             vmem((CHUNKS, 2, 2, tall, width), BF16),
             vmem((CHUNKS, 3, tall, width), BF16),
-            vmem((3, here, model), BF16),
+            vmem((6, here // 2, model), BF16),
             vmem((length, 3 * model), BF16),
-            vmem((3, here, model), BF16),
+            vmem((2, 2, here, model), BF16),
             vmem((2, 2, text_kept, model), BF16),
             vmem((16, 128), F32),
             vmem((here, model), BF16), vmem((here, model), F32), vmem((here, model), BF16),
@@ -1037,7 +1149,7 @@
             dma((CHUNKS, 2)), dma((CHUNKS, 2)),
             dma((CHUNKS, 2)), dma((CHUNKS, 2)),
             dma((CHUNKS, 3)), dma((CHUNKS, 3)),
-            dma((3,)), dma((3,)), dma((6,)), dma((6,)), dma((6,)), dma((6,)),
+            dma((4,)), dma((4,)), dma((6,)), dma((6,)), dma((6,)), dma((6,)),
             dma((2,)), dma((2,)), pltpu.SemaphoreType.REGULAR,
         ],
         compiler_params=pltpu.CompilerParams(
@@ -1053,15 +1165,15 @@
         return like(shape, F32)
 
     seq_share = model // seq_count
-    return pl.pallas_call(
+    results = pl.pallas_call(
         finish_kernel,
         out_shape=(
-            like((1, here, model)), shard(1, here, model), shard(1, TXT, model),
+            like((1, here, model)), shard(1, here, model), shard(TXT, 1, model),
             shard(1, 1, model), shard(tall, 6 * seq_share), shard(6 * tall),
             shard(tall, 3 * seq_share), shard(tall, seq_share), shard(tall),
             shard(tall, seq_share), shard(tall, 2 * seq_share), shard(tall, seq_share),
             shard(tall, hidden // seq_count), shard(hidden // rows_count),
-            shard(hidden // rows_count, seq_share), shard(tall),
+            shard(seq_share, hidden // rows_count), shard(tall),
         ),
         in_specs=in_vmem(7) + smem(1) + in_vmem(1),
         out_specs=tuple(in_vmem(16)),
@@ -1071,6 +1183,10 @@
         compiler_params=pltpu.CompilerParams(vmem_limit_bytes=VMEM_MOST),
         name="finish_layer",
     )(done, d_frames, d_text, output, e_all, l_all, step_embed, segments, w_ada)
+    results = list(results)
+    results[2] = results[2].transpose(1, 0, 2)
+    results[14] = results[14].T
+    return tuple(results)
 
 
 def solution(mesh):

time: 208 us -> 177 us (0.85)
  Pallas kernels: 203 us -> 176 us
  local copies, waits for them, and re-layouts: 3.74 us -> 0 us
    pallas_call x1, Pallas kernels: 136 us -> 113 us  [per_device(): pl.pallas_call(backward_kernel, out_shape=(like((CHUNKS, tall, width), F3...]
    pallas_call x1, Pallas kernels: 59 us -> 54.1 us  [per_device(): pl.pallas_call(forward_kernel, out_shape=(square, like((here, hidden)), l...]
    pallas_call x2 -> x0, local copies, waits for them, and re-layouts: 3.74 us -> none  [per_device(): pl.pallas_call(finish_kernel, out_shape=(like((1, here, model)), shard(1,...]
where the time goes in v4:
time: 177 us
  Pallas kernels  176 us (99%)
    pallas_call x1, Pallas kernels, per_device(): pl.pallas_call(backward_kernel, out_shape=(like((CHUNKS, tall, width), F3...  113 us
    pallas_call x1, Pallas kernels, per_device(): pl.pallas_call(forward_kernel, out_shape=(square, like((here, hidden)), l...  54.1 us
    pallas_call x1, Pallas kernels, per_device(): pl.pallas_call(finish_kernel, out_shape=(like((1, here, model)), shard(1,...  8.42 us

profile of v4, /device:TPU:0, one launch (start us, length us, event | category | flops | bytes accessed | tf_op | source)
XLA Modules:
  0.0 176.7 jit_solution(6386486614187735685)
XLA Ops:
  0.7 54.1 %forward_layer.1 = (bf16[256,768]{1,0:T(8,128)(2,1)}, bf16[256,3072]{1,0:T(8,128)(2,1)}, bf16[768,256]{1,0:T(8,128)(2,1)}, bf16[256,768]{1,0:T(8,128)(2,1)}, bf1...) custom-call(bf16[1,256,768]{2,1,0:T(8,128)(2,1)} %frames_h.1, ...), custom_call_target="tpu_custom_call" | custom-call | tf_op jit(solution)/shard_map/forward_layer/pallas_call | solution.py:1089
  54.7 113.3 %backward_layer.1 = (f32[8,96,384]{2,1,0:T(8,128)}, f32[256,768]{1,0:T(8,128)}, f32[80,768]{1,0:T(8,128)}, bf16[2,4,2,2,16,768]{5,4,3,2,1,0:T(8,128)(2,1)}, bf16[2,4,2,2,16,128]{5,4,3,2,1,0:T(8,128)(2,1)}) custom-call(bf16[256,3072]{1,0:T(8,128)(2,1)} %get-tuple-element.59.act, bf16[768,256]{1,0:T(8,128)(2,1)} %get-tuple-element.60.gm_t, ...), custom_call_target="tpu_custom_call" | custom-call | tf_op jit(solution)/shard_map/backward_layer/pallas_call | solution.py:1124
  168.1 8.4 %finish_layer.1 = (bf16[1,256,768]{2,1,0:T(8,128)(2,1)}, f32[1,256,768]{2,1,0:T(8,128)}, f32[77,1,768]{2,1,0:T(1,128)}, f32[1,1,768]{2,1,0:T(1,128)}, f32[96,115...) custom-call(f32[8,96,384]{2,1,0:T(8,128)} %get-tuple-element.80.done, ...), custom_call_target="tpu_custom_call" | custom-call | tf_op jit(solution)/shard_map/finish_layer/pallas_call | solution.py:1168

commit v5 on v4

--- a/solution.py
+++ b/solution.py
@@ -304,9 +304,9 @@
 def forward_kernel(
     frames, cot, text, step, seg_s, seg,
     w_ada, b_ada, w_qkv, w_out, g_cross, w_cq, w_ckv, w_co, w_up, b_up, w_down, b_down,
-    output, act, gm_t, h3, gpre, h2, cross, gqc, gc, gkvc, attn, ga, gattn, gx1, query,
-    kv, h_all, lse, mods, text_part, early, text_mine,
-    fr, ada_v, qkv_v, out_v, cq_v, ckv_v, co_v, up_v, down_v, prob_c, acc_m, acc_u,
+    output, act, gm_t, h3, gpre, h2, cross, gqc, gkvc, attn, query,
+    kv, h_all, lse, mods, early, text_mine, branch, x_one, x_two, acc_u, prob_c,
+    fr, ada_v, qkv_v, out_v, cq_v, ckv_v, co_v, up_v, down_v, gm, acc_m,
     item, up_bias, local, send, recv,
 ):
     seq = lax.axis_index("seq")
@@ -416,10 +416,10 @@
 
     loads[3].wait()
     branch_a = dot(attn[...], out_v[...])
-    x_one = frames_f32(fr[seq]) + row(2) * branch_a
-    gx1[...] = branch_a
+    x_one[...] = frames_f32(fr[seq]) + row(2) * branch_a
+    branch[...] = branch_a
     gain = g_cross[...].astype(F32)[None]
-    normed_1, inverse_1 = norm_parts(x_one)
+    normed_1, unused = norm_parts(x_one[...])
     h2[...] = (normed_1 * gain).astype(BF16)
     loads[5].wait()
     query_c = dot(h2[...], cq_v[...]).astype(BF16)
@@ -437,20 +437,21 @@
         for half in range(2):
             scores = dot_t(pick_half(pair, half), gkvc[:, at])
             probs, unused = softmax_rows(jnp.where(key_lane < TXT, scores, NEG_FILL))
-            prob_c[2 * p + half] = probs
-            outs.append(dot(probs.astype(BF16), gkvc[:, value_at]))
+            low = probs.astype(BF16)
+            prob_c[2 * p + half] = low
+            outs.append(dot(low, gkvc[:, value_at]))
         cross[:, at] = join_halves(*outs).astype(BF16)
 
     loads[6].wait()
-    x_two = x_one + dot(cross[...], co_v[...])
-    normed_2, inverse_2 = norm_parts(x_two)
+    x_two[...] = x_one[...] + dot(cross[...], co_v[...])
+    normed_2, unused = norm_parts(x_two[...])
     h3[...] = (normed_2 * (1.0 + row(4)) + row(3)).astype(BF16)
     grad_out = cot[0].astype(F32)
     grad_m = row(5) * grad_out
     gm_low = grad_m.astype(BF16)
     gm_t[...] = gm_low.astype(F32).T.astype(BF16)
     early[9:10, :] = col_sum(gm_low.astype(F32))
-    gc[...] = gm_low
+    gm[...] = gm_low
     acc_m[...] = jnp.zeros_like(acc_m)
     acc_u[...] = jnp.zeros_like(acc_u)
     loads[7].wait()
@@ -469,7 +470,7 @@
         slope = 0.5 * (1.0 + tanh) + 0.5 * pre * (1.0 - tanh * tanh) * (
             GELU_SCALE * (1.0 + 3.0 * 0.044715 * pre * pre)
         )
-        grad_pre = (dot_t(gc[...], down_v[at, :]) * slope).astype(BF16)
+        grad_pre = (dot_t(gm[...], down_v[at, :]) * slope).astype(BF16)
         gpre[:, at] = grad_pre
         acc_u[...] += dot_t(grad_pre, up_v[:, at])
 
@@ -477,44 +478,14 @@
         at = slice(quarter * model, (quarter + 1) * model)
         early[5 + quarter : 6 + quarter, :] = col_sum(gpre[:, at].astype(F32))
     branch_m = acc_m[...] + b_down[...].astype(F32)[None]
-    output[...] = (x_two + row(5) * branch_m).astype(BF16)
+    output[...] = (x_two[...] + row(5) * branch_m).astype(BF16)
     early[3:4, :] = col_sum(grad_out * branch_m)
     up_three = acc_u[...]
     early[1:2, :] = col_sum(up_three)
     early[2:3, :] = col_sum(up_three * normed_2)
-    grad_x2 = grad_out + norm_back(normed_2, inverse_2, up_three * (1.0 + row(4)))
-    acc_m[...] = grad_x2
-    gc[...] = grad_x2.astype(BF16)
-    ga[...] = dot_t(gc[...], co_v[...]).astype(BF16)
-
-    @pl.loop(0, HEADS // 2, unroll=True)
-    def _(p):
-        at = lanes(p)
-        value_at = lanes(p + HEADS // 2)
-        key_pair, value_pair = gkvc[:, at], gkvc[:, value_at]
-        query_pair, up_pair = gqc[:, at], ga[:, at]
-        d_q, d_k, d_v = [], [], []
-        for half in range(2):
-            probs = prob_c[2 * p + half]
-            grad_probs = dot_t(pick_half(up_pair, half), value_pair)
-            inner = jnp.sum(probs * grad_probs, axis=-1, keepdims=True)
-            grad_scores = (probs * (grad_probs - inner)).astype(BF16)
-            d_q.append(dot(grad_scores, key_pair))
-            d_k.append(t_dot(grad_scores, query_pair))
-            d_v.append(t_dot(probs.astype(BF16), up_pair))
-        gqc[:, at] = (join_halves(*d_q) * HEAD ** (-0.5)).astype(BF16)
-        gkvc[:, at] = (join_halves(*d_k) * HEAD ** (-0.5)).astype(BF16)
-        gkvc[:, value_at] = join_halves(*d_v).astype(BF16)
-
-    text_part[...] = dot_t(gkvc[...], ckv_v[...]).astype(BF16)
-    up_two = dot_t(gqc[...], cq_v[...])
-    early[4:5, :] = col_sum(up_two * normed_1)
-    grad_x1 = acc_m[...] + norm_back(normed_1, inverse_1, up_two * gain)
-    early[0:1, :] = col_sum(grad_x1 * gx1[...])
+    early[0:1, :] = jnp.zeros((1, model), F32)
+    early[4:5, :] = jnp.zeros((1, model), F32)
     early[11:16, :] = jnp.zeros((5, model), F32)
-    gx1[...] = grad_x1
-    ga[...] = (row(2) * grad_x1).astype(BF16)
-    gattn[...] = dot_t(ga[...], out_v[...]).astype(BF16)
     for copy in (to_x, to_y, fwd_x, fwd_y):
         copy.wait_send()
 
@@ -526,16 +497,19 @@
 GELU_SCALE = 0.7978845608028654
 
 
-ORDER = (2, 0, 3, 1, 4, 5, 6, 7)
-DEEP = (0, 1)
+ORDER = (1, 0, 2, 3, 4, 5, 6, 7)
+DEEP = (0, 4)
+FLAT = (1, 2, 3, 5, 6, 7)
 
 
 def backward_kernel(
-    act, gm_t, h3, gpre, h2, cross, gqc, gc, gkvc, attn, ga, mods, text_part, early, text,
-    seg_s, seg, gattn_h, gx1_h, query_h, kv_h, h_all_h, lse_h, frames_h, w_qkv_h,
+    act, gm_t, h3, gpre, h2, cross, attn, mods, early, text, g_cross,
+    seg_s, seg, query_h, kv_h, h_all_h, lse_h, frames_h, w_qkv_h,
+    gqc_h, gkvc_h, cot_h, branch_h, x_one_h, x_two_h, up_h, prob_h, w_co, w_cq, w_out, w_ckv,
     out, d_frames, d_text, e_all, l_all,
     G, R0, R1, R2, R3, R4, dqkv, up_low, T, late,
-    gattn, gx1, query, kv, h_all, lse, frames, w_qkv, local,
+    gattn, gx1, kv, h_all, lse, w_qkv, local,
+    gqc, gkvc, gc, ga, branch, x_one, x_two, prob_c,
     s0, r0, s1, r1, s2, r2, s3, r3, s4, r4, se, re, sl, rl, st, rt, free,
 ):
     seq = lax.axis_index("seq")
@@ -549,34 +523,37 @@
     zh, zl = z // 2, z % 2
     near_peer = {"rows": (zh * 2 + 1 - zl) * 2 + c}
     far_peer = {"rows": ((1 - zh) * 2 + zl) * 2 + c}
+    here, model = gc.shape
+    first_loads = [
+        (up_h, d_frames), (x_two_h, x_two), (cot_h.at[0], gattn),
+        (w_co, dqkv.at[:model, :model]), (gkvc_h, gkvc), (gqc_h, gqc), (prob_h, prob_c),
+        (w_cq, dqkv.at[:model, model : 2 * model]), (x_one_h, x_one), (branch_h, branch),
+        (w_ckv, w_qkv.at[:, : 2 * model]), (w_out, dqkv.at[:model, 2 * model :]),
+        (kv_h, kv), (lse_h, lse), (h_all_h, h_all),
+        (query_h, gqc), (frames_h.at[0], gc), (w_qkv_h, w_qkv),
+    ]
     loads = [
-        pltpu.make_async_copy(src, dst, local.at[i])
-        for i, (src, dst) in enumerate(
-            [
-                (query_h, query), (kv_h, kv), (gattn_h, gattn), (lse_h, lse),
-                (w_qkv_h, w_qkv), (h_all_h, h_all), (gx1_h, gx1), (frames_h.at[0], frames),
-            ]
-        )
+        pltpu.make_async_copy(src, dst, local.at[i]) for i, (src, dst) in enumerate(first_loads)
     ]
+    last_load = loads.pop()
+    frames_load = loads.pop()
+    query_load = loads.pop()
     for load in loads:
         load.start()
     enter([core_peer, x_peer, y_peer] + z_peers)
 
     tall, width = G.shape[-2:]
-    here, model = frames.shape
     mask = seg[...] == seg_s[0, seq * here]
 
     def gather_copies(table, send, recv):
-        mine = table.at[c, z, y, x]
-        pair = table.at[c, z, y]
-        plane = table.at[c, z]
+        mine, line, sheet = table.at[c, z, y, x], table.at[c, :, y, x], table.at[c, :, y]
         return (
-            [remote(mine, mine, send.at[0], recv.at[0], x_peer)],
-            [remote(pair, pair, send.at[1], recv.at[1], y_peer)],
             [
-                remote(plane, plane, send.at[1 + d], recv.at[1 + d], z_peers[d - 1])
+                remote(mine, mine, send.at[d - 1], recv.at[d - 1], z_peers[d - 1])
                 for d in (1, 2, 3)
             ],
+            [remote(line, line, send.at[3], recv.at[3], x_peer)],
+            [remote(sheet, sheet, send.at[4], recv.at[4], y_peer)],
             [remote(table.at[c], table.at[c], send.at[5], recv.at[5], core_peer)],
         )
 
@@ -669,14 +646,19 @@
             remote(G.at[k, c, 2:4, y, 1 - x], R2.at[k, 1], s2.at[k, 1], r2.at[k, 1], x_peer),
         )
 
-    def z_copies(k):
+    def z_near(k):
         return [
             remote(
-                G.at[k, c, lax.rem(z + d, 4), y, x], R3.at[k, d - 1],
-                s3.at[k, d - 1], r3.at[k, d - 1], z_peers[d - 1],
+                G.at[k, c, h * 2 + 1 - zl, y, x], R3.at[k, h],
+                s3.at[k, h], r3.at[k, h], near_peer,
             )
-            for d in (1, 2, 3)
+            for h in range(2)
         ]
+
+    def z_far(k):
+        return remote(
+            G.at[k, c, (1 - zh) * 2 + zl, y, x], R3.at[k, 2], s3.at[k, 2], r3.at[k, 2], far_peer
+        )
 
     def near_copies(k):
         return [
@@ -692,7 +674,7 @@
         )
 
     def pair_copies(k):
-        if k % 2 == 0:
+        if k == 0:
             return [
                 remote(
                     G.at[k, c, z, other, 1 - x], R3.at[k, other],
@@ -709,7 +691,7 @@
         ]
 
     def last_copy(k):
-        if k % 2 == 0:
+        if k == 0:
             return remote(
                 G.at[k, c, z, 1 - y, x], R3.at[k, 2], s2.at[k, 0], r2.at[k, 0], y_peer
             )
@@ -745,7 +727,7 @@
         for copy in pair_copies(k):
             copy.wait_recv()
         for other in range(2):
-            if k % 2 == 0:
+            if k == 0:
                 G[k, c, z, other, x] = add(G[k, c, z, other, x], R3[k, other])
             else:
                 G[k, c, z, y, other] = add(G[k, c, z, y, other], R3[k, other])
@@ -797,50 +779,102 @@
         for zz in range(2):
             G[k, c, zz, y, x] = add(G[k, c, zz, y, x], R2[k, 0, zz])
             G[k, c, 2 + zz, y, x] = add(G[k, c, 2 + zz, y, x], R2[k, 1, zz])
-        for copy in z_copies(k):
+        for copy in z_near(k):
             copy.start()
 
     def phase4(k):
-        for copy in z_copies(k):
+        for copy in z_near(k):
             copy.wait_recv()
-        total = G[k, c, z, y, x].astype(F32)
-        for d in range(3):
-            total = total + R3[k, d].astype(F32)
-        out[k] = total
-
-    e_all[c, z, y, x] = early[...].astype(BF16)
-    T[y, x] = text_part[: T.shape[2], :]
+        for h in range(2):
+            at = h * 2 + zl
+            G[k, c, at, y, x] = add(G[k, c, at, y, x], R3[k, h])
+        z_far(k).start()
+
+    def phase5(k):
+        z_far(k).wait_recv()
+        out[k] = G[k, c, z, y, x].astype(F32) + R3[k, 2].astype(F32)
+
+    phase0(1)
+    phase0(0)
+    phase1(1)
     phase0(2)
-    phase0(0)
+    deep1(0)
+    phase0(3)
     phase1(2)
+    phase1(3)
+    for load in loads:
+        load.wait()
+
+    def row(at):
+        return mods[at : at + 1, :]
+
+    co_v, cq_v = dqkv.at[:model, :model], dqkv.at[:model, model : 2 * model]
+    out_v, ckv_v = dqkv.at[:model, 2 * model :], w_qkv.at[:, : 2 * model]
+    normed_2, inverse_2 = norm_parts(x_two[...])
+    gx1[...] = gattn[...].astype(F32) + norm_back(
+        normed_2, inverse_2, d_frames[...] * (1.0 + row(4))
+    )
+    gc[...] = gx1[...].astype(BF16)
+    ga[...] = dot_t(gc[...], co_v[...]).astype(BF16)
+
+    @pl.loop(0, HEADS // 2, unroll=True)
+    def _(p):
+        at = lanes(p)
+        value_at = lanes(p + HEADS // 2)
+        key_pair, value_pair = gkvc[:, at], gkvc[:, value_at]
+        query_pair, up_pair = gqc[:, at], ga[:, at]
+        d_q, d_k, d_v = [], [], []
+        for half in range(2):
+            low = prob_c[2 * p + half]
+            probs = low.astype(F32)
+            grad_probs = dot_t(pick_half(up_pair, half), value_pair)
+            inner = jnp.sum(probs * grad_probs, axis=-1, keepdims=True)
+            grad_scores = (probs * (grad_probs - inner)).astype(BF16)
+            d_q.append(dot(grad_scores, key_pair))
+            d_k.append(t_dot(grad_scores, query_pair))
+            d_v.append(t_dot(low, up_pair))
+        gqc[:, at] = (join_halves(*d_q) * HEAD ** (-0.5)).astype(BF16)
+        gkvc[:, at] = (join_halves(*d_k) * HEAD ** (-0.5)).astype(BF16)
+        gkvc[:, value_at] = join_halves(*d_v).astype(BF16)
+
+    phase2(1)
+    T[y, x] = dot_t(gkvc[: T.shape[2], :], ckv_v[...]).astype(BF16)
+    last_load.start()
+    advance(text_steps, 0)
+    normed_1, inverse_1 = norm_parts(x_one[...])
+    up_two = dot_t(gqc[...], cq_v[...])
+    grad_x1 = gx1[...] + norm_back(normed_1, inverse_1, up_two * g_cross[...].astype(F32)[None])
+    gx1[...] = grad_x1
+    ga[...] = (row(2) * grad_x1).astype(BF16)
+    gattn[...] = dot_t(ga[...], out_v[...]).astype(BF16)
+    row_of = lax.broadcasted_iota(jnp.int32, early.shape, 0)
+    whole = jnp.where(row_of == 0, col_sum(grad_x1 * branch[...]), early[...])
+    whole = jnp.where(row_of == 4, col_sum(up_two * normed_1), whole)
+    e_all[c, z, y, x] = whole.astype(BF16)
     advance(early_steps, 0)
-    advance(text_steps, 0)
-    phase0(3)
-    deep1(0)
-    phase0(1)
-    phase1(3)
     phase0(4)
-    deep1(1)
+    frames_load.start()
+    query_load.start()
+    phase0(5)
+    deep1(4)
+    phase1(5)
+    phase2(2)
+    deep2(0)
     advance(early_steps, 1)
     advance(text_steps, 1)
-    phase0(5)
-    phase1(4)
-    phase1(5)
-    advance(early_steps, 2)
-
+    phase2(3)
+
+    query_load.wait()
     own = pl.ds(pl.multiple_of(seq * here, here), here)
     dqkv[:, :model] = jnp.zeros((dqkv.shape[0], model), BF16)
     lane_of = lax.broadcasted_iota(jnp.int32, lse.shape, 1)
-    for load in loads:
-        load.wait()
-
     @pl.loop(0, HEADS // 2)
     def _(p):
         at = lanes(p)
         key_at = lanes(p + HEADS // 2)
         value_at = lanes(p + HEADS)
         key_pair, value_pair = kv[:, at], kv[:, key_at]
-        query_pair, up_pair = query[:, at], gattn[:, at]
+        query_pair, up_pair = gqc[:, at], gattn[:, at]
         scaled = query_pair * jnp.asarray(HEAD ** (-0.5), BF16)
         d_q, d_k, d_v = [], [], []
         for half in range(2):
@@ -873,20 +907,24 @@
         remote(up_low.at[1 - y, x, :part], R4.at[4], s4.at[2], r4.at[2], y_peer),
         remote(up_low.at[y, 1 - x, part:], R4.at[5], s4.at[3], r4.at[3], x_peer),
     )
-    deep2(0)
+    last_load.wait()
+    advance(early_steps, 2)
     for block in range(4):
         up_low[block // 2, block % 2] = up_block(block).astype(BF16)
     for copy in up_first:
         copy.start()
     phase0(6)
-    phase2(2)
-    deep2(1)
+    phase3(1)
+    deep3(0)
     phase0(7)
     phase1(6)
-    phase2(3)
+    deep2(4)
     phase1(7)
     phase3(2)
-    deep3(0)
+    phase4(1)
+    phase2(5)
+    phase3(3)
+    phase4(2)
     for copy in up_first:
         copy.wait_recv()
     for i in range(2):
@@ -896,19 +934,19 @@
         copy.start()
     advance(early_steps, 3)
     advance(text_steps, 2)
-    phase2(4)
-    phase3(3)
-    deep3(1)
     deep4(0)
-    phase2(5)
-    phase3(4)
-    deep4(1)
+    deep3(4)
+    phase4(3)
+    phase3(5)
     deep5(0)
+    phase2(6)
+    deep4(4)
     for copy in up_second:
         copy.wait_recv()
     up_one = dot_t(dqkv[own, :model], w_qkv[:, :model]) + up_low[y, x].astype(F32)
     up_one = up_one + jnp.concatenate([R4[4], R4[5]], axis=0).astype(F32)
-    normed, inverse = norm_parts(frames[...].astype(F32))
+    frames_load.wait()
+    normed, inverse = norm_parts(gc[...].astype(F32))
     for i, total in enumerate((col_sum(up_one), col_sum(up_one * normed))):
         for j in range(model // 128):
             at = i * (model // 128) + j
@@ -923,20 +961,20 @@
             seg_s[0, i * here] == seq, 1.0, 0.0
         )
     d_text[...] = total
-    phase2(6)
-    phase3(5)
+    phase4(5)
+    phase3(6)
     advance(late_steps, 1)
-    deep5(1)
     phase2(7)
-    phase3(6)
+    deep5(4)
+    phase4(6)
     advance(late_steps, 2)
     phase3(7)
     advance(late_steps, 3)
-
-    @pl.loop(len(DEEP), CHUNKS)
-    def _(k):
-        phase4(k)
-
+    for k in FLAT[:-2]:
+        phase5(k)
+    phase4(7)
+    for k in FLAT[-2:]:
+        phase5(k)
     advance(early_steps, 4)
     advance(late_steps, 4)
     for k in range(CHUNKS):
@@ -945,9 +983,8 @@
         for copy in deep_copies(k):
             copy.wait_send()
 
-    @pl.loop(len(DEEP), CHUNKS)
-    def _(k):
-        for copy in (*first_copies(k), *second_copies(k), *z_copies(k)):
+    for k in FLAT:
+        for copy in (*first_copies(k), *second_copies(k), *z_near(k), z_far(k)):
             copy.wait_send()
 
     for copy in (*up_first, *up_second):
@@ -1083,17 +1120,18 @@
     square = like((here, model))
     dma = pltpu.SemaphoreType.DMA
     vmem = pltpu.VMEM
+    wide = like((here, model), F32)
     (
-        output, act, gm_t, h3, gpre, h2, cross, gqc, gc, gkvc, attn, ga, gattn, gx1, query,
-        kv, h_all, lse, mods, text_part, early, text_mine,
+        output, act, gm_t, h3, gpre, h2, cross, gqc, gkvc, attn, query,
+        kv, h_all, lse, mods, early, text_mine, branch, x_one, x_two, up_three, prob_c,
     ) = pl.pallas_call(
         forward_kernel,
         out_shape=(
             square, like((here, hidden)), like((model, here)), square, like((here, hidden)),
-            square, square, square, square, like((text_rows, 2 * model)), square, square,
-            square, like((here, model), F32), square, like((length, 2 * model)),
-            like((length, model)), like((here, 128), F32), like((8, model), F32),
-            like((text_rows, model)), like((16, model), F32), like((text_rows, model)),
+            square, square, square, like((text_rows, 2 * model)), square, square,
+            like((length, 2 * model)), like((length, model)), like((here, 128), F32),
+            like((8, model), F32), like((16, model), F32), like((text_rows, model)),
+            wide, wide, wide, wide, like((HEADS, here, text_rows)),
         ),
         in_specs=in_any(1) + in_vmem(3) + smem(1) + in_vmem(1)
         + in_any(1) + in_vmem(1) + in_any(2) + in_vmem(1) + in_any(4) + in_vmem(1)
@@ -1104,8 +1142,7 @@
             vmem(w_ada.shape, BF16), vmem(w_qkv.shape, BF16), vmem(w_out.shape, BF16),
             vmem(w_cq.shape, BF16), vmem(w_ckv.shape, BF16), vmem(w_co.shape, BF16),
             vmem(w_up.shape, BF16), vmem(w_down.shape, BF16),
-            vmem((HEADS, here, text_rows), F32),
-            vmem((here, model), F32), vmem((here, model), F32),
+            vmem((here, model), BF16), vmem((here, model), F32),
             vmem((step_rows, 6 * model), F32),
             vmem((1, hidden), F32),
             dma((9,)), dma((4,)), dma((4,)),
@@ -1128,7 +1165,7 @@
             like((text_kept, model), F32), like(table + (16, model)),
             like(table + (16, 128)),
         ),
-        in_specs=in_vmem(15) + smem(1) + in_vmem(1) + in_any(8),
+        in_specs=in_vmem(11) + smem(1) + in_vmem(1) + in_any(18),
         out_specs=tuple(in_vmem(5)),
         scratch_shapes=[
             vmem((CHUNKS,) + table + (tall, width), BF16),
@@ -1141,10 +1178,14 @@
             vmem((2, 2, here, model), BF16),
             vmem((2, 2, text_kept, model), BF16),
             vmem((16, 128), F32),
-            vmem((here, model), BF16), vmem((here, model), F32), vmem((here, model), BF16),
+            vmem((here, model), BF16), vmem((here, model), F32),
             vmem((length, 2 * model), BF16), vmem((length, model), BF16),
-            vmem((here, 128), F32), vmem((here, model), BF16), vmem(w_qkv.shape, BF16),
-            dma((8,)),
+            vmem((here, 128), F32), vmem(w_qkv.shape, BF16),
+            dma((18,)),
+            vmem((here, model), BF16), vmem((text_rows, 2 * model), BF16),
+            vmem((here, model), BF16), vmem((here, model), BF16),
+            vmem((here, model), F32), vmem((here, model), F32), vmem((here, model), F32),
+            vmem((HEADS, here, text_rows), BF16),
             dma((CHUNKS,)), dma((CHUNKS,)),
             dma((CHUNKS, 2)), dma((CHUNKS, 2)),
             dma((CHUNKS, 2)), dma((CHUNKS, 2)),
@@ -1157,8 +1198,9 @@
         ),
         name="backward_layer",
     )(
-        act, gm_t, h3, gpre, h2, cross, gqc, gc, gkvc, attn, ga, mods, text_part, early,
-        text_mine, segments, segments, gattn, gx1, query, kv, h_all, lse, frames, w_qkv,
+        act, gm_t, h3, gpre, h2, cross, attn, mods, early, text_mine, g_cross,
+        segments, segments, query, kv, h_all, lse, frames, w_qkv,
+        gqc, gkvc, cotangent, branch, x_one, x_two, up_three, prob_c, w_co, w_cq, w_out, w_ckv,
     )
 
     def shard(*shape):

time: 177 us -> 172 us (0.972)
  Pallas kernels: 176 us -> 171 us
    pallas_call x1, Pallas kernels: 54.1 us -> 48.6 us  [per_device(): pl.pallas_call(forward_kernel, out_shape=(square, like((here, hidden)), l...]
where the time goes in v5:
time: 172 us
  Pallas kernels  171 us (99%)
    pallas_call x1, Pallas kernels, per_device(): pl.pallas_call(backward_kernel, out_shape=(like((CHUNKS, tall, width), F3...  114 us
    pallas_call x1, Pallas kernels, per_device(): pl.pallas_call(forward_kernel, out_shape=(square, like((here, hidden)), l...  48.6 us
    pallas_call x1, Pallas kernels, per_device(): pl.pallas_call(finish_kernel, out_shape=(like((1, here, model)), shard(1,...  8.42 us

profile of v5, /device:TPU:0, one launch (start us, length us, event | category | flops | bytes accessed | tf_op | source)
XLA Modules:
  0.0 172.1 jit_solution(17771154804293927078)
XLA Ops:
  0.6 48.6 %forward_layer.1 = (bf16[256,768]{1,0:T(8,128)(2,1)}, bf16[256,3072]{1,0:T(8,128)(2,1)}, bf16[768,256]{1,0:T(8,128)(2,1)}, bf16[256,768]{1,0:T(8,128)(2,1)}, bf1...) custom-call(bf16[1,256,768]{2,1,0:T(8,128)(2,1)} %frames_h.1, ...), custom_call_target="tpu_custom_call" | custom-call | tf_op jit(solution)/shard_map/forward_layer/pallas_call | solution.py:1127
  49.2 114.3 %backward_layer.1 = (f32[8,96,384]{2,1,0:T(8,128)}, f32[256,768]{1,0:T(8,128)}, f32[80,768]{1,0:T(8,128)}, bf16[2,4,2,2,16,768]{5,4,3,2,1,0:T(8,128)(2,1)}, bf16[2,4,2,2,16,128]{5,4,3,2,1,0:T(8,128)(2,1)}) custom-call(bf16[256,3072]{1,0:T(8,128)(2,1)} %get-tuple-element.59.act, bf16[768,256]{1,0:T(8,128)(2,1)} %get-tuple-element.60.gm_t, ...), custom_call_target="tpu_custom_call" | custom-call | tf_op jit(solution)/shard_map/backward_layer/pallas_call | solution.py:1161
  163.5 8.4 %finish_layer.1 = (bf16[1,256,768]{2,1,0:T(8,128)(2,1)}, f32[1,256,768]{2,1,0:T(8,128)}, f32[77,1,768]{2,1,0:T(1,128)}, f32[1,1,768]{2,1,0:T(1,128)}, f32[96,115...) custom-call(f32[8,96,384]{2,1,0:T(8,128)} %get-tuple-element.80.done, ...), custom_call_target="tpu_custom_call" | custom-call | tf_op jit(solution)/shard_map/finish_layer/pallas_call | solution.py:1210
